TPU v7x, 256 devices: a whole 4x4x8 slice. The times are simulated.
256 devices in a mesh: ctx: 64 (over x, z, core), head: 4 (over y).
Axes of the slice: x: 4, y: 4, z: 8, core: 2. Of those that a mesh axis runs over, the one named last changes fastest.
Arguments:
- lin_query: bfloat16 [8192, 8192], P('ctx', 'head'), may hold values from -6 to 6
- lin_key: bfloat16 [8192, 8192], P('ctx', 'head'), may hold values from -6 to 6
- lin_value: bfloat16 [8192, 8192], P('ctx', 'head'), may hold values from -6 to 6
- log_decay: float32 [8192, 64], P('ctx', 'head'), may hold values from -1 to 0, as said below
- soft_query: bfloat16 [8192, 8192], P('ctx', 'head'), may hold values from -24 to 24
- soft_key: bfloat16 [8192, 8192], P('ctx', 'head'), may hold values from -24 to 24
- soft_value: bfloat16 [8192, 8192], P('ctx', 'head'), may hold values from -6 to 6
Outputs:
- lin_out: bfloat16 [8192, 8192], P('ctx', 'head')
- soft_out: bfloat16 [8192, 8192], P('ctx', 'head')
Inputs may be any that keep to these rules, and one draw needn't show every extreme that they name: `log_decay`: never positive.
All inputs are finite; a program needn't handle non-finite values.
Results may differ from a plain program's by a relative error of at most 0.0065.
Values may be sent and summed in bfloat16 or wider, within the bound.
No kernel may reach another device: no remote copies, remote signals or barrier semaphores. Data moves between devices by JAX's collectives and lax.ppermute only.
A program may use at most 192 MiB of HBM per device.

v0:
```python
import jax
import jax.numpy as jnp
from jax import lax
from jax.sharding import PartitionSpec as P

HEAD_DIM = 128


norm_eps = 1e-06
masked_score = -1e30
key_span = 512
query_span = 512


def entering(value, axis, join, neutral):
    count, mine = (lax.axis_size(axis), lax.axis_index(axis))
    pieces = jax.tree.map(lambda part: lax.all_gather(part, axis), value)
    subtotal = jax.tree.map(
        lambda part, zero: jnp.full_like(part, 0) + jnp.asarray(zero, part.dtype), value, neutral
    )

    def step(position, subtotal):
        longer = join(subtotal, jax.tree.map(lambda part: part[position], pieces))
        return jax.tree.map(lambda new, old: jnp.where(position < mine, new, old), longer, subtotal)

    return lax.fori_loop(0, count - 1, step, subtotal)


def merge_states(earlier, later):
    decay_early, state_early = earlier
    decay_late, state_late = later
    return (decay_early * decay_late, decay_late[:, None, None] * state_early + state_late)


def lightning_core(lin_query, lin_key, lin_value, log_decay):
    tokens = lin_query.shape[0]
    heads_here = log_decay.shape[1]
    query_heads = lin_query.reshape(tokens, heads_here, HEAD_DIM)
    key_heads = lin_key.reshape(tokens, heads_here, HEAD_DIM)
    value_heads = lin_value.reshape(tokens, heads_here, HEAD_DIM)
    running_sum = jnp.cumsum(log_decay, axis=0)
    ending = running_sum[-1]
    scores = jnp.einsum("thd,shd->hts", query_heads, key_heads, preferred_element_type=jnp.float32)
    causal = jnp.arange(tokens)[:, None] >= jnp.arange(tokens)[None, :]
    spread = running_sum.T[:, :, None] - running_sum.T[:, None, :]
    decayed = (
        jnp.where(causal[None], jnp.exp(jnp.where(causal[None], spread, 0.0)), 0.0) * scores
    ).astype(jnp.bfloat16)
    inside = jnp.einsum("hts,shd->thd", decayed, value_heads, preferred_element_type=jnp.float32)
    to_end = jnp.exp(ending[None, :] - running_sum)
    key_scaled = (key_heads.astype(jnp.float32) * to_end[:, :, None]).astype(jnp.bfloat16)
    block_state = jnp.einsum(
        "shd,she->hde", key_scaled, value_heads, preferred_element_type=jnp.float32
    )
    block_decay = jnp.exp(ending)
    before = entering(
        (block_decay, block_state),
        "ctx",
        merge_states,
        (jnp.ones_like(block_decay), jnp.zeros_like(block_state)),
    )
    prior_state = before[1]
    query_scaled = (query_heads.astype(jnp.float32) * jnp.exp(running_sum)[:, :, None]).astype(
        jnp.bfloat16
    )
    outside = jnp.einsum(
        "thd,hde->the",
        query_scaled,
        prior_state.astype(jnp.bfloat16),
        preferred_element_type=jnp.float32,
    )
    total = inside + outside
    normed = total * lax.rsqrt(jnp.mean(total * total, axis=-1, keepdims=True) + norm_eps)
    return normed.reshape(tokens, heads_here * HEAD_DIM).astype(jnp.bfloat16)


def prepare_queries(query_mine, tokens, quarter, head_slot):
    rows_all = query_mine.shape[0]
    heads_now = query_mine.shape[1] // HEAD_DIM
    blocks_count = rows_all // query_span
    query_blocks = query_mine.reshape(blocks_count, query_span, heads_now, HEAD_DIM)
    index_all = jnp.arange(rows_all, dtype=jnp.int32)
    token_slots = index_all // quarter * tokens + head_slot * quarter + index_all % quarter
    initial = (
        jnp.full((blocks_count, query_span, heads_now), masked_score, jnp.float32),
        jnp.zeros((blocks_count, query_span, heads_now), jnp.float32),
        jnp.zeros((blocks_count, query_span, heads_now, HEAD_DIM), jnp.float32),
    )
    return (query_blocks, token_slots.reshape(blocks_count, query_span), initial)


def attend_keys(carry, query_blocks, query_places, keys_flat, values_flat, key_places):
    key_total = keys_flat.shape[0]
    heads_now = query_blocks.shape[2]
    keys_heads = keys_flat.reshape(key_total, heads_now, HEAD_DIM)
    values_heads = values_flat.reshape(key_total, heads_now, HEAD_DIM)
    score_scale = HEAD_DIM ** (-0.5)

    def per_block(packed):
        best_start, mass_start, accum_start, query_tile, query_where = packed
        latest_query = jnp.max(query_where)

        def per_span(span_index, running):
            start_row = span_index * key_span
            key_where = lax.dynamic_slice_in_dim(key_places, start_row, key_span, 0)

            def compute(state_now):
                best_now, mass_now, accum_now = state_now
                key_tile = lax.dynamic_slice_in_dim(keys_heads, start_row, key_span, 0)
                value_tile = lax.dynamic_slice_in_dim(values_heads, start_row, key_span, 0)
                scores = (
                    jnp.einsum(
                        "qhd,khd->qhk", query_tile, key_tile, preferred_element_type=jnp.float32
                    )
                    * score_scale
                )
                allowed = (key_where[None, :] <= query_where[:, None])[:, None, :]
                scores = jnp.where(allowed, scores, masked_score)
                best_next = jnp.maximum(best_now, jnp.max(scores, axis=-1))
                expo = jnp.where(allowed, jnp.exp(scores - best_next[:, :, None]), 0.0)
                shrink = jnp.exp(best_now - best_next)
                mass_next = mass_now * shrink + jnp.sum(expo, axis=-1)
                accum_next = accum_now * shrink[:, :, None] + jnp.einsum(
                    "qhk,khd->qhd",
                    expo.astype(jnp.bfloat16),
                    value_tile,
                    preferred_element_type=jnp.float32,
                )
                return (best_next, mass_next, accum_next)

            def unchanged(state_now):
                return state_now

            return lax.cond(jnp.min(key_where) <= latest_query, compute, unchanged, running)

        return lax.fori_loop(
            0, key_total // key_span, per_span, (best_start, mass_start, accum_start)
        )

    return lax.map(per_block, (carry[0], carry[1], carry[2], query_blocks, query_places))


def softmax_core(soft_query, soft_key, soft_value):
    tokens = soft_query.shape[0]
    quarter = tokens // lax.axis_size("head")
    head_slot = lax.axis_index("head")
    query_moved, key_moved, value_moved = (
        lax.all_to_all(soft_query, "head", split_axis=0, concat_axis=1, tiled=True),
        lax.all_to_all(soft_key, "head", split_axis=0, concat_axis=1, tiled=True),
        lax.all_to_all(soft_value, "head", split_axis=0, concat_axis=1, tiled=True),
    )
    query_mine, key_mine, value_mine = (
        lax.all_to_all(query_moved, "ctx", split_axis=1, concat_axis=0, tiled=True),
        lax.all_to_all(key_moved, "ctx", split_axis=1, concat_axis=0, tiled=True),
        lax.all_to_all(value_moved, "ctx", split_axis=1, concat_axis=0, tiled=True),
    )
    query_blocks, query_places, initial = prepare_queries(query_mine, tokens, quarter, head_slot)
    resident_rows = key_mine.shape[0]
    pieces = (
        lax.all_gather(key_mine, "head", axis=0, tiled=True),
        lax.all_gather(value_mine, "head", axis=0, tiled=True),
    )
    key_total = pieces[0].shape[0]
    index_all = jnp.arange(key_total, dtype=jnp.int32)
    source = index_all // resident_rows
    within = index_all % resident_rows
    token_slots = within // quarter * tokens + source * quarter + within % quarter
    result = attend_keys(initial, query_blocks, query_places, pieces[0], pieces[1], token_slots)
    best_final, mass_final, accum_final = result
    outcome = (
        (accum_final / mass_final[..., None]).reshape(query_mine.shape[0], -1).astype(jnp.bfloat16)
    )
    return lax.all_to_all(
        lax.all_to_all(outcome, "ctx", split_axis=0, concat_axis=1, tiled=True),
        "head",
        split_axis=1,
        concat_axis=0,
        tiled=True,
    )


def shards(lin_query, lin_key, lin_value, log_decay, soft_query, soft_key, soft_value):
    lin_out = lightning_core(lin_query, lin_key, lin_value, log_decay)
    soft_out = softmax_core(soft_query, soft_key, soft_value)
    return (lin_out, soft_out)


def solution(mesh):
    in_specs = (
        P("ctx", "head"),
        P("ctx", "head"),
        P("ctx", "head"),
        P("ctx", "head"),
        P("ctx", "head"),
        P("ctx", "head"),
        P("ctx", "head"),
    )
    out_specs = (P("ctx", "head"), P("ctx", "head"))
    return jax.shard_map(shards, mesh=mesh, in_specs=in_specs, out_specs=out_specs, check_vma=False)
```

profile of v0, /device:TPU:1, one launch (start us, length us, event | category | flops | bytes accessed | tf_op | source)
XLA Modules:
  0.0 550.6 jit_solution(8589705963273592994)
XLA Ops:
  7.2 13.0 %all_to_all.134 = bf16[4,32,2048]{2,1,0:T(8,128)(2,1)S(1)} all-to-all(bf16[4,32,2048]{2,1,0:T(8,128)(2,1)} %bitcast.149), channel_id=1, replica_groups=mesh['ctx'=64,'head'=4] {'head'}, dimensions={0} | all-to-all | bytes 1048576 | tf_op jit(solution)/shard_map/all_to_all | solution.py:149
  21.3 31.3 %all_to_all.135 = bf16[32,64,128]{2,0,1:T(8,128)(2,1)} all-to-all(bf16[32,64,128]{2,0,1:T(8,128)(2,1)S(1)} %copy.74), channel_id=1, replica_groups=mesh['ctx'=64,'head'=4] {'ctx'}, dimensions={1} | all-to-all | bytes 1048576 | tf_op jit(solution)/shard_map/all_to_all | solution.py:154
  52.7 11.7 %all_to_all.136 = bf16[4,32,2048]{2,1,0:T(8,128)(2,1)S(1)} all-to-all(bf16[4,32,2048]{2,1,0:T(8,128)(2,1)S(1)} %bitcast.150), channel_id=1, replica_groups=mesh['ctx'=64,'head'=4] {'head'}, dimensions={0} | all-to-all | bytes 1048576 | tf_op jit(solution)/shard_map/all_to_all | solution.py:150
  65.5 24.3 %all_to_all.137 = bf16[32,64,128]{2,0,1:T(8,128)(2,1)} all-to-all(bf16[32,64,128]{2,0,1:T(8,128)(2,1)S(1)} %copy.76), channel_id=1, replica_groups=mesh['ctx'=64,'head'=4] {'ctx'}, dimensions={1} | all-to-all | bytes 1048576 | tf_op jit(solution)/shard_map/all_to_all | solution.py:155
  91.9 13.5 %all_to_all.138 = bf16[4,32,2048]{2,1,0:T(8,128)(2,1)S(1)} all-to-all(bf16[4,32,2048]{2,1,0:T(8,128)(2,1)S(1)} %bitcast.151), channel_id=1, replica_groups=mesh['ctx'=64,'head'=4] {'head'}, dimensions={0} | all-to-all | bytes 1048576 | tf_op jit(solution)/shard_map/all_to_all | solution.py:148
  107.3 7.2 %all-to-all-start.1 = ((bf16[32,64,128]{2,0,1:T(8,128)(2,1)}), bf16[32,64,128]{2,0,1:T(8,128)(2,1)S(1)}, u32[]{:S(2)}, u32[]{:S(2)}) async-start(bf16[32,64,128]{2,0,1:T(8,128)(2,1)} %copy.72), calls=%async_computation.1 | async-start | bytes 1048576 | tf_op jit(solution)/shard_map/all_to_all | solution.py:153
  114.6 17.3 %all-to-all-done.1 = bf16[32,64,128]{2,0,1:T(8,128)(2,1)S(1)} async-done(((bf16[32,64,128]{2,0,1:T(8,128)(2,1)}), bf16[32,64,128]{2,0,1:T(8,128)(2,1)S(1)}, u32[]{:S(2)}, u32[]{:S(2)}) %all-to-all-start.1) | async-done | bytes 524320 | tf_op jit(solution)/shard_map/all_to_all | solution.py:153
  131.9 243.1 %while.46 = (s32[]{:T(128)}, f32[4,512,1]{1,0,2:T(4,128)S(1)}, f32[4,512,1,128]{3,1,0,2:T(8,128)}, s32[4,512]{1,0:T(4,128)S(1)}, bf16[4,512,1,128]{3,1,2,0:T(8,1...) while((s32[]{:T(128)}, f32[4,512,1]{1,0,2:T(4,128)S(1)}, ...), condition=%wide.region_13.14_spmd.clone, body=%wide.region_4.13_spmd.clone.sunk | while | flops 137783296 | bytes 5731476 | solution.py:140
  132.7 41.9 %while.48 = (s32[]{:T(128)}, f32[512,1]{0,1:T(1,128)S(1)}, f32[512,1]{0,1:T(1,128)S(1)}, f32[512,1,128]{0,2,1:T(8,128)S(1)}, s32[8192]{0:T(1024)S(1)}, /*index=5...) while((s32[]{:T(128)}, f32[512,1]{0,1:T(1,128)S(1)}, ...), condition=%wide.region_12.12_spmd, body=%wide.region_6.11_spmd.sunk | while | flops 137496064 | bytes 4112755 | solution.py:136
  134.6 2.9 conditional.2
  145.0 2.9 conditional.2
  155.5 2.9 conditional.2
  166.0 2.9 conditional.2
  176.2 53.4 %while.48 = (s32[]{:T(128)}, f32[512,1]{0,1:T(1,128)S(1)}, f32[512,1]{0,1:T(1,128)S(1)}, f32[512,1,128]{0,2,1:T(8,128)S(1)}, s32[8192]{0:T(1024)S(1)}, /*index=5...) while((s32[]{:T(128)}, f32[512,1]{0,1:T(1,128)S(1)}, ...), condition=%wide.region_12.12_spmd, body=%wide.region_6.11_spmd.sunk | while | flops 137496064 | bytes 4112755 | solution.py:136
  178.1 2.9 conditional.2
  182.9 2.9 conditional.2
  191.4 3.0 conditional.2
  196.3 2.9 conditional.2
  204.8 2.9 conditional.2
  209.6 2.9 conditional.2
  218.2 2.9 conditional.2
  223.0 2.9 conditional.2
  231.3 64.9 %while.48 = (s32[]{:T(128)}, f32[512,1]{0,1:T(1,128)S(1)}, f32[512,1]{0,1:T(1,128)S(1)}, f32[512,1,128]{0,2,1:T(8,128)S(1)}, s32[8192]{0:T(1024)S(1)}, /*index=5...) while((s32[]{:T(128)}, f32[512,1]{0,1:T(1,128)S(1)}, ...), condition=%wide.region_12.12_spmd, body=%wide.region_6.11_spmd.sunk | while | flops 137496064 | bytes 4112755 | solution.py:136
  233.2 2.9 conditional.2
  238.0 3.0 conditional.2
  242.8 2.9 conditional.2
  249.5 2.9 conditional.2
  254.2 2.9 conditional.2
  259.0 2.9 conditional.2
  265.7 2.9 conditional.2
  270.4 2.9 conditional.2
  275.2 2.9 conditional.2
  281.9 2.9 conditional.2
  286.6 2.9 conditional.2
  291.4 2.9 conditional.2
  297.9 76.3 %while.48 = (s32[]{:T(128)}, f32[512,1]{0,1:T(1,128)S(1)}, f32[512,1]{0,1:T(1,128)S(1)}, f32[512,1,128]{0,2,1:T(8,128)S(1)}, s32[8192]{0:T(1024)S(1)}, /*index=5...) while((s32[]{:T(128)}, f32[512,1]{0,1:T(1,128)S(1)}, ...), condition=%wide.region_12.12_spmd, body=%wide.region_6.11_spmd.sunk | while | flops 137496064 | bytes 4112755 | solution.py:136
  299.7 2.9 conditional.2
  304.5 2.9 conditional.2
  309.3 2.9 conditional.2
  314.0 2.9 conditional.2
  318.8 2.9 conditional.2
  323.5 2.9 conditional.2
  328.3 2.9 conditional.2
  333.1 2.9 conditional.2
  337.8 2.9 conditional.2
  342.6 2.9 conditional.2
  347.4 2.9 conditional.2
  352.2 2.9 conditional.2
  357.0 2.9 conditional.2
  361.7 2.9 conditional.2
  366.5 2.9 conditional.2
  371.2 2.9 conditional.2
  375.0 2.4 divide_convert_fusion
  377.4 6.6 %all-to-all-start.6 = ((bf16[64,32,128]{2,1,0:T(8,128)(2,1)}), bf16[64,32,128]{2,1,0:T(8,128)(2,1)S(1)}, u32[]{:S(2)}, u32[]{:S(2)}) async-start(bf16[64,32,128]{2,1,0:T(8,128)(2,1)} %bitcast.35), calls=%async_computation.6 | async-start | bytes 1048576 | tf_op jit(solution)/shard_map/all_to_all | solution.py:174
  384.1 48.1 %all-gather.1 = f32[64,1,16]{2,1,0:T(1,128)S(1)} all-gather(f32[1,1,16]{2,1,0:T(1,128)S(1)} %get-tuple-element.467), channel_id=1, replica_groups=mesh['ctx'=64,'head'=4] {'ctx'}, dimensions={0}, use_global_device_ids=true | all-gather | bytes 4160 | tf_op jit(solution)/shard_map/all_gather | solution.py:17
  433.7 3.5 all-to-all-start.7
  437.2 1.7 convolution_bitcast_fusion.2
  438.9 7.7 %all-to-all-done.7 = bf16[32,4,2048]{2,0,1:T(8,128)(2,1)S(1)} async-done(((bf16[32,4,2048]{2,0,1:T(8,128)(2,1)}), bf16[32,4,2048]{2,0,1:T(8,128)(2,1)S(1)}, u32[]{:S(2)}, u32[]{:S(2)}) %all-to-all-start.7) | async-done | bytes 524320 | tf_op jit(solution)/shard_map/all_to_all | solution.py:173
  446.6 94.5 %while.47 = (s32[]{:T(128)}, f32[16,128,128]{2,1,0:T(8,128)S(1)}, s32[]{:T(128)}, f32[64,16]{1,0:T(8,128)S(1)}, f32[64,16,128,128]{3,2,1,0:T(8,128)}, /*index=5*/s32[]{:T(128)}, s32[]{:T(128)}) while((s32[]{:T(128)}, f32[16,128,128]{2,1,0:T(8,128)S(1)}, s32[]{:T(128)}, f32[64,16]{1,0:T(8,128)S(1)}, f32[64,16,128,128]{3,2,1,0:T(8,128)}, ...), condition=%wide.region_2.3_spmd.clone, body=%wide.region_1.2_spmd.clone.sunk | while | flops 1048580 | bytes 3146025 | solution.py:26
  446.6 1.5 fusion.83
  448.2 1.5 fusion.83
  449.7 1.5 fusion.83
  452.7 1.5 fusion.83
  454.2 1.5 fusion.83
  (542 shorter events, 258.8 us)
Async XLA Ops:
  7.2 430.1 %copy-start = (bf16[128,2048]{1,0:T(8,128)(2,1)S(1)}, bf16[128,2048]{1,0:T(8,128)(2,1)}, u32[]{:S(2)}) copy-start(bf16[128,2048]{1,0:T(8,128)(2,1)} %param.15) | copy-start | bytes 1572868
  7.2 124.7 %all-gather.6.cloned.1.call-start = ((), (), s32[]{:S(2)}) async-start(), calls=%async_computation.8 | async-start | bytes 2621440 | tf_op jit(solution)/shard_map/all_gather | solution.py:160
  20.6 32.1 %copy-start.2 = (bf16[128,2048]{1,0:T(8,128)(2,1)S(1)}, bf16[128,2048]{1,0:T(8,128)(2,1)}, u32[]{:S(2)}) copy-start(bf16[128,2048]{1,0:T(8,128)(2,1)} %param.21) | copy-start | bytes 1572868
  52.7 79.3 %all-gather.8.cloned.1.call-start = ((), (), s32[]{:S(2)}) async-start(), calls=%async_computation.9 | async-start | bytes 2621440 | tf_op jit(solution)/shard_map/all_gather | solution.py:161
  64.8 25.1 %copy-start.7 = (f32[128,16]{0,1:T(8,128)S(1)}, f32[128,16]{0,1:T(8,128)}, u32[]{:S(2)}) copy-start(f32[128,16]{0,1:T(8,128)} %param.18) | copy-start | bytes 24580
  64.8 25.5 %copy-start.3 = (bf16[128,2048]{1,0:T(8,128)(2,1)S(1)}, bf16[128,2048]{1,0:T(8,128)(2,1)}, u32[]{:S(2)}) copy-start(bf16[128,2048]{1,0:T(8,128)(2,1)} %param.16) | copy-start | bytes 1572868
  65.5 25.1 %copy-start.5 = (bf16[128,2048]{1,0:T(8,128)(2,1)S(1)}, bf16[128,2048]{1,0:T(8,128)(2,1)}, u32[]{:S(2)}) copy-start(bf16[128,2048]{1,0:T(8,128)(2,1)} %param.17) | copy-start | bytes 1572868
  89.9 356.8 %all-gather.10.cloned.1.call-start = ((), (), s32[]{:S(2)}) async-start(), calls=%async_computation.10 | async-start | bytes 68157440 | tf_op jit(solution)/shard_map/all_gather | solution.py:17
  90.3 1.6 copy-start.4
  107.3 24.6 %all-to-all-start.1 = ((bf16[32,64,128]{2,0,1:T(8,128)(2,1)}), bf16[32,64,128]{2,0,1:T(8,128)(2,1)S(1)}, u32[]{:S(2)}, u32[]{:S(2)}) async-start(bf16[32,64,128]{2,0,1:T(8,128)(2,1)} %copy.72), calls=%async_computation.1 | async-start | bytes 1048576 | tf_op jit(solution)/shard_map/all_to_all | solution.py:153
  377.4 54.9 %all-to-all-start.6 = ((bf16[64,32,128]{2,1,0:T(8,128)(2,1)}), bf16[64,32,128]{2,1,0:T(8,128)(2,1)S(1)}, u32[]{:S(2)}, u32[]{:S(2)}) async-start(bf16[64,32,128]{2,1,0:T(8,128)(2,1)} %bitcast.35), calls=%async_computation.6 | async-start | bytes 1048576 | tf_op jit(solution)/shard_map/all_to_all | solution.py:174
  432.6 4.6 copy-start.6
  433.7 12.9 %all-to-all-start.7 = ((bf16[32,4,2048]{2,0,1:T(8,128)(2,1)}), bf16[32,4,2048]{2,0,1:T(8,128)(2,1)S(1)}, u32[]{:S(2)}, u32[]{:S(2)}) async-start(bf16[32,4,2048]{2,0,1:T(8,128)(2,1)} %copy.80), calls=%async_computation.7 | async-start | bytes 1048576 | tf_op jit(solution)/shard_map/all_to_all | solution.py:173
  446.6 94.5 %copy-start.1 = (f32[128,16,128]{0,2,1:T(8,128)S(1)}, f32[128,16,128]{0,2,1:T(8,128)}, u32[]{:S(2)}) copy-start(f32[128,16,128]{0,2,1:T(8,128)} %convolution_bitcast_fusion.2) | copy-start | bytes 3145732
Sparse Core Ops, SparseCore 0:
  52.8 29.1 all-gather.5
  90.0 31.2 all-gather.7
  124.0 233.8 all-gather.9
where the time goes:
time: 556 us; the launch traced here: 551 us
  other arithmetic  151 us (27%)
  blocking collectives  142 us (26%)
  matrix products  106 us (19%)
  loops' own time  82.4 us (15%)
  waiting for transfers between devices  25 us (4%)
  starting transfers between devices  17.4 us (3%)
  between operations  14 us (3%)
  local copies, waits for them, and re-layouts  12.3 us (2%)
    select_n x63, other arithmetic, step(): jnp.where(position < mine, new, old)  91.9 us
    another operation x4, loops' own time, per_block(): lax.fori_loop(0, key_total // key_span, per_span, (best_start, mass_start...  77.7 us
    dot_general x40, matrix products, compute(): jnp.einsum('qhk,khd->qhd', expo.astype(jnp.bfloat16), value_tile, preferr...  53.2 us
    dot_general x40, matrix products, compute(): jnp.einsum('qhd,khd->qhk', query_tile, key_tile, preferred_element_type=j...  49.3 us
    all_gather x1, blocking collectives, entering(): pieces = jax.tree.map(lambda part: lax.all_gather(part, axis), value)  48.1 us
    reduce_min x64, other arithmetic, per_span(): jnp.min(key_where) <= latest_query  43.1 us
    all_to_all x1, blocking collectives, softmax_core(): lax.all_to_all(key_moved, 'ctx', split_axis=1, concat_axis=0, tiled=True)  31.3 us
    all_to_all x1, blocking collectives, softmax_core(): lax.all_to_all(value_moved, 'ctx', split_axis=1, concat_axis=0, tiled=True)  24.3 us
  transfers between devices with their start and end apart: 6, of which 2 were waited for; matrix products, arithmetic and copies ran while one was open for 31% of the time, Pallas kernels for 0%

commit v1 on v0

v1 whole, which is shorter than its diff:
```python
import functools
import math

import jax
import jax.numpy as jnp
import numpy as np
from jax import lax
from jax.experimental import pallas as pl
from jax.experimental.pallas import tpu as pltpu
from jax.sharding import PartitionSpec as P

HEAD_DIM = 128
TOKENS = 128
HEADS_HERE = 16
BLOCKS = 64
PIECE = 32

norm_eps = 1e-06
masked_score = -1e30
exponent_scale = HEAD_DIM ** (-0.5) * math.log2(math.e)
X_STEP = 16
QUERY_TILE = 8


def place_of(device):
    x, z, core = device // 16, device // 2 % 8, device % 2
    return 2 * z + x // 2, 2 * (x % 2) + core


def columns(head):
    return slice(head * HEAD_DIM, (head + 1) * HEAD_DIM)


def rows(quarter):
    return slice(quarter * PIECE, (quarter + 1) * PIECE)


def whole():
    return pl.BlockSpec(memory_space=pltpu.VMEM)


def dot(left, right, left_dim, right_dim, precision=None):
    return lax.dot_general(
        left,
        right,
        (((left_dim,), (right_dim,)), ((), ())),
        precision=precision,
        preferred_element_type=jnp.float32,
    )


def call(kernel, out_shape, operands, flops, scratch=(), smem=0):
    bytes_in = sum(math.prod(o.shape) * o.dtype.itemsize for o in operands)
    bytes_out = math.prod(out_shape.shape) * out_shape.dtype.itemsize
    return pl.pallas_call(
        kernel,
        out_shape=out_shape,
        in_specs=[pl.BlockSpec(memory_space=pltpu.SMEM)] * smem
        + [whole() for _ in operands[smem:]],
        out_specs=whole(),
        scratch_shapes=list(scratch),
        compiler_params=pltpu.CompilerParams(vmem_limit_bytes=48 << 20),
        cost_estimate=pl.CostEstimate(
            flops=flops, bytes_accessed=bytes_in + bytes_out, transcendentals=0
        ),
    )(*operands)


def pack_keys_kernel(key_ref, value_ref, out_ref):
    for device in range(BLOCKS):
        head, quarter = place_of(device)
        out_ref[device, 0:PIECE, :] = key_ref[rows(quarter), columns(head)]
        out_ref[device, PIECE : 2 * PIECE, :] = value_ref[rows(quarter), columns(head)]


def lower_triangle():
    shape = (TOKENS, TOKENS)
    return lax.broadcasted_iota(jnp.int32, shape, 0) >= lax.broadcasted_iota(jnp.int32, shape, 1)


def running_sums(decay):
    ones = jnp.where(lower_triangle(), 1.0, 0.0).astype(jnp.float32)
    return dot(ones, decay, 1, 0, lax.Precision.HIGHEST)


def states_kernel(key_ref, value_ref, decay_ref, query_ref, out_ref):
    running_sum = running_sums(decay_ref[...])
    part = lax.broadcasted_iota(jnp.int32, (8, HEAD_DIM), 0)
    for head in range(HEADS_HERE):
        sums = running_sum[:, head : head + 1]
        ending = running_sum[TOKENS - 1 : TOKENS, head : head + 1]
        key_wide = key_ref[:, columns(head)].astype(jnp.float32)
        key_scaled = (key_wide * jnp.exp(ending - sums)).astype(jnp.bfloat16)
        state = dot(key_scaled, value_ref[:, columns(head)], 0, 0).astype(jnp.bfloat16)
        coarse = ending.astype(jnp.bfloat16).astype(jnp.float32)
        middle = (ending - coarse).astype(jnp.bfloat16).astype(jnp.float32)
        fine = ending - coarse - middle
        parts = jnp.where(part == 0, coarse, jnp.where(part == 1, middle, fine))
        parts = parts.astype(jnp.bfloat16)
        for quarter in range(4):
            out_ref[4 * head + quarter, PIECE : 2 * PIECE, :] = state[rows(quarter), :]
            out_ref[4 * head + quarter, 2 * PIECE :, :] = parts
    for device in range(BLOCKS):
        head, quarter = place_of(device)
        out_ref[device, 0:PIECE, :] = query_ref[rows(quarter), columns(head)]


def scan_kernel(moved_ref, out_ref):
    def step(block, carry):
        out_ref[block] = carry.astype(jnp.bfloat16)
        parts = moved_ref[block, 2 * PIECE :, :].astype(jnp.float32)
        ending = parts[0:1] + parts[1:2] + parts[2:3]
        state = moved_ref[block, PIECE : 2 * PIECE, :].astype(jnp.float32)
        return jnp.exp(ending) * carry + state

    lax.fori_loop(0, BLOCKS, step, jnp.zeros((PIECE, HEAD_DIM), jnp.float32), unroll=4)


def attention_kernel(quarter_ref, query_ref, kv0, kv1, kv2, kv3, out_ref, best_ref, total_ref):
    segments = (kv0, kv1, kv2, kv3)
    mine = quarter_ref[0]
    count = QUERY_TILE * PIECE
    ones = jnp.ones((count, HEAD_DIM), jnp.bfloat16)

    def tile(index):
        return pl.ds(pl.multiple_of(index * QUERY_TILE, QUERY_TILE), QUERY_TILE)

    def positions(dim, quarter):
        row = lax.broadcasted_iota(jnp.int32, (count, count), dim)
        return (row // PIECE) * TOKENS + row % PIECE + quarter * PIECE

    def per_tile(query_tile, nothing):
        query = query_ref[tile(query_tile), 0:PIECE, :].reshape(count, HEAD_DIM)
        best_ref[...] = jnp.full_like(best_ref, masked_score)
        total_ref[...] = jnp.zeros_like(total_ref)

        def attend(key_tile, masked):
            scores = []
            for which, segment in enumerate(segments):
                key = segment[tile(key_tile), 0:PIECE, :].reshape(count, HEAD_DIM)
                score = dot(query, key, 1, 1)
                if masked:
                    allowed = positions(1, mine ^ which) <= positions(0, mine)
                    score = jnp.where(allowed, score, masked_score)
                scores.append(score)
            top = functools.reduce(jnp.maximum, scores)
            best = best_ref[...]
            best_next = jnp.maximum(best, jnp.max(top, axis=1, keepdims=True))
            best_ref[...] = best_next
            shrink = jnp.exp2((best - best_next) * exponent_scale)
            best_wide = jnp.concatenate([best_next, best_next], axis=1)
            total = total_ref[...] * jnp.concatenate([shrink, shrink], axis=1)
            for score, segment in zip(scores, segments):
                weight = jnp.exp2((score - best_wide) * exponent_scale).astype(jnp.bfloat16)
                value = segment[tile(key_tile), PIECE : 2 * PIECE, :].reshape(count, HEAD_DIM)
                total += dot(weight, jnp.concatenate([value, ones], axis=1), 1, 0)
            total_ref[...] = total

        def unmasked(key_tile, nothing):
            attend(key_tile, False)
            return nothing

        lax.fori_loop(0, query_tile, unmasked, 0)
        attend(query_tile, True)
        outcome = total_ref[:, :HEAD_DIM] / total_ref[:, HEAD_DIM:]
        out_ref[tile(query_tile)] = outcome.astype(jnp.bfloat16).reshape(
            QUERY_TILE, PIECE, HEAD_DIM
        )
        return nothing

    lax.fori_loop(0, BLOCKS // QUERY_TILE, per_tile, 0)


def lightning_kernel(query_ref, key_ref, value_ref, decay_ref, prior_ref, out_ref):
    decay = decay_ref[...]
    causal = lower_triangle()
    running_sum = running_sums(decay)
    later = jnp.where(causal, 0.0, 1.0).astype(jnp.float32)
    shape = (TOKENS, TOKENS)
    upper = lax.broadcasted_iota(jnp.int32, shape, 0) <= lax.broadcasted_iota(jnp.int32, shape, 1)
    upper = jnp.where(upper, 1.0, 0.0).astype(jnp.float32)
    running_row = dot(decay, upper, 0, 0, lax.Precision.HIGHEST)
    for head in range(HEADS_HERE):
        sums = running_sum[:, head : head + 1]
        spread = sums - running_row[head : head + 1, :]
        query = query_ref[:, columns(head)]
        value = value_ref[:, columns(head)]
        scores = dot(query, key_ref[:, columns(head)], 1, 1)
        decayed = jnp.where(causal, jnp.exp(jnp.where(causal, spread, 0.0)), 0.0) * scores
        total = dot(decayed.astype(jnp.bfloat16), value, 1, 0)
        query_scaled = (query.astype(jnp.float32) * jnp.exp(sums)).astype(jnp.bfloat16)
        prior = prior_ref[4 * head : 4 * head + 4].reshape(HEAD_DIM, HEAD_DIM)
        total += dot(query_scaled, prior, 1, 0)
        mean = jnp.mean(total * total, axis=1, keepdims=True)
        out_ref[:, columns(head)] = (total * lax.rsqrt(mean + norm_eps)).astype(jnp.bfloat16)


def unpack_kernel(moved_ref, out_ref):
    for device in range(BLOCKS):
        head, quarter = place_of(device)
        out_ref[rows(quarter), columns(head)] = moved_ref[device]


def exchange(value):
    return lax.all_to_all(value, "ctx", split_axis=0, concat_axis=0, tiled=True)


def swap(value, step):
    return lax.ppermute(value, "ctx", [(d, d ^ step) for d in range(BLOCKS)])


def shards(lin_query, lin_key, lin_value, log_decay, soft_query, soft_key, soft_value):
    half = jnp.bfloat16
    shape = jax.ShapeDtypeStruct
    index = lax.axis_index("ctx")
    quarter = (index // X_STEP % 2 * 2 + index % 2).astype(jnp.int32).reshape(1)

    packed_keys = call(
        pack_keys_kernel, shape((BLOCKS, 2 * PIECE, HEAD_DIM), half), (soft_key, soft_value), 1000
    )
    kv0 = exchange(packed_keys)
    packed_queries = call(
        states_kernel,
        shape((BLOCKS, 2 * PIECE + 8, HEAD_DIM), half),
        (lin_key, lin_value, log_decay, soft_query),
        10**8,
    )
    kv2 = swap(kv0, X_STEP)
    kv1 = swap(kv0, 1)
    queries = exchange(packed_queries)
    kv3 = swap(kv2, 1)
    piece = shape((BLOCKS, PIECE, HEAD_DIM), half)
    prior = exchange(call(scan_kernel, piece, (queries,), 10**6))
    count = QUERY_TILE * PIECE
    attended = call(
        attention_kernel,
        piece,
        (quarter, queries, kv0, kv1, kv2, kv3),
        10**10,
        (
            pltpu.VMEM((count, HEAD_DIM), jnp.float32),
            pltpu.VMEM((count, 2 * HEAD_DIM), jnp.float32),
        ),
        smem=1,
    )
    returned = exchange(attended)
    whole_out = shape((TOKENS, HEADS_HERE * HEAD_DIM), half)
    lin_out = call(
        lightning_kernel, whole_out, (lin_query, lin_key, lin_value, log_decay, prior), 2 * 10**8
    )
    soft_out = call(unpack_kernel, whole_out, (returned,), 1000)
    return (lin_out, soft_out)


def solution(mesh):
    spec = P("ctx", "head")
    return jax.shard_map(
        shards, mesh=mesh, in_specs=(spec,) * 7, out_specs=(spec, spec), check_vma=False
    )
```

time: 556 us -> 163 us (0.29)
  other arithmetic: 151 us -> 0 us
  blocking collectives: 142 us -> 0 us
  matrix products: 106 us -> 0 us
  loops' own time: 82.4 us -> 0 us
  waiting for transfers between devices: 25 us -> 75.1 us
  Pallas kernels: 0 us -> 42.2 us
  starting transfers between devices: 17.4 us -> 42.6 us
  between operations: 14 us -> 0.77 us
  local copies, waits for them, and re-layouts: 12.3 us -> 2.19 us
    dot_general x83 -> x0, matrix products: 106 us -> none  [the longest x40 53.2 us: compute(): jnp.einsum('qhk,khd->qhd', expo.astype(jnp.bfloat16), value_tile, preferr...]
    all_to_all x5 -> x0, blocking collectives: 93.8 us -> none  [the longest x1 31.3 us: softmax_core(): lax.all_to_all(key_moved, 'ctx', split_axis=1, concat_axis=0, tiled=True)]
    select_n x63 -> x0, other arithmetic: 91.9 us -> none  [step(): jnp.where(position < mine, new, old)]
    another operation x70 -> x0, loops' own time: 82.4 us -> none  [the longest x4 77.7 us: per_block(): lax.fori_loop(0, key_total // key_span, per_span, (best_start, mass_start...]
    all_gather x1 -> x0, blocking collectives: 48.1 us -> none  [entering(): pieces = jax.tree.map(lambda part: lax.all_gather(part, axis), value)]
    reduce_min x64 -> x0, other arithmetic: 43.1 us -> none  [per_span(): jnp.min(key_where) <= latest_query]
    pallas_call x0 -> x6, Pallas kernels: none -> 42.2 us  [call(): pl.pallas_call(kernel, out_shape=out_shape, in_specs=[pl.BlockSpec(memory...]
    ppermute x0 -> x3, waiting for transfers between devices: none -> 35.1 us  [swap(): return lax.ppermute(value, 'ctx', [(d, d ^ step) for d in range(BLOCKS)])]
  transfers between devices with their start and end apart: 6 -> 7, of which waited for: 2 -> 3; matrix products, arithmetic and copies ran while one was open for 31% -> 0% of each run, Pallas kernels for 0% -> 25%
where the time goes in v1:
time: 163 us
  waiting for transfers between devices  75.1 us (46%)
  starting transfers between devices  42.6 us (26%)
  Pallas kernels  42.2 us (26%)
  local copies, waits for them, and re-layouts  2.19 us (1%)
    pallas_call x6, Pallas kernels, call(): pl.pallas_call(kernel, out_shape=out_shape, in_specs=[pl.BlockSpec(memory...  42.2 us
    all_to_all x4, waiting for transfers between devices, exchange(): return lax.all_to_all(value, 'ctx', split_axis=0, concat_axis=0, tiled=True)  40 us
    all_to_all x4, starting transfers between devices, exchange(): return lax.all_to_all(value, 'ctx', split_axis=0, concat_axis=0, tiled=True)  39.6 us
    ppermute x3, waiting for transfers between devices, swap(): return lax.ppermute(value, 'ctx', [(d, d ^ step) for d in range(BLOCKS)])  35.1 us
  transfers between devices with their start and end apart: 7, of which 3 were waited for; matrix products, arithmetic and copies ran while one was open for 0% of the time, Pallas kernels for 25%

profile of v1, /device:TPU:1, one launch (start us, length us, event | category | flops | bytes accessed | tf_op | source)
XLA Modules:
  0.0 162.9 jit_solution(4166822659476286437)
XLA Ops:
  0.6 0.0 copy-start.2
  0.6 1.0 copy-done.2
  1.7 0.0 copy-start.3
  1.7 1.0 copy-done.3
  2.7 1.2 shard_map.89
  3.9 0.0 copy-start.6
  3.9 0.0 copy-start
  3.9 0.0 copy-start.1
  3.9 0.0 copy-start.4
  3.9 13.3 %all-to-all-start.2 = ((bf16[64,64,128]{2,1,0:T(8,128)(2,1)}), bf16[64,64,128]{2,1,0:T(8,128)(2,1)}, u32[]{:S(2)}, u32[]{:S(2)}) async-start(bf16[64,64,128]{2,1,0:T(8,128)(2,1)} %shard_map.89), calls=%async_computation.2 | async-start | bytes 2097152 | tf_op jit(solution)/shard_map/all_to_all | solution.py:205
  17.2 0.0 copy-done.6
  17.2 0.1 copy.10.decay_ref
  17.3 0.0 copy-done
  17.3 0.0 copy-done.1
  17.3 0.0 copy-done.4
  17.4 2.2 %shard_map.86 = bf16[64,72,128]{2,1,0:T(8,128)(2,1)} custom-call(bf16[128,2048]{1,0:T(8,128)(2,1)S(1)} %copy-done, bf16[128,2048]{1,0:T(8,128)(2,1)S(1)} %copy-done.1, f32[128,16]{1,0:T(8,128)S(1)} %copy.10.decay_ref, bf16[128,2048]{1,0:T(8,128)(2,1)S(1)} %copy-done.4), custom_call_target="tpu_custom_call" | custom-call | flops 100000000 | bytes 2760704 | tf_op jit(solution)/shard_map/pallas_call | solution.py:55
  19.5 26.2 %all-to-all-done.2.kv0 = bf16[64,64,128]{2,1,0:T(8,128)(2,1)} async-done(((bf16[64,64,128]{2,1,0:T(8,128)(2,1)}), bf16[64,64,128]{2,1,0:T(8,128)(2,1)}, u32[]{:S(2)}, u32[]{:S(2)}) %all-to-all-start.2) | async-done | bytes 1048608 | tf_op jit(solution)/shard_map/all_to_all | solution.py:205
  45.7 6.2 %all-to-all-start = ((bf16[64,72,128]{2,1,0:T(8,128)(2,1)}), bf16[64,72,128]{2,1,0:T(8,128)(2,1)S(1)}, u32[]{:S(2)}, u32[]{:S(2)}) async-start(bf16[64,72,128]{2,1,0:T(8,128)(2,1)} %shard_map.86), calls=%async_computation | async-start | bytes 2359296 | tf_op jit(solution)/shard_map/all_to_all | solution.py:205
  51.9 1.5 collective-permute-start.1
  53.4 0.6 collective-permute-start
  54.0 35.1 %collective-permute-done.1.kv2 = bf16[64,64,128]{2,1,0:T(8,128)(2,1)} collective-permute-done((bf16[64,64,128]{2,1,0:T(8,128)(2,1)}, bf16[64,64,128]{2,1,0:T(8,128)(2,1)}, u32[]{:S(2)}, u32[]{:S(2)}) %collective-permute-start.1) | collective-permute-done | bytes 1048608 | tf_op jit(solution)/shard_map/ppermute | solution.py:209
  89.1 0.9 collective-permute-start.2
  90.0 0.0 all-to-all-done.moved_ref.query_ref
  90.0 1.2 shard_map.87
  91.2 9.7 %all-to-all-start.1 = ((bf16[64,32,128]{2,1,0:T(8,128)(2,1)}), bf16[64,32,128]{2,1,0:T(8,128)(2,1)S(1)}, u32[]{:S(2)}, u32[]{:S(2)}) async-start(bf16[64,32,128]{2,1,0:T(8,128)(2,1)} %shard_map.87), calls=%async_computation.1 | async-start | bytes 1048576 | tf_op jit(solution)/shard_map/all_to_all | solution.py:205
  100.9 0.0 collective-permute-done.kv1
  100.9 0.0 collective-permute-done.2.kv3
  100.9 33.3 %shard_map.90 = bf16[64,32,128]{2,1,0:T(8,128)(2,1)} custom-call(s32[1]{0:T(128)} %bitcast.quarter_ref, bf16[64,72,128]{2,1,0:T(8,128)(2,1)S(1)} %all-to-all-done.moved_ref.query_ref, bf16[64,64,128]{2,1,0:T(8,128)(2,1)} %all-to-all-done.2.kv0, bf16[64,64,128]{2,1,0:T(8,128)(2,1)} %collective-permute-done.kv1, ...), custom_call_target="tpu_custom_call" | custom-call | flops 10000000000 | bytes 5898244 | tf_op jit(solution)/shard_map/pallas_call | solution.py:55
  134.2 0.0 copy-start.5
  134.2 0.0 all-to-all-done.1.prior_ref
  134.2 10.5 %all-to-all-start.3 = ((bf16[64,32,128]{2,1,0:T(8,128)(2,1)}), bf16[64,32,128]{2,1,0:T(8,128)(2,1)S(1)}, u32[]{:S(2)}, u32[]{:S(2)}) async-start(bf16[64,32,128]{2,1,0:T(8,128)(2,1)} %shard_map.90), calls=%async_computation.3 | async-start | bytes 1048576 | tf_op jit(solution)/shard_map/all_to_all | solution.py:205
  144.7 0.0 copy-done.5
  144.7 3.5 %shard_map.88 = bf16[128,2048]{1,0:T(8,128)(2,1)} custom-call(bf16[128,2048]{1,0:T(8,128)(2,1)S(1)} %copy-done.5, bf16[128,2048]{1,0:T(8,128)(2,1)S(1)} %copy-done, bf16[128,2048]{1,0:T(8,128)(2,1)S(1)} %copy-done.1, f32[128,16]{1,0:T(8,128)S(1)} %copy.10.decay_ref, bf16[64,32,128]{2,1,0:T(8,128)(2,1)S(1)} %all-to-all-done.1.prior_ref), custom_call_target="tpu_custom_call" | custom-call | flops 200000000 | bytes 2629632 | tf_op jit(solution)/shard_map/pallas_call | solution.py:55
  148.2 13.9 %all-to-all-done.3.moved_ref = bf16[64,32,128]{2,1,0:T(8,128)(2,1)S(1)} async-done(((bf16[64,32,128]{2,1,0:T(8,128)(2,1)}), bf16[64,32,128]{2,1,0:T(8,128)(2,1)S(1)}, u32[]{:S(2)}, u32[]{:S(2)}) %all-to-all-start.3) | async-done | bytes 524320 | tf_op jit(solution)/shard_map/all_to_all | solution.py:205
  162.0 0.9 shard_map.91
Async XLA Ops:
  0.6 1.0 copy-start.2
  1.7 1.0 copy-start.3
  3.9 13.3 %copy-start.6 = (f32[128,16]{0,1:T(8,128)S(1)}, f32[128,16]{0,1:T(8,128)}, u32[]{:S(2)}) copy-start(f32[128,16]{0,1:T(8,128)} %param.10) | copy-start | bytes 24580
  3.9 13.4 %copy-start = (bf16[128,2048]{1,0:T(8,128)(2,1)S(1)}, bf16[128,2048]{1,0:T(8,128)(2,1)}, u32[]{:S(2)}) copy-start(bf16[128,2048]{1,0:T(8,128)(2,1)} %key_ref.4) | copy-start | bytes 1572868
  3.9 13.5 %copy-start.1 = (bf16[128,2048]{1,0:T(8,128)(2,1)S(1)}, bf16[128,2048]{1,0:T(8,128)(2,1)}, u32[]{:S(2)}) copy-start(bf16[128,2048]{1,0:T(8,128)(2,1)} %value_ref.4) | copy-start | bytes 1572868
  3.9 13.5 %copy-start.4 = (bf16[128,2048]{1,0:T(8,128)(2,1)S(1)}, bf16[128,2048]{1,0:T(8,128)(2,1)}, u32[]{:S(2)}) copy-start(bf16[128,2048]{1,0:T(8,128)(2,1)} %query_ref.2) | copy-start | bytes 1572868
  3.9 41.8 %all-to-all-start.2 = ((bf16[64,64,128]{2,1,0:T(8,128)(2,1)}), bf16[64,64,128]{2,1,0:T(8,128)(2,1)}, u32[]{:S(2)}, u32[]{:S(2)}) async-start(bf16[64,64,128]{2,1,0:T(8,128)(2,1)} %shard_map.89), calls=%async_computation.2 | async-start | bytes 2097152 | tf_op jit(solution)/shard_map/all_to_all | solution.py:205
  45.7 44.3 %all-to-all-start = ((bf16[64,72,128]{2,1,0:T(8,128)(2,1)}), bf16[64,72,128]{2,1,0:T(8,128)(2,1)S(1)}, u32[]{:S(2)}, u32[]{:S(2)}) async-start(bf16[64,72,128]{2,1,0:T(8,128)(2,1)} %shard_map.86), calls=%async_computation | async-start | bytes 2359296 | tf_op jit(solution)/shard_map/all_to_all | solution.py:205
  51.9 37.2 %collective-permute-start.1 = (bf16[64,64,128]{2,1,0:T(8,128)(2,1)}, bf16[64,64,128]{2,1,0:T(8,128)(2,1)}, u32[]{:S(2)}, u32[]{:S(2)}) collective-permute-start(bf16[64,64,128]{2,1,0:T(8,128)(2,1)} %all-to-all-done.2.kv0), channel_id=1, source_target_pairs={{0,64},{4,68},{8,72},{12,76},{16,80},{20,84},{24,88},{28,92},{32,9... | collective-permute-start | bytes 3145736 | tf_op jit(solution)/shard_map/ppermute | solution.py:209
  53.4 47.5 %collective-permute-start = (bf16[64,64,128]{2,1,0:T(8,128)(2,1)}, bf16[64,64,128]{2,1,0:T(8,128)(2,1)}, u32[]{:S(2)}, u32[]{:S(2)}) collective-permute-start(bf16[64,64,128]{2,1,0:T(8,128)(2,1)} %all-to-all-done.2.kv0), channel_id=1, source_target_pairs={{0,4},{4,0},{8,12},{12,8},{16,20},{20,16},{24,28},{28,24},{32,36},... | collective-permute-start | bytes 3145736 | tf_op jit(solution)/shard_map/ppermute | solution.py:209
  89.1 11.8 %collective-permute-start.2 = (bf16[64,64,128]{2,1,0:T(8,128)(2,1)}, bf16[64,64,128]{2,1,0:T(8,128)(2,1)}, u32[]{:S(2)}, u32[]{:S(2)}) collective-permute-start(bf16[64,64,128]{2,1,0:T(8,128)(2,1)} %collective-permute-done.1.kv2), channel_id=1, source_target_pairs={{0,4},{4,0},{8,12},{12,8},{16,20},{20,16},{24,28},{28,24},{32,36},... | collective-permute-start | bytes 3145736 | tf_op jit(solution)/shard_map/ppermute | solution.py:209
  91.2 43.1 %all-to-all-start.1 = ((bf16[64,32,128]{2,1,0:T(8,128)(2,1)}), bf16[64,32,128]{2,1,0:T(8,128)(2,1)S(1)}, u32[]{:S(2)}, u32[]{:S(2)}) async-start(bf16[64,32,128]{2,1,0:T(8,128)(2,1)} %shard_map.87), calls=%async_computation.1 | async-start | bytes 1048576 | tf_op jit(solution)/shard_map/all_to_all | solution.py:205
  134.2 10.5 %copy-start.5 = (bf16[128,2048]{1,0:T(8,128)(2,1)S(1)}, bf16[128,2048]{1,0:T(8,128)(2,1)}, u32[]{:S(2)}) copy-start(bf16[128,2048]{1,0:T(8,128)(2,1)} %query_ref.3) | copy-start | bytes 1572868
  134.2 27.8 %all-to-all-start.3 = ((bf16[64,32,128]{2,1,0:T(8,128)(2,1)}), bf16[64,32,128]{2,1,0:T(8,128)(2,1)S(1)}, u32[]{:S(2)}, u32[]{:S(2)}) async-start(bf16[64,32,128]{2,1,0:T(8,128)(2,1)} %shard_map.90), calls=%async_computation.3 | async-start | bytes 1048576 | tf_op jit(solution)/shard_map/all_to_all | solution.py:205

commit v2 on v1

v2 whole, which is shorter than its diff:
```python
import functools
import math

import jax
import jax.numpy as jnp
import numpy as np
from jax import lax
from jax.experimental import pallas as pl
from jax.experimental.pallas import tpu as pltpu
from jax.sharding import PartitionSpec as P

HEAD_DIM = 128
TOKENS = 128
HEADS_HERE = 16
BLOCKS = 64
PIECE = 32

norm_eps = 1e-06
masked_score = -1e30
exponent_scale = HEAD_DIM ** (-0.5) * math.log2(math.e)
X_STEP = 16
QUERY_TILE = 16


def place_of(device):
    x, z, core = device // 16, device // 2 % 8, device % 2
    return 2 * z + x // 2, 2 * (x % 2) + core


def columns(head):
    return slice(head * HEAD_DIM, (head + 1) * HEAD_DIM)


def rows(quarter):
    return slice(quarter * PIECE, (quarter + 1) * PIECE)


def whole():
    return pl.BlockSpec(memory_space=pltpu.VMEM)


def dot(left, right, left_dim, right_dim, precision=None):
    return lax.dot_general(
        left,
        right,
        (((left_dim,), (right_dim,)), ((), ())),
        precision=precision,
        preferred_element_type=jnp.float32,
    )


def call(kernel, out_shape, operands, flops, scratch=(), smem=0, limit=16):
    moved = [*operands, *jax.tree.leaves(out_shape)]
    return pl.pallas_call(
        kernel,
        out_shape=out_shape,
        in_specs=[pl.BlockSpec(memory_space=pltpu.SMEM)] * smem
        + [whole() for _ in operands[smem:]],
        out_specs=jax.tree.map(lambda _: whole(), out_shape),
        scratch_shapes=list(scratch),
        compiler_params=pltpu.CompilerParams(vmem_limit_bytes=limit << 20),
        cost_estimate=pl.CostEstimate(
            flops=flops,
            bytes_accessed=sum(math.prod(o.shape) * o.dtype.itemsize for o in moved),
            transcendentals=0,
        ),
    )(*operands)


def pack_kernel(query_ref, key_ref, value_ref, out_ref):
    for device in range(BLOCKS):
        head, quarter = place_of(device)
        for which, source in enumerate((query_ref, key_ref, value_ref)):
            out_ref[device, rows(which), :] = source[rows(quarter), columns(head)]


def lower_triangle():
    shape = (TOKENS, TOKENS)
    return lax.broadcasted_iota(jnp.int32, shape, 0) >= lax.broadcasted_iota(jnp.int32, shape, 1)


def running_sums(decay):
    ones = jnp.where(lower_triangle(), 1.0, 0.0).astype(jnp.float32)
    return dot(ones, decay, 1, 0, lax.Precision.HIGHEST)


def states_kernel(key_ref, value_ref, decay_ref, out_ref):
    running_sum = running_sums(decay_ref[...])
    part = lax.broadcasted_iota(jnp.int32, (8, HEAD_DIM), 0)
    for head in range(HEADS_HERE):
        sums = running_sum[:, head : head + 1]
        ending = running_sum[TOKENS - 1 : TOKENS, head : head + 1]
        key_wide = key_ref[:, columns(head)].astype(jnp.float32)
        key_scaled = (key_wide * jnp.exp(ending - sums)).astype(jnp.bfloat16)
        state = dot(key_scaled, value_ref[:, columns(head)], 0, 0).astype(jnp.bfloat16)
        coarse = ending.astype(jnp.bfloat16).astype(jnp.float32)
        middle = (ending - coarse).astype(jnp.bfloat16).astype(jnp.float32)
        fine = ending - coarse - middle
        parts = jnp.where(part == 0, coarse, jnp.where(part == 1, middle, fine))
        parts = parts.astype(jnp.bfloat16)
        for quarter in range(4):
            out_ref[4 * head + quarter, 0:PIECE, :] = state[rows(quarter), :]
            out_ref[4 * head + quarter, PIECE:, :] = parts


def scan_kernel(moved_ref, out_ref):
    def step(block, carry):
        out_ref[block] = carry.astype(jnp.bfloat16)
        parts = moved_ref[block, PIECE:, :].astype(jnp.float32)
        ending = parts[0:1] + parts[1:2] + parts[2:3]
        state = moved_ref[block, 0:PIECE, :].astype(jnp.float32)
        return jnp.exp(ending) * carry + state

    lax.fori_loop(0, BLOCKS, step, jnp.zeros((PIECE, HEAD_DIM), jnp.float32), unroll=4)


def attention_kernel(
    which, first, last_tile, has_state, finishes, quarter_ref, query_ref, *refs
):
    count = QUERY_TILE * PIECE
    number = len(which)
    segments, refs = refs[:number], refs[number:]
    if has_state:
        (best_in, total_in), refs = refs[:2], refs[3:]
    results, (best_ref, total_ref, score_ref, bias_ref) = refs[:-4], refs[-4:]
    mine = quarter_ref[0]
    ones = jnp.ones((count, HEAD_DIM), jnp.bfloat16)
    lanes = count // HEAD_DIM

    def tile(index):
        return pl.ds(pl.multiple_of(index * QUERY_TILE, QUERY_TILE), QUERY_TILE)

    def tile_rows(index):
        return pl.ds(pl.multiple_of(index * count, count), count)

    def positions(shape, dim, quarter):
        row = lax.broadcasted_iota(jnp.int32, shape, dim)
        return (row // PIECE) * TOKENS + row % PIECE + quarter * PIECE

    def widen(value):
        return jnp.concatenate([value] * lanes, axis=1)

    query_places = widen(positions((count, HEAD_DIM), 0, mine))
    for slot, step in enumerate(which):
        allowed = positions((1, count), 1, mine ^ step) <= query_places
        bias_ref[slot] = jnp.where(allowed, 0.0, masked_score)

    def per_tile(query_tile, carry):
        query = query_ref[tile(query_tile), rows(0), :].reshape(count, HEAD_DIM)
        if has_state:
            best_ref[...] = best_in[tile_rows(query_tile), :]
        else:
            best_ref[...] = jnp.full_like(best_ref, masked_score)

        def find_best(key_tile, masked):
            best = best_ref[...]
            for slot, segment in enumerate(segments):
                key = segment[tile(key_tile), rows(segment.shape[1] // PIECE - 2), :].reshape(count, HEAD_DIM)
                score = dot(query, key, 1, 1)
                if masked:
                    score += bias_ref[slot]
                score_ref[number * (key_tile - first) + slot] = score
                for lane in range(lanes):
                    best = jnp.maximum(best, score[:, columns(lane)])
            best_ref[...] = best

        def unmasked(key_tile, nothing):
            find_best(key_tile, False)
            return nothing

        lax.fori_loop(first, jnp.minimum(query_tile, last_tile), unmasked, 0)

        @pl.when(jnp.logical_and(query_tile >= first, query_tile < last_tile))
        def _():
            find_best(query_tile, True)

        best = jnp.broadcast_to(jnp.max(best_ref[...], axis=1, keepdims=True), best_ref.shape)
        best_ref[...] = best
        if has_state:
            shrink = jnp.exp2((best_in[tile_rows(query_tile), :] - best) * exponent_scale)
            total_ref[...] = total_in[tile_rows(query_tile), :] * jnp.concatenate(
                [shrink, shrink], axis=1
            )
        else:
            total_ref[...] = jnp.zeros_like(total_ref)

        def add_up(key_tile, nothing):
            best_wide = widen(best_ref[...])
            weights, values = [], []
            for slot, segment in enumerate(segments):
                score = score_ref[number * (key_tile - first) + slot]
                weight = jnp.exp2((score - best_wide) * exponent_scale)
                weights.append(weight.astype(jnp.bfloat16))
                value = segment[tile(key_tile), rows(segment.shape[1] // PIECE - 1), :].reshape(count, HEAD_DIM)
                values.append(jnp.concatenate([value, ones], axis=1))
            total_ref[...] += dot(
                jnp.concatenate(weights, axis=1), jnp.concatenate(values, axis=0), 1, 0
            )
            return nothing

        lax.fori_loop(first, jnp.minimum(query_tile + 1, last_tile), add_up, 0)
        if finishes:
            outcome = total_ref[:, :HEAD_DIM] / total_ref[:, HEAD_DIM:]
            results[0][tile(query_tile)] = outcome.astype(jnp.bfloat16).reshape(
                QUERY_TILE, PIECE, HEAD_DIM
            )
        else:
            results[0][tile_rows(query_tile), :] = best_ref[...]
            results[1][tile_rows(query_tile), :] = total_ref[...]
        return carry

    lax.fori_loop(0, BLOCKS // QUERY_TILE, per_tile, 0)


def attend(which, key_tiles, quarter, queries, segments, state, finishes, token=()):
    shape = jax.ShapeDtypeStruct
    count = QUERY_TILE * PIECE
    first, last_tile = key_tiles
    kernel = functools.partial(
        attention_kernel, which, first, last_tile, state is not None, finishes
    )
    if finishes:
        out_shape = shape((BLOCKS, PIECE, HEAD_DIM), jnp.bfloat16)
    else:
        out_shape = (
            shape((BLOCKS * PIECE, HEAD_DIM), jnp.float32),
            shape((BLOCKS * PIECE, 2 * HEAD_DIM), jnp.float32),
        )
    return call(
        kernel,
        out_shape,
        (quarter, queries, *segments, *(state or ()), *token),
        3 * 10**9 * len(which),
        (
            pltpu.VMEM((count, HEAD_DIM), jnp.float32),
            pltpu.VMEM((count, 2 * HEAD_DIM), jnp.float32),
            pltpu.VMEM((len(which) * (last_tile - first), count, count), jnp.float32),
            pltpu.VMEM((len(which), count, count), jnp.float32),
        ),
        smem=1,
        limit=24,
    )


def lightning_kernel(query_ref, key_ref, value_ref, decay_ref, prior_ref, out_ref):
    decay = decay_ref[...]
    causal = lower_triangle()
    running_sum = running_sums(decay)
    later = jnp.where(causal, 0.0, 1.0).astype(jnp.float32)
    shape = (TOKENS, TOKENS)
    upper = lax.broadcasted_iota(jnp.int32, shape, 0) <= lax.broadcasted_iota(jnp.int32, shape, 1)
    upper = jnp.where(upper, 1.0, 0.0).astype(jnp.float32)
    running_row = dot(decay, upper, 0, 0, lax.Precision.HIGHEST)
    for head in range(HEADS_HERE):
        sums = running_sum[:, head : head + 1]
        spread = sums - running_row[head : head + 1, :]
        query = query_ref[:, columns(head)]
        value = value_ref[:, columns(head)]
        scores = dot(query, key_ref[:, columns(head)], 1, 1)
        decayed = jnp.where(causal, jnp.exp(jnp.where(causal, spread, 0.0)), 0.0) * scores
        total = dot(decayed.astype(jnp.bfloat16), value, 1, 0)
        query_scaled = (query.astype(jnp.float32) * jnp.exp(sums)).astype(jnp.bfloat16)
        prior = prior_ref[4 * head : 4 * head + 4].reshape(HEAD_DIM, HEAD_DIM)
        total += dot(query_scaled, prior, 1, 0)
        mean = jnp.mean(total * total, axis=1, keepdims=True)
        out_ref[:, columns(head)] = (total * lax.rsqrt(mean + norm_eps)).astype(jnp.bfloat16)


def unpack_kernel(moved_ref, out_ref):
    for device in range(BLOCKS):
        head, quarter = place_of(device)
        out_ref[rows(quarter), columns(head)] = moved_ref[device]


def exchange(value):
    return lax.all_to_all(value, "ctx", split_axis=0, concat_axis=0, tiled=True)


def swap(value, step):
    return lax.ppermute(value, "ctx", [(d, d ^ step) for d in range(BLOCKS)])


def shards(lin_query, lin_key, lin_value, log_decay, soft_query, soft_key, soft_value):
    half = jnp.bfloat16
    shape = jax.ShapeDtypeStruct
    index = lax.axis_index("ctx")
    quarter = (index // X_STEP % 2 * 2 + index % 2).astype(jnp.int32).reshape(1)

    kv0 = exchange(
        call(
            pack_kernel,
            shape((BLOCKS, 3 * PIECE, HEAD_DIM), half),
            (soft_query, soft_key, soft_value),
            1000,
        )
    )
    states = call(
        states_kernel,
        shape((BLOCKS, PIECE + 8, HEAD_DIM), half),
        (lin_key, lin_value, log_decay),
        10**8,
    )
    kv0, states = lax.optimization_barrier((kv0, states))
    kv2 = swap(kv0[:, PIECE:], X_STEP)
    kv1 = swap(kv0[:, PIECE:], 1)
    moved_states = exchange(states)
    piece = shape((BLOCKS, PIECE, HEAD_DIM), half)
    tiles = (0, BLOCKS // QUERY_TILE)
    state = attend((0, 1), tiles, quarter, kv0, (kv0, kv1), None, False)
    token, kv2, moved_states = lax.optimization_barrier((state[0][0:8, :], kv2, moved_states))
    kv3 = swap(kv2, 1)
    prior = exchange(call(scan_kernel, piece, (moved_states,), 10**6))
    attended = attend((2, 3), tiles, quarter, kv0, (kv2, kv3), state, True, (token,))
    returned = exchange(attended)
    whole_out = shape((TOKENS, HEADS_HERE * HEAD_DIM), half)
    lin_out = call(
        lightning_kernel, whole_out, (lin_query, lin_key, lin_value, log_decay, prior), 2 * 10**8
    )
    soft_out = call(unpack_kernel, whole_out, (returned,), 1000)
    return (lin_out, soft_out)


def solution(mesh):
    spec = P("ctx", "head")
    return jax.shard_map(
        shards, mesh=mesh, in_specs=(spec,) * 7, out_specs=(spec, spec), check_vma=False
    )
```

time: 163 us -> 154 us (0.945)
  Pallas kernels: 42.2 us -> 32.7 us
  local copies, waits for them, and re-layouts: 2.19 us -> 11.3 us
  waiting for transfers between devices: 75.1 us -> 68.3 us
  starting transfers between devices: 42.6 us -> 39.7 us
    ppermute x3, waiting for transfers between devices: 35.1 us -> 16.7 us  [swap(): return lax.ppermute(value, 'ctx', [(d, d ^ step) for d in range(BLOCKS)])]
    all_to_all x4, waiting for transfers between devices: 40 us -> 51.5 us  [exchange(): return lax.all_to_all(value, 'ctx', split_axis=0, concat_axis=0, tiled=True)]
    pallas_call x6 -> x7, Pallas kernels: 42.2 us -> 32.7 us  [call(): pl.pallas_call(kernel, out_shape=out_shape, in_specs=[pl.BlockSpec(memory...]
    unnamed x15 -> x25, local copies, waits for them, and re-layouts: 2.19 us -> 10.2 us
    all_to_all x4, starting transfers between devices: 39.6 us -> 37.2 us  [exchange(): return lax.all_to_all(value, 'ctx', split_axis=0, concat_axis=0, tiled=True)]
  transfers between devices with their start and end apart: 7 -> 7, of which waited for: 3 -> 4; matrix products, arithmetic and copies ran while one was open for 0% -> 0% of each run, Pallas kernels for 25% -> 20%
where the time goes in v2:
time: 154 us; the launch traced here: 153 us
  waiting for transfers between devices  68.3 us (44%)
  starting transfers between devices  39.7 us (26%)
  Pallas kernels  32.7 us (21%)
  local copies, waits for them, and re-layouts  11.3 us (7%)
    all_to_all x4, waiting for transfers between devices, exchange(): return lax.all_to_all(value, 'ctx', split_axis=0, concat_axis=0, tiled=True)  51.5 us
    all_to_all x4, starting transfers between devices, exchange(): return lax.all_to_all(value, 'ctx', split_axis=0, concat_axis=0, tiled=True)  37.2 us
    pallas_call x7, Pallas kernels, call(): pl.pallas_call(kernel, out_shape=out_shape, in_specs=[pl.BlockSpec(memory...  32.7 us
    ppermute x3, waiting for transfers between devices, swap(): return lax.ppermute(value, 'ctx', [(d, d ^ step) for d in range(BLOCKS)])  16.7 us
    unnamed x25, local copies, waits for them, and re-layouts  10.2 us
  transfers between devices with their start and end apart: 7, of which 4 were waited for; matrix products, arithmetic and copies ran while one was open for 0% of the time, Pallas kernels for 20%

profile of v2, /device:TPU:1, one launch (start us, length us, event | category | flops | bytes accessed | tf_op | source)
XLA Modules:
  0.0 152.7 jit_solution(17073860819818748613)
XLA Ops:
  0.6 0.0 copy-start.3
  0.6 1.0 copy-done.3
  1.7 0.0 copy-start.4
  1.7 1.0 copy-done.4
  2.7 0.0 copy-start.5
  2.7 1.0 copy-done.5
  3.8 1.4 shard_map.86
  5.2 0.0 copy-start.11
  5.2 0.0 copy-start
  5.2 0.0 copy-start.1
  5.2 13.1 %all-to-all-start = ((bf16[64,96,128]{2,1,0:T(8,128)(2,1)}), bf16[64,96,128]{2,1,0:T(8,128)(2,1)S(1)}, u32[]{:S(2)}, u32[]{:S(2)}) async-start(bf16[64,96,128]{2,1,0:T(8,128)(2,1)} %shard_map.86), calls=%async_computation | async-start | bytes 3145728 | tf_op jit(solution)/shard_map/all_to_all | solution.py:276
  18.3 0.0 copy-done.11
  18.3 0.1 copy.10.decay_ref
  18.4 0.0 copy-done
  18.4 0.0 copy-done.1
  18.4 2.0 %shard_map.87 = bf16[64,40,128]{2,1,0:T(8,128)(2,1)} custom-call(bf16[128,2048]{1,0:T(8,128)(2,1)S(1)} %copy-done, bf16[128,2048]{1,0:T(8,128)(2,1)S(1)} %copy-done.1, f32[128,16]{1,0:T(8,128)S(1)} %copy.10.decay_ref), custom_call_target="tpu_custom_call" | custom-call | flops 100000000 | bytes 1712128 | tf_op jit(solution)/shard_map/pallas_call | solution.py:54
  20.4 37.7 %all-to-all-done.query_ref.refs_0_ = bf16[64,96,128]{2,1,0:T(8,128)(2,1)S(1)} async-done(((bf16[64,96,128]{2,1,0:T(8,128)(2,1)}), bf16[64,96,128]{2,1,0:T(8,128)(2,1)S(1)}, u32[]{:S(2)}, u32[]{:S(2)}) %all-to-all-start) | async-done | bytes 1572896 | tf_op jit(solution)/shard_map/all_to_all | solution.py:276
  58.1 1.1 slice.7
  59.2 0.2 collective-permute-start
  59.4 6.1 %all-to-all-start.1 = ((bf16[64,40,128]{2,1,0:T(8,128)(2,1)}), bf16[64,40,128]{2,1,0:T(8,128)(2,1)S(1)}, u32[]{:S(2)}, u32[]{:S(2)}) async-start(bf16[64,40,128]{2,1,0:T(8,128)(2,1)} %shard_map.87), calls=%async_computation.1 | async-start | bytes 1310720 | tf_op jit(solution)/shard_map/all_to_all | solution.py:276
  65.5 1.5 collective-permute-start.1
  67.0 0.0 collective-permute-done.refs_1_
  67.0 11.2 %shard_map.88 = (f32[2048,128]{1,0:T(8,128)S(1)}, f32[2048,256]{1,0:T(8,128)S(1)}) custom-call(s32[1]{0:T(128)} %bitcast.quarter_ref, bf16[64,96,128]{2,1,0:T(8,128)(2,1)S(1)} %all-to-all-done.query_ref.refs_0_, bf16[64,96,128]{2,1,0:T(8,128)(2,1)S(1)} %all-to-all-done.query_ref.refs_0_, bf16[64,64,128]{2,1,0:T(8,128)(2,1)} %collective-permute-done.refs_1_), custom_call_target="tpu_custom_call" | custom-call | flops 6000000000 | bytes 7340036 | tf_op jit(solution)/shard_map/pallas_call | solution.py:54
  78.2 0.0 copy-start.9
  78.2 1.3 copy-done.9
  79.5 0.0 copy-start.7
  79.5 1.0 copy-done.7
  80.5 16.7 %collective-permute-done.1.refs_0_ = bf16[64,64,128]{2,1,0:T(8,128)(2,1)} collective-permute-done((bf16[64,64,128]{2,1,0:T(8,128)(2,1)}, bf16[64,64,128]{2,1,0:T(8,128)(2,1)}, u32[]{:S(2)}, u32[]{:S(2)}) %collective-permute-start.1) | collective-permute-done | bytes 1048608 | tf_op jit(solution)/shard_map/ppermute | solution.py:280
  97.2 0.0 all-to-all-done.1.moved_ref
  97.2 0.8 collective-permute-start.2
  98.1 0.4 shard_map.89
  98.4 0.0 copy-start.2
  98.4 0.8 copy-done.2
  99.2 9.8 %all-to-all-start.2 = ((bf16[64,32,128]{2,1,0:T(8,128)(2,1)}), bf16[64,32,128]{2,1,0:T(8,128)(2,1)}, u32[]{:S(2)}, u32[]{:S(2)}) async-start(bf16[64,32,128]{2,1,0:T(8,128)(2,1)} %copy-done.2), calls=%async_computation.2 | async-start | bytes 1048576 | tf_op jit(solution)/shard_map/all_to_all | solution.py:276
  109.0 0.0 collective-permute-done.2.refs_1_
  109.0 0.0 copy-start.8
  109.0 1.2 copy-done.8
  110.3 0.0 copy-start.10
  110.3 1.6 %copy-done.10 = f32[2048,256]{1,0:T(8,128)S(1)} copy-done((f32[2048,256]{1,0:T(8,128)S(1)}, f32[2048,256]{1,0:T(8,128)}, u32[]{:S(2)}) %copy-start.10) | copy-done | bytes 2097176
  111.8 12.3 %shard_map.91 = bf16[64,32,128]{2,1,0:T(8,128)(2,1)} custom-call(s32[1]{0:T(128)} %bitcast.quarter_ref, bf16[64,96,128]{2,1,0:T(8,128)(2,1)S(1)} %all-to-all-done.query_ref.refs_0_, bf16[64,64,128]{2,1,0:T(8,128)(2,1)} %collective-permute-done.1.refs_0_, bf16[64,64,128]{2,1,0:T(8,128)(2,1)} %collective-permute-done.2.refs_1_, f32[2048,128]{1,0:T(8,128)S(1)} %copy-done.8, ...), custom_call_target="tpu_custom_call" | custom-call | flops 6000000000 | bytes 7344132 | tf_op jit(solution)/shard_map/pallas_call | solution.py:54
  124.2 2.1 %all-to-all-done.2.prior_ref = bf16[64,32,128]{2,1,0:T(8,128)(2,1)} async-done(((bf16[64,32,128]{2,1,0:T(8,128)(2,1)}), bf16[64,32,128]{2,1,0:T(8,128)(2,1)}, u32[]{:S(2)}, u32[]{:S(2)}) %all-to-all-start.2) | async-done | bytes 524320 | tf_op jit(solution)/shard_map/all_to_all | solution.py:276
  126.3 8.2 %all-to-all-start.3 = ((bf16[64,32,128]{2,1,0:T(8,128)(2,1)}), bf16[64,32,128]{2,1,0:T(8,128)(2,1)S(1)}, u32[]{:S(2)}, u32[]{:S(2)}) async-start(bf16[64,32,128]{2,1,0:T(8,128)(2,1)} %shard_map.91), calls=%async_computation.3 | async-start | bytes 1048576 | tf_op jit(solution)/shard_map/all_to_all | solution.py:276
  134.5 0.0 copy-start.6
  134.5 1.0 copy-done.6
  135.5 4.5 %shard_map.90 = bf16[128,2048]{1,0:T(8,128)(2,1)} custom-call(bf16[128,2048]{1,0:T(8,128)(2,1)S(1)} %copy-done.6, bf16[128,2048]{1,0:T(8,128)(2,1)S(1)} %copy-done, bf16[128,2048]{1,0:T(8,128)(2,1)S(1)} %copy-done.1, f32[128,16]{1,0:T(8,128)S(1)} %copy.10.decay_ref, bf16[64,32,128]{2,1,0:T(8,128)(2,1)} %all-to-all-done.2.prior_ref), custom_call_target="tpu_custom_call" | custom-call | flops 200000000 | bytes 2629632 | tf_op jit(solution)/shard_map/pallas_call | solution.py:54
  140.1 11.8 %all-to-all-done.3.moved_ref = bf16[64,32,128]{2,1,0:T(8,128)(2,1)S(1)} async-done(((bf16[64,32,128]{2,1,0:T(8,128)(2,1)}), bf16[64,32,128]{2,1,0:T(8,128)(2,1)S(1)}, u32[]{:S(2)}, u32[]{:S(2)}) %all-to-all-start.3) | async-done | bytes 524320 | tf_op jit(solution)/shard_map/all_to_all | solution.py:276
  151.8 0.9 shard_map.92
  (1 shorter events, 0.0 us)
Async XLA Ops:
  0.6 1.0 copy-start.3
  1.7 1.0 copy-start.4
  2.7 1.0 copy-start.5
  5.2 13.1 %copy-start.11 = (f32[128,16]{0,1:T(8,128)S(1)}, f32[128,16]{0,1:T(8,128)}, u32[]{:S(2)}) copy-start(f32[128,16]{0,1:T(8,128)} %param.10) | copy-start | bytes 24580
  5.2 13.2 %copy-start = (bf16[128,2048]{1,0:T(8,128)(2,1)S(1)}, bf16[128,2048]{1,0:T(8,128)(2,1)}, u32[]{:S(2)}) copy-start(bf16[128,2048]{1,0:T(8,128)(2,1)} %key_ref.5) | copy-start | bytes 1572868
  5.2 13.2 %copy-start.1 = (bf16[128,2048]{1,0:T(8,128)(2,1)S(1)}, bf16[128,2048]{1,0:T(8,128)(2,1)}, u32[]{:S(2)}) copy-start(bf16[128,2048]{1,0:T(8,128)(2,1)} %value_ref.5) | copy-start | bytes 1572868
  5.2 52.9 %all-to-all-start = ((bf16[64,96,128]{2,1,0:T(8,128)(2,1)}), bf16[64,96,128]{2,1,0:T(8,128)(2,1)S(1)}, u32[]{:S(2)}, u32[]{:S(2)}) async-start(bf16[64,96,128]{2,1,0:T(8,128)(2,1)} %shard_map.86), calls=%async_computation | async-start | bytes 3145728 | tf_op jit(solution)/shard_map/all_to_all | solution.py:276
  59.2 7.7 %collective-permute-start = (bf16[64,64,128]{2,1,0:T(8,128)(2,1)}, bf16[64,64,128]{2,1,0:T(8,128)(2,1)}, u32[]{:S(2)}, u32[]{:S(2)}) collective-permute-start(bf16[64,64,128]{2,1,0:T(8,128)(2,1)} %slice.7), channel_id=1, source_target_pairs={{0,4},{4,0},{8,12},{12,8},{16,20},{20,16},{24,28},{28,24},{32,36},... | collective-permute-start | bytes 3145736 | tf_op jit(solution)/shard_map/ppermute | solution.py:280
  59.4 37.8 %all-to-all-start.1 = ((bf16[64,40,128]{2,1,0:T(8,128)(2,1)}), bf16[64,40,128]{2,1,0:T(8,128)(2,1)S(1)}, u32[]{:S(2)}, u32[]{:S(2)}) async-start(bf16[64,40,128]{2,1,0:T(8,128)(2,1)} %shard_map.87), calls=%async_computation.1 | async-start | bytes 1310720 | tf_op jit(solution)/shard_map/all_to_all | solution.py:276
  65.5 31.7 %collective-permute-start.1 = (bf16[64,64,128]{2,1,0:T(8,128)(2,1)}, bf16[64,64,128]{2,1,0:T(8,128)(2,1)}, u32[]{:S(2)}, u32[]{:S(2)}) collective-permute-start(bf16[64,64,128]{2,1,0:T(8,128)(2,1)} %slice.7), channel_id=1, source_target_pairs={{0,64},{4,68},{8,72},{12,76},{16,80},{20,84},{24,88},{28,92},{32,9... | collective-permute-start | bytes 3145736 | tf_op jit(solution)/shard_map/ppermute | solution.py:280
  78.2 1.3 copy-start.9
  79.5 1.0 copy-start.7
  97.2 11.8 %collective-permute-start.2 = (bf16[64,64,128]{2,1,0:T(8,128)(2,1)}, bf16[64,64,128]{2,1,0:T(8,128)(2,1)}, u32[]{:S(2)}, u32[]{:S(2)}) collective-permute-start(bf16[64,64,128]{2,1,0:T(8,128)(2,1)} %collective-permute-done.1.refs_0_), channel_id=1, source_target_pairs={{0,4},{4,0},{8,12},{12,8},{16,20},{20,16},{24,28},{28,24},{32,36},... | collective-permute-start | bytes 3145736 | tf_op jit(solution)/shard_map/ppermute | solution.py:280
  98.4 0.8 copy-start.2
  99.2 27.0 %all-to-all-start.2 = ((bf16[64,32,128]{2,1,0:T(8,128)(2,1)}), bf16[64,32,128]{2,1,0:T(8,128)(2,1)}, u32[]{:S(2)}, u32[]{:S(2)}) async-start(bf16[64,32,128]{2,1,0:T(8,128)(2,1)} %copy-done.2), calls=%async_computation.2 | async-start | bytes 1048576 | tf_op jit(solution)/shard_map/all_to_all | solution.py:276
  109.0 1.2 copy-start.8
  110.3 1.6 %copy-start.10 = (f32[2048,256]{1,0:T(8,128)S(1)}, f32[2048,256]{1,0:T(8,128)}, u32[]{:S(2)}) copy-start(f32[2048,256]{1,0:T(8,128)} %copy-done.9) | copy-start | bytes 6291460
  126.3 25.6 %all-to-all-start.3 = ((bf16[64,32,128]{2,1,0:T(8,128)(2,1)}), bf16[64,32,128]{2,1,0:T(8,128)(2,1)S(1)}, u32[]{:S(2)}, u32[]{:S(2)}) async-start(bf16[64,32,128]{2,1,0:T(8,128)(2,1)} %shard_map.91), calls=%async_computation.3 | async-start | bytes 1048576 | tf_op jit(solution)/shard_map/all_to_all | solution.py:276
  134.5 1.0 copy-start.6

commit v3 on v2

v3 whole, which is shorter than its diff:
```python
import functools
import math

import jax
import jax.numpy as jnp
import numpy as np
from jax import lax
from jax.experimental import pallas as pl
from jax.experimental.pallas import tpu as pltpu
from jax.sharding import PartitionSpec as P

HEAD_DIM = 128
TOKENS = 128
HEADS_HERE = 16
BLOCKS = 64
PIECE = 32

norm_eps = 1e-06
masked_score = -1e30
exponent_scale = HEAD_DIM ** (-0.5) * math.log2(math.e)
X_STEP = 16
X_CHIPS, Z_CHIPS = 4, 8
HALF = HEADS_HERE // 2
QUARTER, X, Z, CORE = range(4)
QUERY_TILE = 16


def place_of(device):
    x, z, core = device // 16, device // 2 % 8, device % 2
    return 2 * z + x // 2, 2 * (x % 2) + core


def columns(head):
    return slice(head * HEAD_DIM, (head + 1) * HEAD_DIM)


def rows(quarter):
    return slice(quarter * PIECE, (quarter + 1) * PIECE)


def whole(space=pltpu.VMEM):
    return pl.BlockSpec(memory_space=space)


def dot(left, right, left_dim, right_dim, precision=None):
    return lax.dot_general(
        left,
        right,
        (((left_dim,), (right_dim,)), ((), ())),
        precision=precision,
        preferred_element_type=jnp.float32,
    )


def call(kernel, out_shape, operands, flops, spaces=None, out_space=pltpu.VMEM, scratch=(), limit=16):
    moved = [*operands, *jax.tree.leaves(out_shape)]
    spaces = spaces or [pltpu.VMEM] * len(operands)
    operands = [
        pltpu.with_memory_space_constraint(o, space) if space is pltpu.HBM else o
        for o, space in zip(operands, spaces)
    ]
    if out_space is pltpu.HBM:
        out_shape = jax.tree.map(lambda o: pltpu.HBM(o.shape, o.dtype), out_shape)
    return pl.pallas_call(
        kernel,
        out_shape=out_shape,
        in_specs=[whole(space) for space in spaces],
        out_specs=jax.tree.map(lambda _: whole(out_space), out_shape),
        scratch_shapes=list(scratch),
        compiler_params=pltpu.CompilerParams(vmem_limit_bytes=limit << 20),
        cost_estimate=pl.CostEstimate(
            flops=flops,
            bytes_accessed=sum(math.prod(o.shape) * o.dtype.itemsize for o in moved),
            transcendentals=0,
        ),
    )(*operands)


def pack_kernel(query_ref, key_ref, value_ref, out_ref, held_ref, semaphores):
    sources = (query_ref, key_ref, value_ref)
    copies = [
        pltpu.make_async_copy(source, held_ref.at[which], semaphores.at[which])
        for which, source in enumerate(sources)
    ]
    for copy in copies:
        copy.start()
    for which, copy in enumerate(copies):
        copy.wait()
        for device in range(BLOCKS):
            head, quarter = place_of(device)
            out_ref[device, rows(which), :] = held_ref[which, rows(quarter), columns(head)]


def lower_triangle():
    shape = (TOKENS, TOKENS)
    return lax.broadcasted_iota(jnp.int32, shape, 0) >= lax.broadcasted_iota(jnp.int32, shape, 1)


def running_sums(decay):
    ones = jnp.where(lower_triangle(), 1.0, 0.0).astype(jnp.float32)
    return dot(ones, decay, 1, 0, lax.Precision.HIGHEST)


def split_parts(value):
    coarse = value.astype(jnp.bfloat16).astype(jnp.float32)
    middle = (value - coarse).astype(jnp.bfloat16).astype(jnp.float32)
    parts = (coarse, middle, value - coarse - middle)
    return jnp.concatenate([part.astype(jnp.bfloat16) for part in parts], axis=0)


def join_parts(parts, heads):
    wide = parts.astype(jnp.float32)
    return wide[0:heads] + wide[heads : 2 * heads] + wide[2 * heads : 3 * heads]


def head_rows(head):
    return slice(head * HEAD_DIM, (head + 1) * HEAD_DIM)


def states_kernel(key_ref, value_ref, decay_ref, out_ref):
    decay = decay_ref[...]
    running_sum = running_sums(decay)
    ones = jnp.ones((TOKENS, HEAD_DIM), jnp.float32)
    endings = dot(decay, ones, 0, 0, lax.Precision.HIGHEST)
    out_ref[HEADS_HERE * HEAD_DIM :, :] = split_parts(endings)
    for head in range(HEADS_HERE):
        sums = running_sum[:, head : head + 1]
        ending = running_sum[TOKENS - 1 : TOKENS, head : head + 1]
        key_wide = key_ref[:, columns(head)].astype(jnp.float32)
        key_scaled = (key_wide * jnp.exp(ending - sums)).astype(jnp.bfloat16)
        state = dot(key_scaled, value_ref[:, columns(head)], 0, 0)
        out_ref[head_rows(head), :] = state.astype(jnp.bfloat16)


def chip_kernel(place_ref, mine_ref, other_ref, out_ref, ending_ref):
    first = place_ref[CORE] == 0
    tail = slice(HEADS_HERE * HEAD_DIM, None)
    mine = join_parts(mine_ref[tail, :], HEADS_HERE)
    other = join_parts(other_ref[tail, :], HEADS_HERE)
    both = mine + other
    later = jnp.where(first, other, mine)
    ending_ref[...] = jnp.where(first, both[0:HALF], both[HALF:])
    out_ref[HALF * HEAD_DIM :, :] = split_parts(ending_ref[...])
    ending_ref[...] = jnp.where(first, later[0:HALF], later[HALF:])
    for head in range(HALF):
        place = place_ref[CORE] * (HALF * HEAD_DIM) + head * HEAD_DIM
        here = pl.ds(pl.multiple_of(place, HEAD_DIM), HEAD_DIM)
        mine = mine_ref[here, :].astype(jnp.float32)
        other = other_ref[here, :].astype(jnp.float32)
        fade = jnp.exp(ending_ref[head : head + 1, :])
        state = jnp.where(first, fade * mine + other, fade * other + mine)
        out_ref[head_rows(head), :] = state.astype(jnp.bfloat16)


def plane_kernel(place_ref, gathered_ref, plane_ref, before_ref, faded_ref):
    mine = place_ref[Z]
    endings = [join_parts(gathered_ref[z, HALF * HEAD_DIM :, :], HALF) for z in range(Z_CHIPS)]
    faded = jnp.zeros((HALF, HEAD_DIM), jnp.float32)
    for z in range(Z_CHIPS):
        faded += jnp.where(z < mine, endings[z], 0.0)
    faded_ref[...] = faded
    plane_ref[HALF * HEAD_DIM :, :] = split_parts(functools.reduce(jnp.add, endings))
    for head in range(HALF):
        carry = jnp.zeros((HEAD_DIM, HEAD_DIM), jnp.float32)
        before = carry
        for z in range(Z_CHIPS):
            before = jnp.where(z == mine, carry, before)
            fade = jnp.exp(endings[z][head : head + 1, :])
            carry = fade * carry + gathered_ref[z, head_rows(head), :].astype(jnp.float32)
        before_ref[head_rows(head), :] = before
        plane_ref[head_rows(head), :] = carry.astype(jnp.bfloat16)


def prior_kernel(place_ref, planes_ref, before_ref, faded_ref, out_ref):
    mine = place_ref[X]
    endings = [join_parts(planes_ref[x, HALF * HEAD_DIM :, :], HALF) for x in range(X_CHIPS)]
    for head in range(HALF):
        carry = jnp.zeros((HEAD_DIM, HEAD_DIM), jnp.float32)
        before = carry
        for x in range(X_CHIPS):
            before = jnp.where(x == mine, carry, before)
            fade = jnp.exp(endings[x][head : head + 1, :])
            carry = fade * carry + planes_ref[x, head_rows(head), :].astype(jnp.float32)
        fade = jnp.exp(faded_ref[head : head + 1, :])
        prior = fade * before + before_ref[head_rows(head), :]
        out_ref[head_rows(head), :] = prior.astype(jnp.bfloat16)


def attention_kernel(
    which, first, last_tile, has_state, finishes, place_ref, query_ref, *refs
):
    count = QUERY_TILE * PIECE
    tiles = BLOCKS // QUERY_TILE
    number = len(which)
    segments, refs = refs[:number], refs[number:]
    if has_state:
        state_in, refs = refs[:2], refs[2 + 1 :]
    results, (best_all, total_all, score_ref, bias_ref, semaphores) = refs[:-5], refs[-5:]
    held = (best_all, total_all)
    mine = place_ref[QUARTER]
    ones = jnp.ones((count, HEAD_DIM), jnp.bfloat16)
    lanes = count // HEAD_DIM

    def tile(index):
        return pl.ds(pl.multiple_of(index * QUERY_TILE, QUERY_TILE), QUERY_TILE)

    def tile_rows(index):
        return pl.ds(pl.multiple_of(index * count, count), count)

    def copy_in(which_array, index):
        here = (tile_rows(index), slice(None))
        return pltpu.make_async_copy(
            state_in[which_array].at[here],
            held[which_array].at[here],
            semaphores.at[0, which_array, index],
        )

    def copy_out(which_array, index):
        here = (tile_rows(index), slice(None))
        return pltpu.make_async_copy(
            held[which_array].at[here],
            results[which_array].at[here],
            semaphores.at[1, which_array, index],
        )

    if has_state:
        for index in range(tiles):
            copy_in(0, index).start()
            copy_in(1, index).start()

    def positions(shape, dim, quarter):
        row = lax.broadcasted_iota(jnp.int32, shape, dim)
        return (row // PIECE) * TOKENS + row % PIECE + quarter * PIECE

    def widen(value):
        return jnp.concatenate([value] * lanes, axis=1)

    query_places = widen(positions((count, HEAD_DIM), 0, mine))
    for slot, step in enumerate(which):
        allowed = positions((1, count), 1, mine ^ step) <= query_places
        bias_ref[slot] = jnp.where(allowed, 0.0, masked_score)

    def per_tile(query_tile, carry):
        best_ref = best_all.at[tile_rows(query_tile)]
        total_ref = total_all.at[tile_rows(query_tile)]
        query = query_ref[tile(query_tile), rows(0), :].reshape(count, HEAD_DIM)
        if has_state:
            copy_in(0, query_tile).wait()
            copy_in(1, query_tile).wait()
            best_before = best_ref[...]
        else:
            best_ref[...] = jnp.full((count, HEAD_DIM), masked_score, jnp.float32)

        def find_best(key_tile, masked):
            best = best_ref[...]
            for slot, segment in enumerate(segments):
                key = segment[tile(key_tile - first), rows(segment.shape[1] // PIECE - 2), :]
                score = dot(query, key.reshape(count, HEAD_DIM), 1, 1)
                if masked:
                    score += bias_ref[slot]
                score_ref[number * (key_tile - first) + slot] = score
                for lane in range(lanes):
                    best = jnp.maximum(best, score[:, columns(lane)])
            best_ref[...] = best

        def unmasked(key_tile, nothing):
            find_best(key_tile, False)
            return nothing

        lax.fori_loop(first, jnp.minimum(query_tile, last_tile), unmasked, 0)
        if first == 0 and last_tile == tiles:
            find_best(query_tile, True)
        else:

            @pl.when(jnp.logical_and(query_tile >= first, query_tile < last_tile))
            def _():
                find_best(query_tile, True)

        best = jnp.broadcast_to(
            jnp.max(best_ref[...], axis=1, keepdims=True), (count, HEAD_DIM)
        )
        best_ref[...] = best
        if has_state:
            shrink = jnp.exp2((best_before - best) * exponent_scale)
            total_ref[...] *= jnp.concatenate([shrink, shrink], axis=1)
        else:
            total_ref[...] = jnp.zeros((count, 2 * HEAD_DIM), jnp.float32)

        def add_up(key_tile, nothing):
            best_wide = widen(best_ref[...])
            weights, values = [], []
            for slot, segment in enumerate(segments):
                score = score_ref[number * (key_tile - first) + slot]
                weight = jnp.exp2((score - best_wide) * exponent_scale)
                weights.append(weight.astype(jnp.bfloat16))
                value = segment[tile(key_tile - first), rows(segment.shape[1] // PIECE - 1), :]
                values.append(jnp.concatenate([value.reshape(count, HEAD_DIM), ones], axis=1))
            total_ref[...] += dot(
                jnp.concatenate(weights, axis=1), jnp.concatenate(values, axis=0), 1, 0
            )
            return nothing

        lax.fori_loop(first, jnp.minimum(query_tile + 1, last_tile), add_up, 0)
        if finishes:
            outcome = total_ref[:, :HEAD_DIM] / total_ref[:, HEAD_DIM:]
            results[0][tile(query_tile)] = outcome.astype(jnp.bfloat16).reshape(
                QUERY_TILE, PIECE, HEAD_DIM
            )
        else:
            copy_out(0, query_tile).start()
            copy_out(1, query_tile).start()
        return carry

    lax.fori_loop(0, tiles, per_tile, 0)
    if not finishes:
        for index in range(tiles):
            copy_out(0, index).wait()
            copy_out(1, index).wait()


def attend(which, key_tiles, place, queries, segments, state, finishes, token=()):
    shape = jax.ShapeDtypeStruct
    count = QUERY_TILE * PIECE
    tiles = BLOCKS // QUERY_TILE
    first, last_tile = key_tiles
    kernel = functools.partial(
        attention_kernel, which, first, last_tile, state is not None, finishes
    )
    best_shape = (BLOCKS * PIECE, HEAD_DIM)
    total_shape = (BLOCKS * PIECE, 2 * HEAD_DIM)
    if finishes:
        out_shape = shape((BLOCKS, PIECE, HEAD_DIM), jnp.bfloat16)
    else:
        out_shape = (shape(best_shape, jnp.float32), shape(total_shape, jnp.float32))
    spaces = [pltpu.SMEM, *[pltpu.VMEM] * (1 + len(segments))]
    if state is not None:
        spaces += [pltpu.HBM, pltpu.HBM, pltpu.VMEM]
    return call(
        kernel,
        out_shape,
        (place, queries, *segments, *(state or ()), *token),
        10**9 * len(which) * (last_tile - first),
        spaces,
        pltpu.VMEM if finishes else pltpu.HBM,
        (
            pltpu.VMEM(best_shape, jnp.float32),
            pltpu.VMEM(total_shape, jnp.float32),
            pltpu.VMEM((len(which) * (last_tile - first), count, count), jnp.float32),
            pltpu.VMEM((len(which), count, count), jnp.float32),
            pltpu.SemaphoreType.DMA((2, 2, tiles)),
        ),
        limit=24,
    )


def lightning_kernel(
    place_ref, query_ref, key_ref, value_ref, decay_ref, mine_ref, other_ref, sibling_ref, out_ref
):
    second = place_ref[CORE] == 1
    endings = join_parts(sibling_ref[HEADS_HERE * HEAD_DIM :, :], HEADS_HERE)
    decay = decay_ref[...]
    causal = lower_triangle()
    running_sum = running_sums(decay)
    later = jnp.where(causal, 0.0, 1.0).astype(jnp.float32)
    shape = (TOKENS, TOKENS)
    upper = lax.broadcasted_iota(jnp.int32, shape, 0) <= lax.broadcasted_iota(jnp.int32, shape, 1)
    upper = jnp.where(upper, 1.0, 0.0).astype(jnp.float32)
    running_row = dot(decay, upper, 0, 0, lax.Precision.HIGHEST)
    for head in range(HEADS_HERE):
        sums = running_sum[:, head : head + 1]
        spread = sums - running_row[head : head + 1, :]
        query = query_ref[:, columns(head)]
        value = value_ref[:, columns(head)]
        scores = dot(query, key_ref[:, columns(head)], 1, 1)
        decayed = jnp.where(causal, jnp.exp(jnp.where(causal, spread, 0.0)), 0.0) * scores
        total = dot(decayed.astype(jnp.bfloat16), value, 1, 0)
        query_scaled = (query.astype(jnp.float32) * jnp.exp(sums)).astype(jnp.bfloat16)
        half, place = head // HALF, head_rows(head % HALF)
        mine = mine_ref[place, :].astype(jnp.float32)
        other = other_ref[place, :].astype(jnp.float32)
        prior = jnp.where(place_ref[CORE] == half, mine, other)
        fade = jnp.exp(endings[head : head + 1, :])
        passed = fade * prior + sibling_ref[head_rows(head), :].astype(jnp.float32)
        prior = jnp.where(second, passed, prior)
        total += dot(query_scaled, prior.astype(jnp.bfloat16), 1, 0)
        mean = jnp.mean(total * total, axis=1, keepdims=True)
        out_ref[:, columns(head)] = (total * lax.rsqrt(mean + norm_eps)).astype(jnp.bfloat16)


def unpack_kernel(moved_ref, order_ref, out_ref):
    for device in range(BLOCKS):
        head, quarter = place_of(device)
        out_ref[rows(quarter), columns(head)] = moved_ref[device]


def exchange(value):
    return lax.all_to_all(value, "ctx", split_axis=0, concat_axis=0, tiled=True)


def swap(value, step):
    return lax.ppermute(value, "ctx", [(d, d ^ step) for d in range(BLOCKS)])


def gather(value, groups):
    return lax.all_gather(value, "ctx", axis=0, axis_index_groups=groups)


def shards(lin_query, lin_key, lin_value, log_decay, soft_query, soft_key, soft_value):
    half = jnp.bfloat16
    shape = jax.ShapeDtypeStruct
    index = lax.axis_index("ctx").astype(jnp.int32)
    x, z, core = index // X_STEP, index // 2 % Z_CHIPS, index % 2
    place = jnp.stack([2 * (x % 2) + core, x, z, core])
    everyone = np.arange(BLOCKS).reshape(X_CHIPS, Z_CHIPS, 2)
    along_z = everyone.transpose(0, 2, 1).reshape(-1, Z_CHIPS).tolist()
    along_x = everyone.transpose(1, 2, 0).reshape(-1, X_CHIPS).tolist()

    width = HEADS_HERE * HEAD_DIM
    packed = call(
        pack_kernel,
        shape((BLOCKS, 3 * PIECE, HEAD_DIM), half),
        (soft_query, soft_key, soft_value),
        1000,
        [pltpu.HBM] * 3,
        scratch=(pltpu.VMEM((3, TOKENS, width), half), pltpu.SemaphoreType.DMA((3,))),
    )
    kv0 = exchange(packed)
    states = call(
        states_kernel,
        shape((width + 3 * HEADS_HERE, HEAD_DIM), half),
        (lin_key, lin_value, log_decay),
        10**8,
    )
    sibling = swap(states, 1)
    on_core = [pltpu.SMEM] + [pltpu.VMEM] * 8
    part = shape((HALF * HEAD_DIM + 3 * HALF, HEAD_DIM), half)
    chip = call(
        chip_kernel,
        part,
        (place, states, sibling),
        10**7,
        on_core[:3],
        scratch=(pltpu.VMEM((HALF, HEAD_DIM), jnp.float32),),
    )
    kv0, chip = lax.optimization_barrier((kv0, chip))
    early = BLOCKS // 2
    kv2a = swap(kv0[:early, PIECE:], X_STEP)
    kv2b = swap(kv0[early:, PIECE:], X_STEP)
    kv1 = swap(kv0[:, PIECE:], 1)
    chips = gather(chip, along_z)

    tiles = BLOCKS // QUERY_TILE
    state = attend((0, 1), (0, tiles), place, kv0, (kv0, kv1), None, False)
    token, kv2a = lax.optimization_barrier((state[0][0:8, :], kv2a))
    kv3a = swap(kv2a, 1)
    state = attend((2, 3), (0, tiles // 2), place, kv0, (kv2a, kv3a), state, False, (token,))
    token, kv2b, chips = lax.optimization_barrier((state[0][0:8, :], kv2b, chips))
    kv3b = swap(kv2b, 1)
    wide = shape((HALF * HEAD_DIM, HEAD_DIM), jnp.float32)
    plane, before, faded = call(
        plane_kernel,
        (part, wide, shape((HALF, HEAD_DIM), jnp.float32)),
        (place, chips),
        10**7,
        on_core[:2],
    )
    planes = gather(plane, along_x)
    attended = attend((2, 3), (tiles // 2, tiles), place, kv0, (kv2b, kv3b), state, True, (token,))
    returned = exchange(attended)
    prior = call(
        prior_kernel,
        shape((HALF * HEAD_DIM, HEAD_DIM), half),
        (place, planes, before, faded),
        10**7,
        on_core[:4],
    )
    other_prior = swap(prior, 1)
    whole_out = shape((TOKENS, width), half)
    lin_out = call(
        lightning_kernel,
        whole_out,
        (place, lin_query, lin_key, lin_value, log_decay, prior, other_prior, sibling),
        2 * 10**8,
        on_core[:8],
    )
    token, returned = lax.optimization_barrier((lin_out[0:8, 0:HEAD_DIM], returned))
    soft_out = call(unpack_kernel, whole_out, (returned, token), 1000)
    return (lin_out, soft_out)


def solution(mesh):
    spec = P("ctx", "head")
    return jax.shard_map(
        shards, mesh=mesh, in_specs=(spec,) * 7, out_specs=(spec, spec), check_vma=False
    )
```

time: 154 us -> 151 us (0.981)
  between operations: 0.76 us -> 14.2 us
  starting transfers between devices: 39.7 us -> 29.8 us
  waiting for transfers between devices: 68.3 us -> 59.2 us
  Pallas kernels: 32.7 us -> 40.4 us
  local copies, waits for them, and re-layouts: 11.3 us -> 7.04 us
    all_gather x0 -> x2, waiting for transfers between devices: none -> 18.6 us  [gather(): return lax.all_gather(value, 'ctx', axis=0, axis_index_groups=groups)]
    all_to_all x4 -> x2, starting transfers between devices: 37.2 us -> 20.6 us  [exchange(): return lax.all_to_all(value, 'ctx', split_axis=0, concat_axis=0, tiled=True)]
    all_to_all x4 -> x2, waiting for transfers between devices: 51.5 us -> 35 us  [exchange(): return lax.all_to_all(value, 'ctx', split_axis=0, concat_axis=0, tiled=True)]
    ppermute x3 -> x7, waiting for transfers between devices: 16.7 us -> 5.55 us  [swap(): return lax.ppermute(value, 'ctx', [(d, d ^ step) for d in range(BLOCKS)])]
    pallas_call x7 -> x10, Pallas kernels: 32.7 us -> 40.4 us  [call(): pl.pallas_call(kernel, out_shape=out_shape, in_specs=[whole(space) for sp...]
    ppermute x3 -> x7, starting transfers between devices: 2.48 us -> 9.09 us  [swap(): return lax.ppermute(value, 'ctx', [(d, d ^ step) for d in range(BLOCKS)])]
    unnamed x25 -> x19, local copies, waits for them, and re-layouts: 10.2 us -> 4.8 us
  transfers between devices with their start and end apart: 7 -> 11, of which waited for: 4 -> 8; matrix products, arithmetic and copies ran while one was open for 0% -> 2% of each run, Pallas kernels for 20% -> 24%
where the time goes in v3:
time: 151 us
  waiting for transfers between devices  59.2 us (39%)
  Pallas kernels  40.4 us (27%)
  starting transfers between devices  29.8 us (20%)
  between operations  14.2 us (9%)
  local copies, waits for them, and re-layouts  7.04 us (5%)
    pallas_call x10, Pallas kernels, call(): pl.pallas_call(kernel, out_shape=out_shape, in_specs=[whole(space) for sp...  40.4 us
    all_to_all x2, waiting for transfers between devices, exchange(): return lax.all_to_all(value, 'ctx', split_axis=0, concat_axis=0, tiled=True)  35 us
    all_to_all x2, starting transfers between devices, exchange(): return lax.all_to_all(value, 'ctx', split_axis=0, concat_axis=0, tiled=True)  20.6 us
    all_gather x2, waiting for transfers between devices, gather(): return lax.all_gather(value, 'ctx', axis=0, axis_index_groups=groups)  18.6 us
    ppermute x7, starting transfers between devices, swap(): return lax.ppermute(value, 'ctx', [(d, d ^ step) for d in range(BLOCKS)])  9.09 us
    ppermute x7, waiting for transfers between devices, swap(): return lax.ppermute(value, 'ctx', [(d, d ^ step) for d in range(BLOCKS)])  5.55 us
    unnamed x19, local copies, waits for them, and re-layouts  4.8 us
  transfers between devices with their start and end apart: 11, of which 8 were waited for; matrix products, arithmetic and copies ran while one was open for 2% of the time, Pallas kernels for 24%

profile of v3, /device:TPU:1, one launch (start us, length us, event | category | flops | bytes accessed | tf_op | source)
XLA Modules:
  0.0 150.7 jit_solution(14099563321545428395)
XLA Ops:
  7.2 2.7 %shard_map.86 = bf16[64,96,128]{2,1,0:T(8,128)(2,1)} custom-call(bf16[128,2048]{1,0:T(8,128)(2,1)} %query_ref.2, bf16[128,2048]{1,0:T(8,128)(2,1)} %key_ref.3, bf16[128,2048]{1,0:T(8,128)(2,1)} %value_ref.3), custom_call_target="tpu_custom_call" | custom-call | flops 1000 | bytes 3145728 | tf_op jit(solution)/shard_map/pallas_call | solution.py:64
  9.8 0.0 copy-start.8
  9.8 0.0 copy-start.1
  9.9 0.0 copy-start.2
  9.9 13.1 %all-to-all-start = ((bf16[64,96,128]{2,1,0:T(8,128)(2,1)}), bf16[64,96,128]{2,1,0:T(8,128)(2,1)S(1)}, u32[]{:S(2)}, u32[]{:S(2)}) async-start(bf16[64,96,128]{2,1,0:T(8,128)(2,1)} %shard_map.86), calls=%async_computation | async-start | bytes 3145728 | tf_op jit(solution)/shard_map/all_to_all | solution.py:397
  23.0 0.0 all-gather.5.cloned.1.call-start
  23.1 0.0 copy-done.8
  23.1 0.1 copy.10.decay_ref
  23.2 0.0 copy-done.1
  23.2 0.0 copy-done.2
  23.2 1.0 shard_map.87.mine_ref
  24.2 0.5 collective-permute-start
  24.8 0.1 pad_add_fusion.place_ref
  24.8 1.5 collective-permute-done.other_ref.sibling_ref
  26.3 1.4 shard_map.88
  27.8 35.0 %all-to-all-done.query_ref.refs_0_ = bf16[64,96,128]{2,1,0:T(8,128)(2,1)S(1)} async-done(((bf16[64,96,128]{2,1,0:T(8,128)(2,1)}), bf16[64,96,128]{2,1,0:T(8,128)(2,1)S(1)}, u32[]{:S(2)}, u32[]{:S(2)}) %all-to-all-start) | async-done | bytes 1572896 | tf_op jit(solution)/shard_map/all_to_all | solution.py:397
  62.8 0.0 all-gather.5.cloned.1.call-update
  62.8 0.0 all-gather.7.cloned.1.call-start
  62.9 0.1 slice.18
  63.0 0.2 collective-permute-start.1
  63.3 0.1 fusion
  63.3 1.2 collective-permute-start.2
  64.5 1.3 collective-permute-done.1.refs_1_
  65.8 11.2 %shard_map.89 = (f32[2048,128]{1,0:T(8,128)}, f32[2048,256]{1,0:T(8,128)}) custom-call(s32[4]{0:T(128)S(1)} %pad_add_fusion.place_ref, bf16[64,96,128]{2,1,0:T(8,128)(2,1)S(1)} %all-to-all-done.query_ref.refs_0_, bf16[64,96,128]{2,1,0:T(8,128)(2,1)S(1)} %all-to-all-done.query_ref.refs_0_, bf16[64,64,128]{2,1,0:T(8,128)(2,1)S(1)} %collective-permute-done.1.refs_1_), custom_call_target="tpu_custom_call" | custom-call | flops 8000000000 | bytes 7340048 | tf_op jit(solution)/shard_map/pallas_call | solution.py:64
  76.9 0.7 slice.19.refs_4_
  77.6 0.0 collective-permute-done.2.refs_0_
  77.6 0.2 collective-permute-start.3
  77.8 1.2 collective-permute-start.4
  79.0 0.6 collective-permute-done.3.refs_1_
  79.5 9.7 %shard_map.90 = (f32[2048,128]{1,0:T(8,128)}, f32[2048,256]{1,0:T(8,128)}) custom-call(s32[4]{0:T(128)S(1)} %pad_add_fusion.place_ref, bf16[64,96,128]{2,1,0:T(8,128)(2,1)S(1)} %all-to-all-done.query_ref.refs_0_, bf16[32,64,128]{2,1,0:T(8,128)(2,1)S(1)} %collective-permute-done.2.refs_0_, bf16[32,64,128]{2,1,0:T(8,128)(2,1)S(1)} %collective-permute-done.3.refs_1_, ...), custom_call_target="tpu_custom_call" | custom-call | flops 4000000000 | bytes 8917008 | tf_op jit(solution)/shard_map/pallas_call | solution.py:64
  89.3 0.7 slice.21.refs_4_
  90.0 1.1 collective-permute-done.4.refs_0_
  91.1 6.6 %all-gather.5.cloned.1.call-done = bf16[8384,128]{1,0:T(8,128)(2,1)} async-done(((bf16[1048,128]{1,0:T(8,128)(2,1)}), bf16[8384,128]{1,0:T(8,128)(2,1)}) %all-gather.5.cloned.1.call-update) | async-done | bytes 2146320 | tf_op jit(solution)/shard_map/all_gather | solution.py:405
  97.6 4.5 %collective-permute-start.6 = (bf16[32,64,128]{2,1,0:T(8,128)(2,1)}, bf16[32,64,128]{2,1,0:T(8,128)(2,1)}, u32[]{:S(2)}, u32[]{:S(2)}) collective-permute-start(bf16[32,64,128]{2,1,0:T(8,128)(2,1)} %collective-permute-done.4.refs_0_), channel_id=1, source_target_pairs={{0,4},{4,0},{8,12},{12,8},{16,20},{20,16},{24,28},{28,24},{32,36},... | collective-permute-start | bytes 1572872 | tf_op jit(solution)/shard_map/ppermute | solution.py:401
  102.2 0.0 copy-start
  102.2 1.6 %copy-done = bf16[8384,128]{1,0:T(8,128)(2,1)S(1)} copy-done((bf16[8384,128]{1,0:T(8,128)(2,1)S(1)}, bf16[8384,128]{1,0:T(8,128)(2,1)}, u32[]{:S(2)}) %copy-start) | copy-done | bytes 2146328
  103.8 1.7 %shard_map.91 = (bf16[1048,128]{1,0:T(8,128)(2,1)}, f32[1024,128]{1,0:T(8,128)S(1)}, f32[8,128]{1,0:T(8,128)S(1)}) custom-call(s32[4]{0:T(128)S(1)} %pad_add_fusion.place_ref, bf16[8,1048,128]{2,1,0:T(8,128)(2,1)S(1)} %bitcast.6), custom_call_target="tpu_custom_call" | custom-call | flops 10000000 | bytes 2942992 | tf_op jit(solution)/shard_map/pallas_call | solution.py:64
  105.5 0.0 copy-start.6
  105.5 0.8 copy-done.6
  106.2 0.0 all-gather.7.cloned.1.call-update
  106.3 0.0 collective-permute-done.6.refs_1_
  106.3 6.9 %shard_map.94 = bf16[64,32,128]{2,1,0:T(8,128)(2,1)} custom-call(s32[4]{0:T(128)S(1)} %pad_add_fusion.place_ref, bf16[64,96,128]{2,1,0:T(8,128)(2,1)S(1)} %all-to-all-done.query_ref.refs_0_, bf16[32,64,128]{2,1,0:T(8,128)(2,1)} %collective-permute-done.4.refs_0_, bf16[32,64,128]{2,1,0:T(8,128)(2,1)} %collective-permute-done.6.refs_1_, ...), custom_call_target="tpu_custom_call" | custom-call | flops 4000000000 | bytes 6295568 | tf_op jit(solution)/shard_map/pallas_call | solution.py:64
  113.2 0.0 copy-start.3
  113.2 0.0 copy-start.5
  113.2 7.5 %all-to-all-start.1 = ((bf16[64,32,128]{2,1,0:T(8,128)(2,1)}), bf16[64,32,128]{2,1,0:T(8,128)(2,1)S(1)}, u32[]{:S(2)}, u32[]{:S(2)}) async-start(bf16[64,32,128]{2,1,0:T(8,128)(2,1)} %shard_map.94), calls=%async_computation.1 | async-start | bytes 1048576 | tf_op jit(solution)/shard_map/all_to_all | solution.py:397
  120.7 12.0 %all-gather.7.cloned.1.call-done = bf16[4192,128]{1,0:T(8,128)(2,1)} async-done(((bf16[1048,128]{1,0:T(8,128)(2,1)}), bf16[4192,128]{1,0:T(8,128)(2,1)}) %all-gather.7.cloned.1.call-update) | async-done | bytes 1073168 | tf_op jit(solution)/shard_map/all_gather | solution.py:405
  132.7 0.0 copy-start.4
  132.7 1.2 copy-done.4
  134.0 0.0 copy-start.7
  134.0 1.0 copy-done.7
  135.0 0.8 shard_map.92.mine_ref
  135.8 1.2 collective-permute-start.5
  137.0 1.2 collective-permute-done.5.other_ref
  138.2 0.0 copy-done.3
  138.2 0.0 copy-done.5
  138.2 4.1 %shard_map.93 = bf16[128,2048]{1,0:T(8,128)(2,1)} custom-call(s32[4]{0:T(128)S(1)} %pad_add_fusion.place_ref, bf16[128,2048]{1,0:T(8,128)(2,1)S(1)} %copy-done.5, bf16[128,2048]{1,0:T(8,128)(2,1)S(1)} %copy-done.1, bf16[128,2048]{1,0:T(8,128)(2,1)S(1)} %copy-done.3, f32[128,16]{1,0:T(8,128)S(1)} %copy.10.decay_ref, ...), custom_call_target="tpu_custom_call" | custom-call | flops 200000000 | bytes 3166224 | tf_op jit(solution)/shard_map/pallas_call | solution.py:64
  142.3 0.7 slice.24.order_ref
  143.0 0.0 all-to-all-done.1.moved_ref
  143.0 0.9 shard_map.95
Async XLA Ops:
  9.8 13.2 %copy-start.8 = (f32[128,16]{0,1:T(8,128)S(1)}, f32[128,16]{0,1:T(8,128)}, u32[]{:S(2)}) copy-start(f32[128,16]{0,1:T(8,128)} %param.10) | copy-start | bytes 24580
  9.8 13.3 %copy-start.1 = (bf16[128,2048]{1,0:T(8,128)(2,1)S(1)}, bf16[128,2048]{1,0:T(8,128)(2,1)}, u32[]{:S(2)}) copy-start(bf16[128,2048]{1,0:T(8,128)(2,1)} %key_ref.5) | copy-start | bytes 1572868
  9.9 13.3 %copy-start.2 = (bf16[128,2048]{1,0:T(8,128)(2,1)S(1)}, bf16[128,2048]{1,0:T(8,128)(2,1)}, u32[]{:S(2)}) copy-start(bf16[128,2048]{1,0:T(8,128)(2,1)} %value_ref.5) | copy-start | bytes 1572868
  9.9 52.9 %all-to-all-start = ((bf16[64,96,128]{2,1,0:T(8,128)(2,1)}), bf16[64,96,128]{2,1,0:T(8,128)(2,1)S(1)}, u32[]{:S(2)}, u32[]{:S(2)}) async-start(bf16[64,96,128]{2,1,0:T(8,128)(2,1)} %shard_map.86), calls=%async_computation | async-start | bytes 3145728 | tf_op jit(solution)/shard_map/all_to_all | solution.py:397
  23.0 74.6 %all-gather.5.cloned.1.call-start = ((), (), s32[]{:S(2)}) async-start(), calls=%async_computation.2 | async-start | bytes 2414592 | tf_op jit(solution)/shard_map/all_gather | solution.py:405
  24.2 2.1 %collective-permute-start = (bf16[2096,128]{1,0:T(8,128)(2,1)S(1)}, bf16[2096,128]{1,0:T(8,128)(2,1)S(1)}, u32[]{:S(2)}, u32[]{:S(2)}) collective-permute-start(bf16[2096,128]{1,0:T(8,128)(2,1)S(1)} %shard_map.87.mine_ref), channel_id=1, source_target_pairs={{0,4},{4,0},{8,12},{12,8},{16,20},{20,16},{24,28},{28,24},{32,36},... | collective-permute-start | bytes 1609736 | tf_op jit(solution)/shard_map/ppermute | solution.py:401
  62.8 69.9 %all-gather.7.cloned.1.call-start = ((), (), s32[]{:S(2)}) async-start(), calls=%async_computation.3 | async-start | bytes 1341440 | tf_op jit(solution)/shard_map/all_gather | solution.py:405
  63.0 2.7 %collective-permute-start.1 = (bf16[64,64,128]{2,1,0:T(8,128)(2,1)S(1)}, bf16[64,64,128]{2,1,0:T(8,128)(2,1)S(1)}, u32[]{:S(2)}, u32[]{:S(2)}) collective-permute-start(bf16[64,64,128]{2,1,0:T(8,128)(2,1)S(1)} %slice.18), channel_id=1, source_target_pairs={{0,4},{4,0},{8,12},{12,8},{16,20},{20,16},{24,28},{28,24},{32,36},... | collective-permute-start | bytes 3145736 | tf_op jit(solution)/shard_map/ppermute | solution.py:401
  63.3 14.3 %collective-permute-start.2 = (bf16[32,64,128]{2,1,0:T(8,128)(2,1)S(1)}, bf16[32,64,128]{2,1,0:T(8,128)(2,1)S(1)}, u32[]{:S(2)}, u32[]{:S(2)}) collective-permute-start(bf16[32,64,128]{2,1,0:T(8,128)(2,1)S(1)} %get-tuple-element.35), channel_id=1, source_target_pairs={{0,64},{4,68},{8,72},{12,76},{16,80},{20,84},{24,88},{28,92},{32,9... | collective-permute-start | bytes 1572872 | tf_op jit(solution)/shard_map/ppermute | solution.py:401
  77.6 1.9 %collective-permute-start.3 = (bf16[32,64,128]{2,1,0:T(8,128)(2,1)S(1)}, bf16[32,64,128]{2,1,0:T(8,128)(2,1)S(1)}, u32[]{:S(2)}, u32[]{:S(2)}) collective-permute-start(bf16[32,64,128]{2,1,0:T(8,128)(2,1)S(1)} %collective-permute-done.2.refs_0_), channel_id=1, source_target_pairs={{0,4},{4,0},{8,12},{12,8},{16,20},{20,16},{24,28},{28,24},{32,36},... | collective-permute-start | bytes 1572872 | tf_op jit(solution)/shard_map/ppermute | solution.py:401
  77.8 13.3 %collective-permute-start.4 = (bf16[32,64,128]{2,1,0:T(8,128)(2,1)S(1)}, bf16[32,64,128]{2,1,0:T(8,128)(2,1)}, u32[]{:S(2)}, u32[]{:S(2)}) collective-permute-start(bf16[32,64,128]{2,1,0:T(8,128)(2,1)S(1)} %get-tuple-element.34), channel_id=1, source_target_pairs={{0,64},{4,68},{8,72},{12,76},{16,80},{20,84},{24,88},{28,92},{32,9... | collective-permute-start | bytes 1572872 | tf_op jit(solution)/shard_map/ppermute | solution.py:401
  97.6 8.6 %collective-permute-start.6 = (bf16[32,64,128]{2,1,0:T(8,128)(2,1)}, bf16[32,64,128]{2,1,0:T(8,128)(2,1)}, u32[]{:S(2)}, u32[]{:S(2)}) collective-permute-start(bf16[32,64,128]{2,1,0:T(8,128)(2,1)} %collective-permute-done.4.refs_0_), channel_id=1, source_target_pairs={{0,4},{4,0},{8,12},{12,8},{16,20},{20,16},{24,28},{28,24},{32,36},... | collective-permute-start | bytes 1572872 | tf_op jit(solution)/shard_map/ppermute | solution.py:401
  102.2 1.6 %copy-start = (bf16[8384,128]{1,0:T(8,128)(2,1)S(1)}, bf16[8384,128]{1,0:T(8,128)(2,1)}, u32[]{:S(2)}) copy-start(bf16[8384,128]{1,0:T(8,128)(2,1)} %all-gather.5.cloned.1.call-done) | copy-start | bytes 6438916
  105.5 0.8 copy-start.6
  113.2 25.0 %copy-start.3 = (bf16[128,2048]{1,0:T(8,128)(2,1)S(1)}, bf16[128,2048]{1,0:T(8,128)(2,1)}, u32[]{:S(2)}) copy-start(bf16[128,2048]{1,0:T(8,128)(2,1)} %value_ref.5) | copy-start | bytes 1572868
  113.2 25.0 %copy-start.5 = (bf16[128,2048]{1,0:T(8,128)(2,1)S(1)}, bf16[128,2048]{1,0:T(8,128)(2,1)}, u32[]{:S(2)}) copy-start(bf16[128,2048]{1,0:T(8,128)(2,1)} %query_ref.3) | copy-start | bytes 1572868
  113.2 29.7 %all-to-all-start.1 = ((bf16[64,32,128]{2,1,0:T(8,128)(2,1)}), bf16[64,32,128]{2,1,0:T(8,128)(2,1)S(1)}, u32[]{:S(2)}, u32[]{:S(2)}) async-start(bf16[64,32,128]{2,1,0:T(8,128)(2,1)} %shard_map.94), calls=%async_computation.1 | async-start | bytes 1048576 | tf_op jit(solution)/shard_map/all_to_all | solution.py:397
  132.7 1.2 copy-start.4
  134.0 1.0 copy-start.7
  135.8 2.4 %collective-permute-start.5 = (bf16[1024,128]{1,0:T(8,128)(2,1)S(1)}, bf16[1024,128]{1,0:T(8,128)(2,1)S(1)}, u32[]{:S(2)}, u32[]{:S(2)}) collective-permute-start(bf16[1024,128]{1,0:T(8,128)(2,1)S(1)} %shard_map.92.mine_ref), channel_id=1, source_target_pairs={{0,4},{4,0},{8,12},{12,8},{16,20},{20,16},{24,28},{28,24},{32,36},... | collective-permute-start | bytes 786440 | tf_op jit(solution)/shard_map/ppermute | solution.py:401
Sparse Core Ops, SparseCore 0:
  62.9 34.6 all-gather.4
  106.4 26.2 all-gather.6

commit v4 on v3

v4 whole, which is shorter than its diff:
```python
import functools
import math

import jax
import jax.numpy as jnp
from jax import lax
from jax.experimental import pallas as pl
from jax.experimental.pallas import tpu as pltpu
from jax.sharding import PartitionSpec as P

HEAD_DIM = 128
TOKENS = 128
HEADS_HERE = 16
BLOCKS = 64
PIECE = 32

norm_eps = 1e-06
masked_score = -1e30
exponent_scale = HEAD_DIM ** (-0.5) * math.log2(math.e)
X_STEP = 16
HALF = HEADS_HERE // 2
SLICE = HALF * HEAD_DIM // BLOCKS
QUARTER, CORE = range(2)
QUERY_TILE = 8


def place_of(device):
    x, z, core = device // 16, device // 2 % 8, device % 2
    return 2 * z + x // 2, 2 * (x % 2) + core


def columns(head):
    return slice(head * HEAD_DIM, (head + 1) * HEAD_DIM)


def rows(quarter):
    return slice(quarter * PIECE, (quarter + 1) * PIECE)


def whole(space=pltpu.VMEM):
    return pl.BlockSpec(memory_space=space)


def dot(left, right, left_dim, right_dim, precision=None):
    return lax.dot_general(
        left,
        right,
        (((left_dim,), (right_dim,)), ((), ())),
        precision=precision,
        preferred_element_type=jnp.float32,
    )


def call(kernel, out_shape, operands, flops, spaces=None, out_spaces=None, scratch=(), limit=16):
    out_shape = tuple(out_shape)
    bytes_moved = sum(math.prod(o.shape) * o.dtype.itemsize for o in (*operands, *out_shape))
    spaces = spaces or [pltpu.VMEM] * len(operands)
    out_spaces = out_spaces or [pltpu.VMEM] * len(out_shape)
    operands = [
        pltpu.with_memory_space_constraint(o, space) if space is pltpu.HBM else o
        for o, space in zip(operands, spaces)
    ]
    out_shape = [
        pltpu.HBM(o.shape, o.dtype) if space is pltpu.HBM else o
        for o, space in zip(out_shape, out_spaces)
    ]
    return pl.pallas_call(
        kernel,
        out_shape=out_shape,
        in_specs=[whole(space) for space in spaces],
        out_specs=[whole(space) for space in out_spaces],
        scratch_shapes=list(scratch),
        compiler_params=pltpu.CompilerParams(vmem_limit_bytes=limit << 20),
        cost_estimate=pl.CostEstimate(
            flops=flops, bytes_accessed=bytes_moved, transcendentals=0
        ),
    )(*operands)


def pack_kernel(query_ref, key_ref, value_ref, out_ref, held_ref, semaphores):
    sources = (query_ref, key_ref, value_ref)
    copies = [
        pltpu.make_async_copy(source, held_ref.at[which], semaphores.at[which])
        for which, source in enumerate(sources)
    ]
    for copy in copies:
        copy.start()
    for which, copy in enumerate(copies):
        copy.wait()
        for device in range(BLOCKS):
            head, quarter = place_of(device)
            out_ref[device, rows(which), :] = held_ref[which, rows(quarter), columns(head)]


def lower_triangle():
    shape = (TOKENS, TOKENS)
    return lax.broadcasted_iota(jnp.int32, shape, 0) >= lax.broadcasted_iota(jnp.int32, shape, 1)


def running_sums(decay):
    ones = jnp.where(lower_triangle(), 1.0, 0.0).astype(jnp.float32)
    return dot(ones, decay, 1, 0, lax.Precision.HIGHEST)


def split_parts(value):
    coarse = value.astype(jnp.bfloat16).astype(jnp.float32)
    middle = (value - coarse).astype(jnp.bfloat16).astype(jnp.float32)
    parts = (coarse, middle, value - coarse - middle)
    return jnp.concatenate([part.astype(jnp.bfloat16) for part in parts], axis=0)


def join_parts(parts, heads):
    wide = parts.astype(jnp.float32)
    return wide[0:heads] + wide[heads : 2 * heads] + wide[2 * heads : 3 * heads]


def head_rows(head):
    return slice(head * HEAD_DIM, (head + 1) * HEAD_DIM)


def states_kernel(key_ref, value_ref, decay_ref, out_ref):
    decay = decay_ref[...]
    running_sum = running_sums(decay)
    ones = jnp.ones((TOKENS, HEAD_DIM), jnp.float32)
    endings = dot(decay, ones, 0, 0, lax.Precision.HIGHEST)
    out_ref[HEADS_HERE * HEAD_DIM :, :] = split_parts(endings)
    for head in range(HEADS_HERE):
        sums = running_sum[:, head : head + 1]
        ending = running_sum[TOKENS - 1 : TOKENS, head : head + 1]
        key_wide = key_ref[:, columns(head)].astype(jnp.float32)
        key_scaled = (key_wide * jnp.exp(ending - sums)).astype(jnp.bfloat16)
        state = dot(key_scaled, value_ref[:, columns(head)], 0, 0)
        out_ref[head_rows(head), :] = state.astype(jnp.bfloat16)


def chip_kernel(place_ref, mine_ref, other_ref, out_ref, ending_ref):
    first = place_ref[CORE] == 0
    tail = slice(HEADS_HERE * HEAD_DIM, None)
    mine = join_parts(mine_ref[tail, :], HEADS_HERE)
    other = join_parts(other_ref[tail, :], HEADS_HERE)
    both = mine + other
    later = jnp.where(first, other, mine)
    ending_ref[...] = jnp.where(first, both[0:HALF], both[HALF:])
    part = lax.broadcasted_iota(jnp.int32, (8, HEAD_DIM), 0)
    for head in range(HALF):
        ending = ending_ref[head : head + 1, :]
        coarse = ending.astype(jnp.bfloat16).astype(jnp.float32)
        middle = (ending - coarse).astype(jnp.bfloat16).astype(jnp.float32)
        fine = ending - coarse - middle
        parts = jnp.where(part == 0, coarse, jnp.where(part == 1, middle, fine))
        for piece in range(HALF):
            out_ref[HALF * head + piece, SLICE:, :] = parts.astype(jnp.bfloat16)
    ending_ref[...] = jnp.where(first, later[0:HALF], later[HALF:])
    for head in range(HALF):
        place = place_ref[CORE] * (HALF * HEAD_DIM) + head * HEAD_DIM
        here = pl.ds(pl.multiple_of(place, HEAD_DIM), HEAD_DIM)
        mine = mine_ref[here, :].astype(jnp.float32)
        other = other_ref[here, :].astype(jnp.float32)
        fade = jnp.exp(ending_ref[head : head + 1, :])
        state = jnp.where(first, fade * mine + other, fade * other + mine)
        pieces = state.astype(jnp.bfloat16).reshape(HALF, SLICE, HEAD_DIM)
        out_ref[HALF * head : HALF * (head + 1), 0:SLICE, :] = pieces


def scan_kernel(moved_ref, out_ref):
    def step(chip, carries):
        following = []
        for core, carry in enumerate(carries):
            source = 2 * chip + core
            out_ref[source] = carry.astype(jnp.bfloat16)
            parts = moved_ref[source, SLICE:, :].astype(jnp.float32)
            ending = parts[0:1] + parts[1:2] + parts[2:3]
            state = moved_ref[source, 0:SLICE, :].astype(jnp.float32)
            following.append(jnp.exp(ending) * carry + state)
        return tuple(following)

    zero = jnp.zeros((SLICE, HEAD_DIM), jnp.float32)
    lax.fori_loop(0, BLOCKS // 2, step, (zero, zero), unroll=4)


def attention_kernel(which, keys, queries, finished, has_state, place_ref, query_ref, *refs):
    count = QUERY_TILE * PIECE
    number = len(which)
    segments, refs = refs[:number], refs[number:]
    if has_state:
        state_in, refs = refs[:2], refs[2 + 1 :]
    if finished.stop and finished.start:
        earlier_ref, refs = refs[0], refs[1:]
    best_all, total_all, score_ref, bias_ref, final_ref, semaphores, final_semaphores = refs[-7:]
    results = refs[:-7]
    held = (best_all, total_all)
    carried = range(finished.stop, queries.stop)
    mine = place_ref[QUARTER]
    ones = jnp.ones((count, HEAD_DIM), jnp.bfloat16)
    lanes = count // HEAD_DIM

    def tile(index):
        return slice(index * QUERY_TILE, (index + 1) * QUERY_TILE)

    def tile_rows(index):
        return pl.ds(index * count, count)

    def state_copies(index, inward):
        copies = []
        for array in range(2):
            inside = held[array].at[tile_rows(index - queries.start), :]
            if inward:
                ends = state_in[array].at[tile_rows(index - queries.start), :], inside
            else:
                ends = inside, results[array - 2].at[tile_rows(index - carried.start), :]
            semaphore = semaphores.at[int(inward), array, index]
            copies.append(pltpu.make_async_copy(*ends, semaphore))
        return copies

    if has_state:
        for index in queries:
            for copy in state_copies(index, True):
                copy.start()
    final_copies = []
    if finished.stop and finished.start:
        place = results[0].at[0 : finished.start * QUERY_TILE]
        final_copies.append(pltpu.make_async_copy(earlier_ref, place, final_semaphores.at[0]))
        final_copies[0].start()

    def positions(shape, dim, quarter):
        row = lax.broadcasted_iota(jnp.int32, shape, dim)
        return (row // PIECE) * TOKENS + row % PIECE + quarter * PIECE

    def widen(value):
        return jnp.concatenate([value] * lanes, axis=1)

    query_places = widen(positions((count, HEAD_DIM), 0, mine))
    for slot, step in enumerate(which):
        allowed = positions((1, count), 1, mine ^ step) <= query_places
        bias_ref[slot] = jnp.where(allowed, 0.0, masked_score)

    for query_tile in queries:
        here = query_tile - queries.start
        best_ref = best_all.at[tile_rows(here), :]
        total_ref = total_all.at[tile_rows(here), :]
        query = query_ref[tile(query_tile), rows(0), :].reshape(count, HEAD_DIM)
        if has_state:
            for copy in state_copies(query_tile, True):
                copy.wait()
            best_before = best_ref[...]
        else:
            best_before = jnp.full((count, HEAD_DIM), masked_score, jnp.float32)
        seen = [key_tile for key_tile in keys if key_tile <= query_tile]

        best = best_before
        for key_tile in seen:
            for slot, segment in enumerate(segments):
                part = tile(key_tile - keys.start)
                key = segment[part, rows(segment.shape[1] // PIECE - 2), :]
                score = dot(query, key.reshape(count, HEAD_DIM), 1, 1)
                if key_tile == query_tile:
                    score += bias_ref[slot]
                score_ref[number * (key_tile - keys.start) + slot] = score
                for lane in range(lanes):
                    best = jnp.maximum(best, score[:, columns(lane)])
        best = jnp.broadcast_to(jnp.max(best, axis=1, keepdims=True), best.shape)
        best_ref[...] = best
        if has_state:
            shrink = jnp.exp2((best_before - best) * exponent_scale)
            total_ref[...] *= jnp.concatenate([shrink, shrink], axis=1)
        else:
            total_ref[...] = jnp.zeros((count, 2 * HEAD_DIM), jnp.float32)

        for key_tile in seen:
            best_wide = widen(best_ref[...])
            weights, values = [], []
            for slot, segment in enumerate(segments):
                score = score_ref[number * (key_tile - keys.start) + slot]
                weight = jnp.exp2((score - best_wide) * exponent_scale)
                weights.append(weight.astype(jnp.bfloat16))
                part = tile(key_tile - keys.start)
                value = segment[part, rows(segment.shape[1] // PIECE - 1), :]
                values.append(jnp.concatenate([value.reshape(count, HEAD_DIM), ones], axis=1))
            total_ref[...] += dot(
                jnp.concatenate(weights, axis=1), jnp.concatenate(values, axis=0), 1, 0
            )
        if query_tile in finished:
            outcome = total_ref[:, :HEAD_DIM] / total_ref[:, HEAD_DIM:]
            slot = tile(query_tile - finished.start)
            final_ref[slot] = outcome.astype(jnp.bfloat16).reshape(QUERY_TILE, PIECE, HEAD_DIM)
            copy = pltpu.make_async_copy(
                final_ref.at[slot],
                results[0].at[tile(query_tile)],
                final_semaphores.at[1 + query_tile],
            )
            copy.start()
            final_copies.append(copy)
        else:
            for copy in state_copies(query_tile, False):
                copy.start()
    for query_tile in carried:
        for copy in state_copies(query_tile, False):
            copy.wait()
    for copy in final_copies:
        copy.wait()


def attend(which, keys, queries, finished, place, packed, segments, state=None, token=(), earlier=()):
    shape = jax.ShapeDtypeStruct
    count = QUERY_TILE * PIECE
    kernel = functools.partial(
        attention_kernel, which, keys, queries, finished, state is not None
    )
    out_shape, out_spaces = [], []
    if finished.stop:
        out_shape.append(shape((finished.stop * QUERY_TILE, PIECE, HEAD_DIM), jnp.bfloat16))
        out_spaces.append(pltpu.HBM)
    left = queries.stop - finished.stop
    if left:
        for width in (HEAD_DIM, 2 * HEAD_DIM):
            out_shape.append(shape((left * count, width), jnp.float32))
            out_spaces.append(pltpu.HBM)
    spaces = [pltpu.SMEM, *[pltpu.VMEM] * (1 + len(segments))]
    if state is not None:
        spaces += [pltpu.HBM, pltpu.HBM, pltpu.VMEM]
    spaces += [pltpu.HBM] * len(earlier)
    return call(
        kernel,
        out_shape,
        (place, packed, *segments, *(state or ()), *token, *earlier),
        2 * 10**8 * len(which) * len(keys),
        spaces,
        out_spaces,
        (
            pltpu.VMEM((len(queries) * count, HEAD_DIM), jnp.float32),
            pltpu.VMEM((len(queries) * count, 2 * HEAD_DIM), jnp.float32),
            pltpu.VMEM((len(which) * len(keys), count, count), jnp.float32),
            pltpu.VMEM((len(which), count, count), jnp.float32),
            pltpu.VMEM((max(len(finished), 1) * QUERY_TILE, PIECE, HEAD_DIM), jnp.bfloat16),
            pltpu.SemaphoreType.DMA((2, 2, BLOCKS // QUERY_TILE)),
            pltpu.SemaphoreType.DMA((1 + BLOCKS // QUERY_TILE,)),
        ),
        limit=24,
    )


def lightning_kernel(
    place_ref, query_ref, key_ref, value_ref, decay_ref, mine_ref, other_ref, sibling_ref, out_ref
):
    second = place_ref[CORE] == 1
    endings = join_parts(sibling_ref[HEADS_HERE * HEAD_DIM :, :], HEADS_HERE)
    decay = decay_ref[...]
    causal = lower_triangle()
    running_sum = running_sums(decay)
    later = jnp.where(causal, 0.0, 1.0).astype(jnp.float32)
    shape = (TOKENS, TOKENS)
    upper = lax.broadcasted_iota(jnp.int32, shape, 0) <= lax.broadcasted_iota(jnp.int32, shape, 1)
    upper = jnp.where(upper, 1.0, 0.0).astype(jnp.float32)
    running_row = dot(decay, upper, 0, 0, lax.Precision.HIGHEST)
    for head in range(HEADS_HERE):
        sums = running_sum[:, head : head + 1]
        spread = sums - running_row[head : head + 1, :]
        query = query_ref[:, columns(head)]
        value = value_ref[:, columns(head)]
        scores = dot(query, key_ref[:, columns(head)], 1, 1)
        decayed = jnp.where(causal, jnp.exp(jnp.where(causal, spread, 0.0)), 0.0) * scores
        total = dot(decayed.astype(jnp.bfloat16), value, 1, 0)
        query_scaled = (query.astype(jnp.float32) * jnp.exp(sums)).astype(jnp.bfloat16)
        half, place = head // HALF, head_rows(head % HALF)
        mine = mine_ref[place, :].astype(jnp.float32)
        other = other_ref[place, :].astype(jnp.float32)
        prior = jnp.where(place_ref[CORE] == half, mine, other)
        fade = jnp.exp(endings[head : head + 1, :])
        passed = fade * prior + sibling_ref[head_rows(head), :].astype(jnp.float32)
        prior = jnp.where(second, passed, prior)
        total += dot(query_scaled, prior.astype(jnp.bfloat16), 1, 0)
        mean = jnp.mean(total * total, axis=1, keepdims=True)
        out_ref[:, columns(head)] = (total * lax.rsqrt(mean + norm_eps)).astype(jnp.bfloat16)


def unpack_kernel(moved_ref, order_ref, out_ref):
    for device in range(BLOCKS):
        head, quarter = place_of(device)
        out_ref[rows(quarter), columns(head)] = moved_ref[device]


def exchange(value):
    return lax.all_to_all(value, "ctx", split_axis=0, concat_axis=0, tiled=True)


def swap(value, step):
    return lax.ppermute(value, "ctx", [(d, d ^ step) for d in range(BLOCKS)])


def shards(lin_query, lin_key, lin_value, log_decay, soft_query, soft_key, soft_value):
    half = jnp.bfloat16
    shape = jax.ShapeDtypeStruct
    index = lax.axis_index("ctx").astype(jnp.int32)
    core = index % 2
    place = jnp.stack([2 * (index // X_STEP % 2) + core, core])
    width = HEADS_HERE * HEAD_DIM
    (packed,) = call(
        pack_kernel,
        [shape((BLOCKS, 3 * PIECE, HEAD_DIM), half)],
        (soft_query, soft_key, soft_value),
        1000,
        [pltpu.HBM] * 3,
        scratch=(pltpu.VMEM((3, TOKENS, width), half), pltpu.SemaphoreType.DMA((3,))),
    )
    kv0 = exchange(packed)
    (states,) = call(
        states_kernel,
        [shape((width + 3 * HEADS_HERE, HEAD_DIM), half)],
        (lin_key, lin_value, log_decay),
        10**8,
    )
    sibling = swap(states, 1)
    on_core = [pltpu.SMEM] + [pltpu.VMEM] * 7
    (chip,) = call(
        chip_kernel,
        [shape((BLOCKS, SLICE + 8, HEAD_DIM), half)],
        (place, states, sibling),
        10**7,
        on_core[:3],
        scratch=(pltpu.VMEM((HALF, HEAD_DIM), jnp.float32),),
    )
    kv0, chip = lax.optimization_barrier((kv0, chip))
    early = BLOCKS // 2
    kv2a = swap(kv0[:early, PIECE:], X_STEP)
    kv1 = swap(kv0[:, PIECE:], 1)
    chips = exchange(chip)

    tiles = BLOCKS // QUERY_TILE
    every, low, high = range(tiles), range(tiles // 2), range(tiles // 2, tiles)
    state = attend((0, 1), every, every, range(0), place, kv0, (kv0, kv1))
    token, kv2a, kv0b = lax.optimization_barrier((state[0][0:8, :], kv2a, kv0[early:, PIECE:]))
    kv3a = swap(kv2a, 1)
    kv2b = swap(kv0b, X_STEP)
    first, *state = attend(
        (2, 3), low, every, low, place, kv0, (kv2a, kv3a), state, (token,)
    )
    token, chips = lax.optimization_barrier((state[0][0:8, :], chips))
    (scanned,) = call(scan_kernel, [shape((BLOCKS, SLICE, HEAD_DIM), half)], (chips,), 10**6)
    token, kv2b = lax.optimization_barrier((token, kv2b))
    kv3b = swap(kv2b, 1)
    prior = exchange(scanned).reshape(HALF * HEAD_DIM, HEAD_DIM)
    (attended,) = attend(
        (2, 3), high, high, high, place, kv0, (kv2b, kv3b), state, (token,), (first,)
    )
    returned = exchange(attended)
    other_prior = swap(prior, 1)
    whole_out = shape((TOKENS, width), half)
    (lin_out,) = call(
        lightning_kernel,
        [whole_out],
        (place, lin_query, lin_key, lin_value, log_decay, prior, other_prior, sibling),
        2 * 10**8,
        on_core[:8],
    )
    token, returned = lax.optimization_barrier((lin_out[0:8, 0:HEAD_DIM], returned))
    (soft_out,) = call(unpack_kernel, [whole_out], (returned, token), 1000)
    return (lin_out, soft_out)


def solution(mesh):
    spec = P("ctx", "head")
    return jax.shard_map(
        shards, mesh=mesh, in_specs=(spec,) * 7, out_specs=(spec, spec), check_vma=False
    )
```

time: 151 us -> 143 us (0.947)
  between operations: 14.2 us -> 0.78 us
  starting transfers between devices: 29.8 us -> 42.6 us
  waiting for transfers between devices: 59.2 us -> 49 us
  Pallas kernels: 40.4 us -> 44.1 us
  local copies, waits for them, and re-layouts: 7.04 us -> 5.49 us
    all_gather x2 -> x0, waiting for transfers between devices: 18.6 us -> none  [gather(): return lax.all_gather(value, 'ctx', axis=0, axis_index_groups=groups)]
    all_to_all x2 -> x4, starting transfers between devices: 20.6 us -> 37.7 us  [exchange(): return lax.all_to_all(value, 'ctx', split_axis=0, concat_axis=0, tiled=True)]
    all_to_all x2 -> x4, waiting for transfers between devices: 35 us -> 46.1 us  [exchange(): return lax.all_to_all(value, 'ctx', split_axis=0, concat_axis=0, tiled=True)]
    ppermute x7, starting transfers between devices: 9.09 us -> 4.84 us  [swap(): return lax.ppermute(value, 'ctx', [(d, d ^ step) for d in range(BLOCKS)])]
    pallas_call x10 -> x9, Pallas kernels: 40.4 us -> 44.1 us  [call(): pl.pallas_call(kernel, out_shape=out_shape, in_specs=[whole(space) for sp...]
    unnamed x19 -> x11, local copies, waits for them, and re-layouts: 4.8 us -> 1.17 us
    ppermute x7, waiting for transfers between devices: 5.55 us -> 2.87 us  [swap(): return lax.ppermute(value, 'ctx', [(d, d ^ step) for d in range(BLOCKS)])]
  transfers between devices with their start and end apart: 11 -> 11, of which waited for: 8 -> 6; matrix products, arithmetic and copies ran while one was open for 2% -> 2% of each run, Pallas kernels for 24% -> 29%
where the time goes in v4:
time: 143 us; the launch traced here: 142 us
  waiting for transfers between devices  49 us (34%)
  Pallas kernels  44.1 us (31%)
  starting transfers between devices  42.6 us (30%)
  local copies, waits for them, and re-layouts  5.49 us (4%)
    all_to_all x4, waiting for transfers between devices, exchange(): return lax.all_to_all(value, 'ctx', split_axis=0, concat_axis=0, tiled=True)  46.1 us
    pallas_call x9, Pallas kernels, call(): pl.pallas_call(kernel, out_shape=out_shape, in_specs=[whole(space) for sp...  44.1 us
    all_to_all x4, starting transfers between devices, exchange(): return lax.all_to_all(value, 'ctx', split_axis=0, concat_axis=0, tiled=True)  37.7 us
    ppermute x7, starting transfers between devices, swap(): return lax.ppermute(value, 'ctx', [(d, d ^ step) for d in range(BLOCKS)])  4.84 us
    ppermute x7, waiting for transfers between devices, swap(): return lax.ppermute(value, 'ctx', [(d, d ^ step) for d in range(BLOCKS)])  2.87 us
  transfers between devices with their start and end apart: 11, of which 6 were waited for; matrix products, arithmetic and copies ran while one was open for 2% of the time, Pallas kernels for 29%

profile of v4, /device:TPU:1, one launch (start us, length us, event | category | flops | bytes accessed | tf_op | source)
XLA Modules:
  0.0 142.1 jit_solution(14300436490122896500)
XLA Ops:
  0.6 2.6 %shard_map.86 = bf16[64,96,128]{2,1,0:T(8,128)(2,1)} custom-call(bf16[128,2048]{1,0:T(8,128)(2,1)} %query_ref.2, bf16[128,2048]{1,0:T(8,128)(2,1)} %key_ref.3, bf16[128,2048]{1,0:T(8,128)(2,1)} %value_ref.3), custom_call_target="tpu_custom_call" | custom-call | flops 1000 | bytes 3145728 | tf_op jit(solution)/shard_map/pallas_call | solution.py:67
  3.3 0.0 copy-start.4
  3.3 0.0 copy-start
  3.3 0.0 copy-start.1
  3.3 13.1 %all-to-all-start = ((bf16[64,96,128]{2,1,0:T(8,128)(2,1)}), bf16[64,96,128]{2,1,0:T(8,128)(2,1)S(1)}, u32[]{:S(2)}, u32[]{:S(2)}) async-start(bf16[64,96,128]{2,1,0:T(8,128)(2,1)} %shard_map.86), calls=%async_computation | async-start | bytes 3145728 | tf_op jit(solution)/shard_map/all_to_all | solution.py:383
  16.4 0.0 copy-done.4
  16.5 0.1 copy.10.decay_ref
  16.6 0.0 copy-done
  16.6 0.0 copy-done.1
  16.6 1.0 shard_map.87.mine_ref
  17.6 0.5 collective-permute-start
  18.2 0.1 pad_add_fusion.place_ref
  18.2 1.5 %collective-permute-done.other_ref.sibling_ref = bf16[2096,128]{1,0:T(8,128)(2,1)S(1)} collective-permute-done((bf16[2096,128]{1,0:T(8,128)(2,1)S(1)}, bf16[2096,128]{1,0:T(8,128)(2,1)S(1)}, u32[]{:S(2)}, u32[]{:S(2)}) %collective-permute-start) | collective-permute-done | bytes 536608 | tf_op jit(solution)/shard_map/ppermute | solution.py:387
  19.7 1.5 %shard_map.88 = bf16[64,24,128]{2,1,0:T(8,128)(2,1)} custom-call(s32[2]{0:T(128)S(1)} %pad_add_fusion.place_ref, bf16[2096,128]{1,0:T(8,128)(2,1)S(1)} %shard_map.87.mine_ref, bf16[2096,128]{1,0:T(8,128)(2,1)S(1)} %collective-permute-done.other_ref.sibling_ref), custom_call_target="tpu_custom_call" | custom-call | flops 10000000 | bytes 1466376 | tf_op jit(solution)/shard_map/pallas_call | solution.py:67
  21.2 35.0 %all-to-all-done.query_ref.refs_0_ = bf16[64,96,128]{2,1,0:T(8,128)(2,1)S(1)} async-done(((bf16[64,96,128]{2,1,0:T(8,128)(2,1)}), bf16[64,96,128]{2,1,0:T(8,128)(2,1)S(1)}, u32[]{:S(2)}, u32[]{:S(2)}) %all-to-all-start) | async-done | bytes 1572896 | tf_op jit(solution)/shard_map/all_to_all | solution.py:383
  56.2 1.2 slice.18
  57.4 0.2 collective-permute-start.1
  57.6 1.1 fusion
  58.7 1.1 collective-permute-start.2
  59.7 5.7 %all-to-all-start.1 = ((bf16[64,24,128]{2,1,0:T(8,128)(2,1)}), bf16[64,24,128]{2,1,0:T(8,128)(2,1)S(1)}, u32[]{:S(2)}, u32[]{:S(2)}) async-start(bf16[64,24,128]{2,1,0:T(8,128)(2,1)} %shard_map.88), calls=%async_computation.1 | async-start | bytes 786432 | tf_op jit(solution)/shard_map/all_to_all | solution.py:383
  65.4 0.0 collective-permute-done.1.refs_1_
  65.4 9.8 %shard_map.89 = (f32[2048,128]{1,0:T(8,128)}, f32[2048,256]{1,0:T(8,128)}) custom-call(s32[2]{0:T(128)S(1)} %pad_add_fusion.place_ref, bf16[64,96,128]{2,1,0:T(8,128)(2,1)S(1)} %all-to-all-done.query_ref.refs_0_, bf16[64,96,128]{2,1,0:T(8,128)(2,1)S(1)} %all-to-all-done.query_ref.refs_0_, bf16[64,64,128]{2,1,0:T(8,128)(2,1)} %collective-permute-done.1.refs_1_), custom_call_target="tpu_custom_call" | custom-call | flops 3200000000 | bytes 7340040 | tf_op jit(solution)/shard_map/pallas_call | solution.py:67
  75.2 0.7 slice.19.refs_4_
  75.9 0.0 collective-permute-done.2.refs_0_
  75.9 0.6 collective-permute-start.3
  76.6 1.5 %collective-permute-start.5 = (bf16[32,64,128]{2,1,0:T(8,128)(2,1)}, bf16[32,64,128]{2,1,0:T(8,128)(2,1)}, u32[]{:S(2)}, u32[]{:S(2)}) collective-permute-start(bf16[32,64,128]{2,1,0:T(8,128)(2,1)} %get-tuple-element.27), channel_id=1, source_target_pairs={{0,64},{4,68},{8,72},{12,76},{16,80},{20,84},{24,88},{28,92},{32,9... | collective-permute-start | bytes 1572872 | tf_op jit(solution)/shard_map/ppermute | solution.py:387
  78.1 0.2 collective-permute-done.3.refs_1_
  78.3 12.6 %shard_map.90 = (bf16[32,32,128]{2,1,0:T(8,128)(2,1)}, f32[1024,128]{1,0:T(8,128)}, f32[1024,256]{1,0:T(8,128)}) custom-call(s32[2]{0:T(128)S(1)} %pad_add_fusion.place_ref, bf16[64,96,128]{2,1,0:T(8,128)(2,1)S(1)} %all-to-all-done.query_ref.refs_0_, bf16[32,64,128]{2,1,0:T(8,128)(2,1)} %collective-permute-done.2.refs_0_, ...), custom_call_target="tpu_custom_call" | custom-call | flops 1600000000 | bytes 7606280 | tf_op jit(solution)/shard_map/pallas_call | solution.py:67
  90.9 0.7 slice.22.refs_4_
  91.6 0.0 all-to-all-done.1.moved_ref
  91.6 0.0 collective-permute-done.5.refs_0_
  91.6 0.4 collective-permute-start.6
  92.0 0.9 shard_map.91
  92.9 9.9 %all-to-all-start.2 = ((bf16[64,16,128]{2,1,0:T(8,128)(2,1)}), bf16[64,16,128]{2,1,0:T(8,128)(2,1)S(1)}, u32[]{:S(2)}, u32[]{:S(2)}) async-start(bf16[64,16,128]{2,1,0:T(8,128)(2,1)} %shard_map.91), calls=%async_computation.2 | async-start | bytes 524288 | tf_op jit(solution)/shard_map/all_to_all | solution.py:383
  102.8 0.0 collective-permute-done.6.refs_1_
  102.8 0.0 copy-start.2
  102.8 10.7 %shard_map.93 = bf16[64,32,128]{2,1,0:T(8,128)(2,1)} custom-call(s32[2]{0:T(128)S(1)} %pad_add_fusion.place_ref, bf16[64,96,128]{2,1,0:T(8,128)(2,1)S(1)} %all-to-all-done.query_ref.refs_0_, bf16[32,64,128]{2,1,0:T(8,128)(2,1)} %collective-permute-done.5.refs_0_, bf16[32,64,128]{2,1,0:T(8,128)(2,1)} %collective-permute-done.6.refs_1_, ...), custom_call_target="tpu_custom_call" | custom-call | flops 1600000000 | bytes 4984840 | tf_op jit(solution)/shard_map/pallas_call | solution.py:67
  113.5 1.3 all-to-all-done.2
  114.8 9.1 %all-to-all-start.3 = ((bf16[64,32,128]{2,1,0:T(8,128)(2,1)}), bf16[64,32,128]{2,1,0:T(8,128)(2,1)S(1)}, u32[]{:S(2)}, u32[]{:S(2)}) async-start(bf16[64,32,128]{2,1,0:T(8,128)(2,1)} %shard_map.93), calls=%async_computation.3 | async-start | bytes 1048576 | tf_op jit(solution)/shard_map/all_to_all | solution.py:383
  123.8 0.5 collective-permute-start.4
  124.4 1.2 collective-permute-done.4.other_ref
  125.5 0.0 copy-done.2
  125.5 0.0 copy-start.3
  125.6 1.0 copy-done.3
  126.6 4.1 %shard_map.92 = bf16[128,2048]{1,0:T(8,128)(2,1)} custom-call(s32[2]{0:T(128)S(1)} %pad_add_fusion.place_ref, bf16[128,2048]{1,0:T(8,128)(2,1)S(1)} %copy-done.3, bf16[128,2048]{1,0:T(8,128)(2,1)S(1)} %copy-done, bf16[128,2048]{1,0:T(8,128)(2,1)S(1)} %copy-done.2, f32[128,16]{1,0:T(8,128)S(1)} %copy.10.decay_ref, bf16[1024,128]{1,0:T(8,128)(2,1)S(1)} %bitcast.4, ...), custom_call_target="tpu_custom_call" | custom-call | flops 200000000 | bytes 3166216 | tf_op jit(solution)/shard_map/pallas_call | solution.py:67
  130.7 0.7 slice.24.order_ref
  131.3 9.8 %all-to-all-done.3.moved_ref = bf16[64,32,128]{2,1,0:T(8,128)(2,1)S(1)} async-done(((bf16[64,32,128]{2,1,0:T(8,128)(2,1)}), bf16[64,32,128]{2,1,0:T(8,128)(2,1)S(1)}, u32[]{:S(2)}, u32[]{:S(2)}) %all-to-all-start.3) | async-done | bytes 524320 | tf_op jit(solution)/shard_map/all_to_all | solution.py:383
  141.2 0.9 shard_map.94
Async XLA Ops:
  3.3 13.2 %copy-start.4 = (f32[128,16]{0,1:T(8,128)S(1)}, f32[128,16]{0,1:T(8,128)}, u32[]{:S(2)}) copy-start(f32[128,16]{0,1:T(8,128)} %param.10) | copy-start | bytes 24580
  3.3 13.3 %copy-start = (bf16[128,2048]{1,0:T(8,128)(2,1)S(1)}, bf16[128,2048]{1,0:T(8,128)(2,1)}, u32[]{:S(2)}) copy-start(bf16[128,2048]{1,0:T(8,128)(2,1)} %key_ref.5) | copy-start | bytes 1572868
  3.3 13.3 %copy-start.1 = (bf16[128,2048]{1,0:T(8,128)(2,1)S(1)}, bf16[128,2048]{1,0:T(8,128)(2,1)}, u32[]{:S(2)}) copy-start(bf16[128,2048]{1,0:T(8,128)(2,1)} %value_ref.5) | copy-start | bytes 1572868
  3.3 52.9 %all-to-all-start = ((bf16[64,96,128]{2,1,0:T(8,128)(2,1)}), bf16[64,96,128]{2,1,0:T(8,128)(2,1)S(1)}, u32[]{:S(2)}, u32[]{:S(2)}) async-start(bf16[64,96,128]{2,1,0:T(8,128)(2,1)} %shard_map.86), calls=%async_computation | async-start | bytes 3145728 | tf_op jit(solution)/shard_map/all_to_all | solution.py:383
  17.6 2.1 %collective-permute-start = (bf16[2096,128]{1,0:T(8,128)(2,1)S(1)}, bf16[2096,128]{1,0:T(8,128)(2,1)S(1)}, u32[]{:S(2)}, u32[]{:S(2)}) collective-permute-start(bf16[2096,128]{1,0:T(8,128)(2,1)S(1)} %shard_map.87.mine_ref), channel_id=1, source_target_pairs={{0,4},{4,0},{8,12},{12,8},{16,20},{20,16},{24,28},{28,24},{32,36},... | collective-permute-start | bytes 1609736 | tf_op jit(solution)/shard_map/ppermute | solution.py:387
  57.4 8.0 %collective-permute-start.1 = (bf16[64,64,128]{2,1,0:T(8,128)(2,1)}, bf16[64,64,128]{2,1,0:T(8,128)(2,1)}, u32[]{:S(2)}, u32[]{:S(2)}) collective-permute-start(bf16[64,64,128]{2,1,0:T(8,128)(2,1)} %slice.18), channel_id=1, source_target_pairs={{0,4},{4,0},{8,12},{12,8},{16,20},{20,16},{24,28},{28,24},{32,36},... | collective-permute-start | bytes 3145736 | tf_op jit(solution)/shard_map/ppermute | solution.py:387
  58.7 17.3 %collective-permute-start.2 = (bf16[32,64,128]{2,1,0:T(8,128)(2,1)}, bf16[32,64,128]{2,1,0:T(8,128)(2,1)}, u32[]{:S(2)}, u32[]{:S(2)}) collective-permute-start(bf16[32,64,128]{2,1,0:T(8,128)(2,1)} %get-tuple-element.35), channel_id=1, source_target_pairs={{0,64},{4,68},{8,72},{12,76},{16,80},{20,84},{24,88},{28,92},{32,9... | collective-permute-start | bytes 1572872 | tf_op jit(solution)/shard_map/ppermute | solution.py:387
  59.7 31.9 %all-to-all-start.1 = ((bf16[64,24,128]{2,1,0:T(8,128)(2,1)}), bf16[64,24,128]{2,1,0:T(8,128)(2,1)S(1)}, u32[]{:S(2)}, u32[]{:S(2)}) async-start(bf16[64,24,128]{2,1,0:T(8,128)(2,1)} %shard_map.88), calls=%async_computation.1 | async-start | bytes 786432 | tf_op jit(solution)/shard_map/all_to_all | solution.py:383
  75.9 2.4 %collective-permute-start.3 = (bf16[32,64,128]{2,1,0:T(8,128)(2,1)}, bf16[32,64,128]{2,1,0:T(8,128)(2,1)S(1)}, u32[]{:S(2)}, u32[]{:S(2)}) collective-permute-start(bf16[32,64,128]{2,1,0:T(8,128)(2,1)} %collective-permute-done.2.refs_0_), channel_id=1, source_target_pairs={{0,4},{4,0},{8,12},{12,8},{16,20},{20,16},{24,28},{28,24},{32,36},... | collective-permute-start | bytes 1572872 | tf_op jit(solution)/shard_map/ppermute | solution.py:387
  76.6 15.1 %collective-permute-start.5 = (bf16[32,64,128]{2,1,0:T(8,128)(2,1)}, bf16[32,64,128]{2,1,0:T(8,128)(2,1)}, u32[]{:S(2)}, u32[]{:S(2)}) collective-permute-start(bf16[32,64,128]{2,1,0:T(8,128)(2,1)} %get-tuple-element.27), channel_id=1, source_target_pairs={{0,64},{4,68},{8,72},{12,76},{16,80},{20,84},{24,88},{28,92},{32,9... | collective-permute-start | bytes 1572872 | tf_op jit(solution)/shard_map/ppermute | solution.py:387
  91.6 11.1 %collective-permute-start.6 = (bf16[32,64,128]{2,1,0:T(8,128)(2,1)}, bf16[32,64,128]{2,1,0:T(8,128)(2,1)}, u32[]{:S(2)}, u32[]{:S(2)}) collective-permute-start(bf16[32,64,128]{2,1,0:T(8,128)(2,1)} %collective-permute-done.5.refs_0_), channel_id=1, source_target_pairs={{0,4},{4,0},{8,12},{12,8},{16,20},{20,16},{24,28},{28,24},{32,36},... | collective-permute-start | bytes 1572872 | tf_op jit(solution)/shard_map/ppermute | solution.py:387
  92.9 21.9 %all-to-all-start.2 = ((bf16[64,16,128]{2,1,0:T(8,128)(2,1)}), bf16[64,16,128]{2,1,0:T(8,128)(2,1)S(1)}, u32[]{:S(2)}, u32[]{:S(2)}) async-start(bf16[64,16,128]{2,1,0:T(8,128)(2,1)} %shard_map.91), calls=%async_computation.2 | async-start | bytes 524288 | tf_op jit(solution)/shard_map/all_to_all | solution.py:383
  102.8 22.8 %copy-start.2 = (bf16[128,2048]{1,0:T(8,128)(2,1)S(1)}, bf16[128,2048]{1,0:T(8,128)(2,1)}, u32[]{:S(2)}) copy-start(bf16[128,2048]{1,0:T(8,128)(2,1)} %value_ref.5) | copy-start | bytes 1572868
  114.8 26.4 %all-to-all-start.3 = ((bf16[64,32,128]{2,1,0:T(8,128)(2,1)}), bf16[64,32,128]{2,1,0:T(8,128)(2,1)S(1)}, u32[]{:S(2)}, u32[]{:S(2)}) async-start(bf16[64,32,128]{2,1,0:T(8,128)(2,1)} %shard_map.93), calls=%async_computation.3 | async-start | bytes 1048576 | tf_op jit(solution)/shard_map/all_to_all | solution.py:383
  123.8 1.7 %collective-permute-start.4 = (bf16[1024,128]{1,0:T(8,128)(2,1)S(1)}, bf16[1024,128]{1,0:T(8,128)(2,1)S(1)}, u32[]{:S(2)}, u32[]{:S(2)}) collective-permute-start(bf16[1024,128]{1,0:T(8,128)(2,1)S(1)} %bitcast.3), channel_id=1, source_target_pairs={{0,4},{4,0},{8,12},{12,8},{16,20},{20,16},{24,28},{28,24},{32,36},... | collective-permute-start | bytes 786440 | tf_op jit(solution)/shard_map/ppermute | solution.py:387
  125.5 1.0 copy-start.3

commit v5 on v4

--- a/solution.py
+++ b/solution.py
@@ -178,49 +178,40 @@
     lax.fori_loop(0, BLOCKS // 2, step, (zero, zero), unroll=4)
 
 
-def attention_kernel(which, keys, queries, finished, has_state, place_ref, query_ref, *refs):
+def attention_kernel(which, keys, queries, has_state, finishes, place_ref, query_ref, *refs):
     count = QUERY_TILE * PIECE
-    number = len(which)
-    segments, refs = refs[:number], refs[number:]
+    tiles = BLOCKS // QUERY_TILE
+    halves = 2 if keys.stop > tiles // 2 else 1
+    refs = list(refs)
+    segments = [[refs.pop(0) for _ in range(halves)] for step in which if step]
     if has_state:
-        state_in, refs = refs[:2], refs[2 + 1 :]
-    if finished.stop and finished.start:
-        earlier_ref, refs = refs[0], refs[1:]
-    best_all, total_all, score_ref, bias_ref, final_ref, semaphores, final_semaphores = refs[-7:]
-    results = refs[:-7]
-    held = (best_all, total_all)
-    carried = range(finished.stop, queries.stop)
+        best_in, total_in, earlier = (refs.pop(0) for _ in range(3))
+    refs, (best_ref, total_ref, score_ref, bias_ref, kv_ref, kv_semaphores) = refs[:-6], refs[-6:]
+    kv_copies = []
+    for number, source in enumerate(jax.tree.leaves(segments)):
+        copy = pltpu.make_async_copy(source, kv_ref.at[number], kv_semaphores.at[number])
+        copy.start()
+        kv_copies.append(copy)
+    segments = [
+        [kv_ref.at[place * halves + half] for half in range(halves)]
+        for place in range(len(segments))
+    ]
+    if 0 in which:
+        segments = [[query_ref] * halves] + segments
     mine = place_ref[QUARTER]
     ones = jnp.ones((count, HEAD_DIM), jnp.bfloat16)
     lanes = count // HEAD_DIM
-
-    def tile(index):
-        return slice(index * QUERY_TILE, (index + 1) * QUERY_TILE)
-
-    def tile_rows(index):
-        return pl.ds(index * count, count)
-
-    def state_copies(index, inward):
-        copies = []
-        for array in range(2):
-            inside = held[array].at[tile_rows(index - queries.start), :]
-            if inward:
-                ends = state_in[array].at[tile_rows(index - queries.start), :], inside
-            else:
-                ends = inside, results[array - 2].at[tile_rows(index - carried.start), :]
-            semaphore = semaphores.at[int(inward), array, index]
-            copies.append(pltpu.make_async_copy(*ends, semaphore))
-        return copies
-
+    copies = []
     if has_state:
-        for index in queries:
-            for copy in state_copies(index, True):
-                copy.start()
-    final_copies = []
-    if finished.stop and finished.start:
-        place = results[0].at[0 : finished.start * QUERY_TILE]
-        final_copies.append(pltpu.make_async_copy(earlier_ref, place, final_semaphores.at[0]))
-        final_copies[0].start()
+        held_best, held_total, final_ref, semaphores = refs[-4:]
+        shift = queries.start * QUERY_TILE
+        copies = [
+            pltpu.make_async_copy(best_in, held_best, semaphores.at[0]),
+            pltpu.make_async_copy(total_in, held_total, semaphores.at[1]),
+            pltpu.make_async_copy(earlier, final_ref.at[0:shift], semaphores.at[2]),
+        ]
+        for copy in copies:
+            copy.start()
 
     def positions(shape, dim, quarter):
         row = lax.broadcasted_iota(jnp.int32, shape, dim)
@@ -228,112 +219,135 @@
 
     def widen(value):
         return jnp.concatenate([value] * lanes, axis=1)
+
+    def part_of(segment, key_tile, from_end):
+        array = segment[key_tile // (tiles // 2)]
+        place = key_tile if array.shape[0] == BLOCKS else key_tile % (tiles // 2)
+        blocks = slice(place * QUERY_TILE, (place + 1) * QUERY_TILE)
+        return array[blocks, rows(array.shape[1] // PIECE - from_end), :].reshape(count, HEAD_DIM)
 
     query_places = widen(positions((count, HEAD_DIM), 0, mine))
     for slot, step in enumerate(which):
         allowed = positions((1, count), 1, mine ^ step) <= query_places
         bias_ref[slot] = jnp.where(allowed, 0.0, masked_score)
+    for copy in kv_copies:
+        copy.wait()
 
     for query_tile in queries:
-        here = query_tile - queries.start
-        best_ref = best_all.at[tile_rows(here), :]
-        total_ref = total_all.at[tile_rows(here), :]
-        query = query_ref[tile(query_tile), rows(0), :].reshape(count, HEAD_DIM)
-        if has_state:
-            for copy in state_copies(query_tile, True):
-                copy.wait()
-            best_before = best_ref[...]
-        else:
-            best_before = jnp.full((count, HEAD_DIM), masked_score, jnp.float32)
+        blocks = slice(query_tile * QUERY_TILE, (query_tile + 1) * QUERY_TILE)
+        here = slice((query_tile - queries.start) * count, (query_tile - queries.start + 1) * count)
+        query = query_ref[blocks, rows(0), :].reshape(count, HEAD_DIM)
         seen = [key_tile for key_tile in keys if key_tile <= query_tile]
-
-        best = best_before
+        best_ref[here, :] = jnp.full((count, HEAD_DIM), masked_score, jnp.float32)
         for key_tile in seen:
+            best = best_ref[here, :]
             for slot, segment in enumerate(segments):
-                part = tile(key_tile - keys.start)
-                key = segment[part, rows(segment.shape[1] // PIECE - 2), :]
-                score = dot(query, key.reshape(count, HEAD_DIM), 1, 1)
+                score = dot(query, part_of(segment, key_tile, 2), 1, 1)
                 if key_tile == query_tile:
                     score += bias_ref[slot]
-                score_ref[number * (key_tile - keys.start) + slot] = score
+                score_ref[len(which) * key_tile + slot] = score
                 for lane in range(lanes):
                     best = jnp.maximum(best, score[:, columns(lane)])
-        best = jnp.broadcast_to(jnp.max(best, axis=1, keepdims=True), best.shape)
-        best_ref[...] = best
-        if has_state:
-            shrink = jnp.exp2((best_before - best) * exponent_scale)
-            total_ref[...] *= jnp.concatenate([shrink, shrink], axis=1)
-        else:
-            total_ref[...] = jnp.zeros((count, 2 * HEAD_DIM), jnp.float32)
-
+            best_ref[here, :] = best
+        best = jnp.max(best_ref[here, :], axis=1, keepdims=True)
+        best_ref[here, :] = jnp.broadcast_to(best, (count, HEAD_DIM))
+        total_ref[here, :] = jnp.zeros((count, 2 * HEAD_DIM), jnp.float32)
         for key_tile in seen:
-            best_wide = widen(best_ref[...])
+            best_wide = widen(best_ref[here, :])
             weights, values = [], []
             for slot, segment in enumerate(segments):
-                score = score_ref[number * (key_tile - keys.start) + slot]
+                score = score_ref[len(which) * key_tile + slot]
                 weight = jnp.exp2((score - best_wide) * exponent_scale)
                 weights.append(weight.astype(jnp.bfloat16))
-                part = tile(key_tile - keys.start)
-                value = segment[part, rows(segment.shape[1] // PIECE - 1), :]
-                values.append(jnp.concatenate([value.reshape(count, HEAD_DIM), ones], axis=1))
-            total_ref[...] += dot(
+                values.append(jnp.concatenate([part_of(segment, key_tile, 1), ones], axis=1))
+            total_ref[here, :] += dot(
                 jnp.concatenate(weights, axis=1), jnp.concatenate(values, axis=0), 1, 0
             )
-        if query_tile in finished:
-            outcome = total_ref[:, :HEAD_DIM] / total_ref[:, HEAD_DIM:]
-            slot = tile(query_tile - finished.start)
-            final_ref[slot] = outcome.astype(jnp.bfloat16).reshape(QUERY_TILE, PIECE, HEAD_DIM)
-            copy = pltpu.make_async_copy(
-                final_ref.at[slot],
-                results[0].at[tile(query_tile)],
-                final_semaphores.at[1 + query_tile],
-            )
+        if finishes and not has_state:
+            total = total_ref[here, :]
+            outcome = (total[:, :HEAD_DIM] / total[:, HEAD_DIM:]).astype(jnp.bfloat16)
+            refs[0][blocks] = outcome.reshape(QUERY_TILE, PIECE, HEAD_DIM)
+
+    for copy in copies:
+        copy.wait()
+    if has_state:
+        for query_tile in queries:
+            blocks = slice(query_tile * QUERY_TILE, (query_tile + 1) * QUERY_TILE)
+            start = (query_tile - queries.start) * count
+            here = slice(start, start + count)
+            best = jnp.maximum(best_ref[here, :], held_best[here, :])
+            fresh = jnp.exp2((best_ref[here, :] - best) * exponent_scale)
+            before = jnp.exp2((held_best[here, :] - best) * exponent_scale)
+            low, high = slice(0, HEAD_DIM), slice(HEAD_DIM, 2 * HEAD_DIM)
+            value = fresh * total_ref[here, low] + before * held_total[here, low]
+            mass = fresh * total_ref[here, high] + before * held_total[here, high]
+            outcome = (value / mass).astype(jnp.bfloat16)
+            final_ref[blocks] = outcome.reshape(QUERY_TILE, PIECE, HEAD_DIM)
+        copy = pltpu.make_async_copy(final_ref, refs[0], semaphores.at[3])
+        copy.start()
+        copy.wait()
+    elif finishes:
+        refs[1][...] = total_ref[0:8, 0:HEAD_DIM]
+    else:
+        semaphores = refs[3]
+        outward = [
+            pltpu.make_async_copy(best_ref, refs[0], semaphores.at[0]),
+            pltpu.make_async_copy(total_ref, refs[1], semaphores.at[1]),
+        ]
+        for copy in outward:
             copy.start()
-            final_copies.append(copy)
-        else:
-            for copy in state_copies(query_tile, False):
-                copy.start()
-    for query_tile in carried:
-        for copy in state_copies(query_tile, False):
+        refs[2][...] = best_ref[0:8, :]
+        for copy in outward:
             copy.wait()
-    for copy in final_copies:
-        copy.wait()
-
-
-def attend(which, keys, queries, finished, place, packed, segments, state=None, token=(), earlier=()):
+
+
+def attend(which, keys, queries, place, packed, segments, state=(), token=(), finishes=True):
     shape = jax.ShapeDtypeStruct
     count = QUERY_TILE * PIECE
-    kernel = functools.partial(
-        attention_kernel, which, keys, queries, finished, state is not None
-    )
-    out_shape, out_spaces = [], []
-    if finished.stop:
-        out_shape.append(shape((finished.stop * QUERY_TILE, PIECE, HEAD_DIM), jnp.bfloat16))
-        out_spaces.append(pltpu.HBM)
-    left = queries.stop - finished.stop
-    if left:
-        for width in (HEAD_DIM, 2 * HEAD_DIM):
-            out_shape.append(shape((left * count, width), jnp.float32))
-            out_spaces.append(pltpu.HBM)
-    spaces = [pltpu.SMEM, *[pltpu.VMEM] * (1 + len(segments))]
-    if state is not None:
-        spaces += [pltpu.HBM, pltpu.HBM, pltpu.VMEM]
-    spaces += [pltpu.HBM] * len(earlier)
+    kernel = functools.partial(attention_kernel, which, keys, queries, bool(state), finishes)
+    best_shape = (len(queries) * count, HEAD_DIM)
+    total_shape = (len(queries) * count, 2 * HEAD_DIM)
+    token_shape = shape((8, HEAD_DIM), jnp.float32)
+    scratch = []
+    if state:
+        out_shape = [shape((BLOCKS, PIECE, HEAD_DIM), jnp.bfloat16)]
+        out_spaces = [pltpu.HBM]
+        scratch = [
+            pltpu.VMEM(best_shape, jnp.float32),
+            pltpu.VMEM(total_shape, jnp.float32),
+            pltpu.VMEM((BLOCKS, PIECE, HEAD_DIM), jnp.bfloat16),
+            pltpu.SemaphoreType.DMA((4,)),
+        ]
+    elif finishes:
+        out_shape = [shape((len(queries) * QUERY_TILE, PIECE, HEAD_DIM), jnp.bfloat16), token_shape]
+        out_spaces = [pltpu.VMEM, pltpu.VMEM]
+    else:
+        out_shape = [shape(best_shape, jnp.float32), shape(total_shape, jnp.float32), token_shape]
+        out_spaces = [pltpu.HBM, pltpu.HBM, pltpu.VMEM]
+        scratch = [pltpu.SemaphoreType.DMA((2,))]
+    segments = jax.tree.leaves(segments)
+    spaces = [pltpu.SMEM, pltpu.VMEM, *[pltpu.HBM] * (len(segments) + len(state))]
+    spaces += [pltpu.VMEM] * len(token)
+
+    def without_token(*refs):
+        place = 2 + len(segments) + len(state)
+        kernel(*refs[:place], *refs[place + len(token) :])
+
     return call(
-        kernel,
+        without_token,
         out_shape,
-        (place, packed, *segments, *(state or ()), *token, *earlier),
-        2 * 10**8 * len(which) * len(keys),
+        (place, packed, *segments, *state, *token),
+        10**8 * len(which) * len(keys),
         spaces,
         out_spaces,
         (
-            pltpu.VMEM((len(queries) * count, HEAD_DIM), jnp.float32),
-            pltpu.VMEM((len(queries) * count, 2 * HEAD_DIM), jnp.float32),
+            *scratch,
+            pltpu.VMEM(best_shape, jnp.float32),
+            pltpu.VMEM(total_shape, jnp.float32),
             pltpu.VMEM((len(which) * len(keys), count, count), jnp.float32),
             pltpu.VMEM((len(which), count, count), jnp.float32),
-            pltpu.VMEM((max(len(finished), 1) * QUERY_TILE, PIECE, HEAD_DIM), jnp.bfloat16),
-            pltpu.SemaphoreType.DMA((2, 2, BLOCKS // QUERY_TILE)),
-            pltpu.SemaphoreType.DMA((1 + BLOCKS // QUERY_TILE,)),
+            pltpu.VMEM((len(segments), BLOCKS // 2, 2 * PIECE, HEAD_DIM), jnp.bfloat16),
+            pltpu.SemaphoreType.DMA((len(segments),)),
         ),
         limit=24,
     )
@@ -420,27 +434,37 @@
         scratch=(pltpu.VMEM((HALF, HEAD_DIM), jnp.float32),),
     )
     kv0, chip = lax.optimization_barrier((kv0, chip))
-    early = BLOCKS // 2
-    kv2a = swap(kv0[:early, PIECE:], X_STEP)
-    kv1 = swap(kv0[:, PIECE:], 1)
+    half_blocks = BLOCKS // 2
+    kv0a, kv0 = lax.optimization_barrier((kv0[:half_blocks, PIECE:], kv0))
+    kv0b = kv0[half_blocks:, PIECE:]
+    kv2a = swap(kv0a, X_STEP)
+    kv1a, kv1b = swap(kv0a, 1), swap(kv0b, 1)
     chips = exchange(chip)
 
     tiles = BLOCKS // QUERY_TILE
-    every, low, high = range(tiles), range(tiles // 2), range(tiles // 2, tiles)
-    state = attend((0, 1), every, every, range(0), place, kv0, (kv0, kv1))
-    token, kv2a, kv0b = lax.optimization_barrier((state[0][0:8, :], kv2a, kv0[early:, PIECE:]))
+    early, late = range(tiles // 2), range(tiles // 2, tiles)
+    best, total, token = attend(
+        (0, 1), range(tiles), late, place, kv0, ((kv1a, kv1b),), finishes=False
+    )
+    token, kv2a, kv0b = lax.optimization_barrier((token, kv2a, kv0b))
     kv3a = swap(kv2a, 1)
     kv2b = swap(kv0b, X_STEP)
-    first, *state = attend(
-        (2, 3), low, every, low, place, kv0, (kv2a, kv3a), state, (token,)
-    )
-    token, chips = lax.optimization_barrier((state[0][0:8, :], chips))
+    first, token = attend(
+        (0, 1, 2, 3), early, early, place, kv0, ((kv1a,), (kv2a,), (kv3a,)), (), (token,)
+    )
+    token, chips, kv2b = lax.optimization_barrier((token, chips, kv2b))
+    kv3b = swap(kv2b, 1)
     (scanned,) = call(scan_kernel, [shape((BLOCKS, SLICE, HEAD_DIM), half)], (chips,), 10**6)
-    token, kv2b = lax.optimization_barrier((token, kv2b))
-    kv3b = swap(kv2b, 1)
     prior = exchange(scanned).reshape(HALF * HEAD_DIM, HEAD_DIM)
     (attended,) = attend(
-        (2, 3), high, high, high, place, kv0, (kv2b, kv3b), state, (token,), (first,)
+        (2, 3),
+        range(tiles),
+        late,
+        place,
+        kv0,
+        ((kv2a, kv2b), (kv3a, kv3b)),
+        (best, total, first),
+        (token,),
     )
     returned = exchange(attended)
     other_prior = swap(prior, 1)

time: 143 us -> 138 us (0.965)
  Pallas kernels: 44.1 us -> 35.1 us
  waiting for transfers between devices: 49 us -> 55.1 us
    pallas_call x9, Pallas kernels: 44.1 us -> 35.1 us  [call(): pl.pallas_call(kernel, out_shape=out_shape, in_specs=[whole(space) for sp...]
    ppermute x7 -> x8, waiting for transfers between devices: 2.87 us -> 7.34 us  [swap(): return lax.ppermute(value, 'ctx', [(d, d ^ step) for d in range(BLOCKS)])]
    all_to_all x4, starting transfers between devices: 37.7 us -> 33.8 us  [exchange(): return lax.all_to_all(value, 'ctx', split_axis=0, concat_axis=0, tiled=True)]
    ppermute x7 -> x8, starting transfers between devices: 4.84 us -> 7.56 us  [swap(): return lax.ppermute(value, 'ctx', [(d, d ^ step) for d in range(BLOCKS)])]
    slice x4 -> x2, local copies, waits for them, and re-layouts: 3.65 us -> 1.73 us  [the longest x1 0.86 us: shards(): kv0a, kv0 = lax.optimization_barrier((kv0[:half_blocks, PIECE:], kv0))]
    all_to_all x4, waiting for transfers between devices: 46.1 us -> 47.7 us  [exchange(): return lax.all_to_all(value, 'ctx', split_axis=0, concat_axis=0, tiled=True)]
    unnamed x11 -> x15, local copies, waits for them, and re-layouts: 1.17 us -> 2.65 us
  transfers between devices with their start and end apart: 11 -> 12, of which waited for: 6 -> 7; matrix products, arithmetic and copies ran while one was open for 2% -> 1% of each run, Pallas kernels for 29% -> 23%
where the time goes in v5:
time: 138 us; the launch traced here: 137 us
  waiting for transfers between devices  55.1 us (40%)
  starting transfers between devices  41.4 us (30%)
  Pallas kernels  35.1 us (25%)
  local copies, waits for them, and re-layouts  5.06 us (4%)
    all_to_all x4, waiting for transfers between devices, exchange(): return lax.all_to_all(value, 'ctx', split_axis=0, concat_axis=0, tiled=True)  47.7 us
    pallas_call x9, Pallas kernels, call(): pl.pallas_call(kernel, out_shape=out_shape, in_specs=[whole(space) for sp...  35.1 us
    all_to_all x4, starting transfers between devices, exchange(): return lax.all_to_all(value, 'ctx', split_axis=0, concat_axis=0, tiled=True)  33.8 us
    ppermute x8, starting transfers between devices, swap(): return lax.ppermute(value, 'ctx', [(d, d ^ step) for d in range(BLOCKS)])  7.56 us
    ppermute x8, waiting for transfers between devices, swap(): return lax.ppermute(value, 'ctx', [(d, d ^ step) for d in range(BLOCKS)])  7.34 us
  transfers between devices with their start and end apart: 12, of which 7 were waited for; matrix products, arithmetic and copies ran while one was open for 1% of the time, Pallas kernels for 23%

profile of v5, /device:TPU:1, one launch (start us, length us, event | category | flops | bytes accessed | tf_op | source)
XLA Modules:
  0.0 137.5 jit_solution(11334772279494090865)
XLA Ops:
  0.6 2.6 %shard_map.86 = bf16[64,96,128]{2,1,0:T(8,128)(2,1)} custom-call(bf16[128,2048]{1,0:T(8,128)(2,1)} %query_ref.2, bf16[128,2048]{1,0:T(8,128)(2,1)} %key_ref.3, bf16[128,2048]{1,0:T(8,128)(2,1)} %value_ref.3), custom_call_target="tpu_custom_call" | custom-call | flops 1000 | bytes 3145728 | tf_op jit(solution)/shard_map/pallas_call | solution.py:67
  3.3 0.0 copy-start.6
  3.3 0.0 copy-start
  3.3 0.0 copy-start.1
  3.3 13.1 %all-to-all-start = ((bf16[64,96,128]{2,1,0:T(8,128)(2,1)}), bf16[64,96,128]{2,1,0:T(8,128)(2,1)S(1)}, u32[]{:S(2)}, u32[]{:S(2)}) async-start(bf16[64,96,128]{2,1,0:T(8,128)(2,1)} %shard_map.86), calls=%async_computation | async-start | bytes 3145728 | tf_op jit(solution)/shard_map/all_to_all | solution.py:397
  16.4 0.0 copy-done.6
  16.5 0.1 copy.10.decay_ref
  16.6 0.0 copy-done
  16.6 0.0 copy-done.1
  16.6 1.0 shard_map.87.mine_ref
  17.6 0.5 collective-permute-start
  18.1 0.1 pad_add_fusion.place_ref.refs_0_
  18.2 1.5 %collective-permute-done.other_ref.sibling_ref = bf16[2096,128]{1,0:T(8,128)(2,1)S(1)} collective-permute-done((bf16[2096,128]{1,0:T(8,128)(2,1)S(1)}, bf16[2096,128]{1,0:T(8,128)(2,1)S(1)}, u32[]{:S(2)}, u32[]{:S(2)}) %collective-permute-start) | collective-permute-done | bytes 536608 | tf_op jit(solution)/shard_map/ppermute | solution.py:401
  19.7 1.5 %shard_map.88 = bf16[64,24,128]{2,1,0:T(8,128)(2,1)} custom-call(s32[2]{0:T(128)S(1)} %pad_add_fusion.place_ref.refs_0_, bf16[2096,128]{1,0:T(8,128)(2,1)S(1)} %shard_map.87.mine_ref, bf16[2096,128]{1,0:T(8,128)(2,1)S(1)} %collective-permute-done.other_ref.sibling_ref), custom_call_target="tpu_custom_call" | custom-call | flops 10000000 | bytes 1466376 | tf_op jit(solution)/shard_map/pallas_call | solution.py:67
  21.2 35.0 %all-to-all-done.refs_1_ = bf16[64,96,128]{2,1,0:T(8,128)(2,1)S(1)} async-done(((bf16[64,96,128]{2,1,0:T(8,128)(2,1)}), bf16[64,96,128]{2,1,0:T(8,128)(2,1)S(1)}, u32[]{:S(2)}, u32[]{:S(2)}) %all-to-all-start) | async-done | bytes 1572896 | tf_op jit(solution)/shard_map/all_to_all | solution.py:397
  56.2 0.9 slice.9
  57.1 0.9 slice.10
  58.0 0.2 collective-permute-start.2
  58.1 0.4 collective-permute-start.1
  58.5 1.2 collective-permute-start.3
  59.7 5.6 %all-to-all-start.1 = ((bf16[64,24,128]{2,1,0:T(8,128)(2,1)}), bf16[64,24,128]{2,1,0:T(8,128)(2,1)S(1)}, u32[]{:S(2)}, u32[]{:S(2)}) async-start(bf16[64,24,128]{2,1,0:T(8,128)(2,1)} %shard_map.88), calls=%async_computation.1 | async-start | bytes 786432 | tf_op jit(solution)/shard_map/all_to_all | solution.py:397
  65.3 0.0 collective-permute-done.2.refs_3_
  65.3 0.0 collective-permute-done.1.refs_2_
  65.3 8.4 %shard_map.89 = (f32[1024,128]{1,0:T(8,128)}, f32[1024,256]{1,0:T(8,128)}, f32[8,128]{1,0:T(8,128)S(1)}) custom-call(s32[2]{0:T(128)S(1)} %pad_add_fusion.place_ref.refs_0_, bf16[64,96,128]{2,1,0:T(8,128)(2,1)S(1)} %all-to-all-done.refs_1_, bf16[32,64,128]{2,1,0:T(8,128)(2,1)} %collective-permute-done.1.refs_2_, ...), custom_call_target="tpu_custom_call" | custom-call | flops 1600000000 | bytes 4198408 | tf_op jit(solution)/shard_map/pallas_call | solution.py:67
  73.7 0.2 collective-permute-done.3.refs_3_.refs_2_
  73.9 2.0 %collective-permute-start.4 = (bf16[32,64,128]{2,1,0:T(8,128)(2,1)}, bf16[32,64,128]{2,1,0:T(8,128)(2,1)S(1)}, u32[]{:S(2)}, u32[]{:S(2)}) collective-permute-start(bf16[32,64,128]{2,1,0:T(8,128)(2,1)} %collective-permute-done.3.refs_3_.refs_2_), channel_id=1, source_target_pairs={{0,4},{4,0},{8,12},{12,8},{16,20},{20,16},{24,28},{28,24},{32,36},... | collective-permute-start | bytes 1572872 | tf_op jit(solution)/shard_map/ppermute | solution.py:401
  75.9 2.1 %collective-permute-start.5 = (bf16[32,64,128]{2,1,0:T(8,128)(2,1)}, bf16[32,64,128]{2,1,0:T(8,128)(2,1)}, u32[]{:S(2)}, u32[]{:S(2)}) collective-permute-start(bf16[32,64,128]{2,1,0:T(8,128)(2,1)} %slice.10), channel_id=1, source_target_pairs={{0,64},{4,68},{8,72},{12,76},{16,80},{20,84},{24,88},{28,92},{32,9... | collective-permute-start | bytes 1572872 | tf_op jit(solution)/shard_map/ppermute | solution.py:401
  78.0 0.0 collective-permute-done.4.refs_4_
  78.0 0.0 copy-start.5
  78.0 0.8 copy-done.5
  78.8 6.6 %shard_map.90 = (bf16[32,32,128]{2,1,0:T(8,128)(2,1)S(1)}, f32[8,128]{1,0:T(8,128)S(1)}) custom-call(s32[2]{0:T(128)S(1)} %pad_add_fusion.place_ref.refs_0_, bf16[64,96,128]{2,1,0:T(8,128)(2,1)S(1)} %all-to-all-done.refs_1_, bf16[32,64,128]{2,1,0:T(8,128)(2,1)} %collective-permute-done.1.refs_2_, ...), custom_call_target="tpu_custom_call" | custom-call | flops 1600000000 | bytes 3416072 | tf_op jit(solution)/shard_map/pallas_call | solution.py:67
  85.5 0.0 copy-start.4
  85.5 0.7 copy-done.4
  86.2 0.0 all-to-all-done.1.moved_ref
  86.2 4.5 %collective-permute-done.5.refs_3_ = bf16[32,64,128]{2,1,0:T(8,128)(2,1)} collective-permute-done((bf16[32,64,128]{2,1,0:T(8,128)(2,1)}, bf16[32,64,128]{2,1,0:T(8,128)(2,1)}, u32[]{:S(2)}, u32[]{:S(2)}) %collective-permute-start.5) | collective-permute-done | bytes 524320 | tf_op jit(solution)/shard_map/ppermute | solution.py:401
  90.7 0.6 collective-permute-start.7
  91.2 0.9 shard_map.91
  92.1 7.6 %all-to-all-start.2 = ((bf16[64,16,128]{2,1,0:T(8,128)(2,1)}), bf16[64,16,128]{2,1,0:T(8,128)(2,1)S(1)}, u32[]{:S(2)}, u32[]{:S(2)}) async-start(bf16[64,16,128]{2,1,0:T(8,128)(2,1)} %shard_map.91), calls=%async_computation.2 | async-start | bytes 524288 | tf_op jit(solution)/shard_map/all_to_all | solution.py:397
  99.8 0.0 collective-permute-done.7.refs_5_
  99.8 0.0 copy-start.2
  99.8 9.1 %shard_map.93 = bf16[64,32,128]{2,1,0:T(8,128)(2,1)} custom-call(s32[2]{0:T(128)S(1)} %pad_add_fusion.place_ref.refs_0_, bf16[64,96,128]{2,1,0:T(8,128)(2,1)S(1)} %all-to-all-done.refs_1_, bf16[32,64,128]{2,1,0:T(8,128)(2,1)} %collective-permute-done.3.refs_3_.refs_2_, bf16[32,64,128]{2,1,0:T(8,128)(2,1)} %collective-permute-done.5.refs_3_, ...), custom_call_target="tpu_custom_call" | custom-call | flops 1600000000 | bytes 6033416 | tf_op jit(solution)/shard_map/pallas_call | solution.py:67
  108.9 2.8 %all-to-all-done.2 = bf16[64,16,128]{2,1,0:T(8,128)(2,1)S(1)} async-done(((bf16[64,16,128]{2,1,0:T(8,128)(2,1)}), bf16[64,16,128]{2,1,0:T(8,128)(2,1)S(1)}, u32[]{:S(2)}, u32[]{:S(2)}) %all-to-all-start.2) | async-done | bytes 262176 | tf_op jit(solution)/shard_map/all_to_all | solution.py:397
  111.8 7.5 %all-to-all-start.3 = ((bf16[64,32,128]{2,1,0:T(8,128)(2,1)}), bf16[64,32,128]{2,1,0:T(8,128)(2,1)S(1)}, u32[]{:S(2)}, u32[]{:S(2)}) async-start(bf16[64,32,128]{2,1,0:T(8,128)(2,1)} %shard_map.93), calls=%async_computation.3 | async-start | bytes 1048576 | tf_op jit(solution)/shard_map/all_to_all | solution.py:397
  119.3 0.5 collective-permute-start.6
  119.8 1.2 collective-permute-done.6.other_ref
  121.0 0.0 copy-done.2
  121.0 0.0 copy-start.3
  121.0 1.0 copy-done.3
  122.0 4.1 %shard_map.92 = bf16[128,2048]{1,0:T(8,128)(2,1)} custom-call(s32[2]{0:T(128)S(1)} %pad_add_fusion.place_ref.refs_0_, bf16[128,2048]{1,0:T(8,128)(2,1)S(1)} %copy-done.3, bf16[128,2048]{1,0:T(8,128)(2,1)S(1)} %copy-done, bf16[128,2048]{1,0:T(8,128)(2,1)S(1)} %copy-done.2, f32[128,16]{1,0:T(8,128)S(1)} %copy.10.decay_ref, bf16[1024,128]{1,0:T(8,128)(2,1)S(1)} %bitcast.4, ...), custom_call_target="tpu_custom_call" | custom-call | flops 200000000 | bytes 3166216 | tf_op jit(solution)/shard_map/pallas_call | solution.py:67
  126.1 0.7 slice.12.order_ref
  126.8 9.8 %all-to-all-done.3.moved_ref = bf16[64,32,128]{2,1,0:T(8,128)(2,1)S(1)} async-done(((bf16[64,32,128]{2,1,0:T(8,128)(2,1)}), bf16[64,32,128]{2,1,0:T(8,128)(2,1)S(1)}, u32[]{:S(2)}, u32[]{:S(2)}) %all-to-all-start.3) | async-done | bytes 524320 | tf_op jit(solution)/shard_map/all_to_all | solution.py:397
  136.6 0.9 shard_map.94
Async XLA Ops:
  3.3 13.2 %copy-start.6 = (f32[128,16]{0,1:T(8,128)S(1)}, f32[128,16]{0,1:T(8,128)}, u32[]{:S(2)}) copy-start(f32[128,16]{0,1:T(8,128)} %param.10) | copy-start | bytes 24580
  3.3 13.3 %copy-start = (bf16[128,2048]{1,0:T(8,128)(2,1)S(1)}, bf16[128,2048]{1,0:T(8,128)(2,1)}, u32[]{:S(2)}) copy-start(bf16[128,2048]{1,0:T(8,128)(2,1)} %key_ref.5) | copy-start | bytes 1572868
  3.3 13.3 %copy-start.1 = (bf16[128,2048]{1,0:T(8,128)(2,1)S(1)}, bf16[128,2048]{1,0:T(8,128)(2,1)}, u32[]{:S(2)}) copy-start(bf16[128,2048]{1,0:T(8,128)(2,1)} %value_ref.5) | copy-start | bytes 1572868
  3.3 52.9 %all-to-all-start = ((bf16[64,96,128]{2,1,0:T(8,128)(2,1)}), bf16[64,96,128]{2,1,0:T(8,128)(2,1)S(1)}, u32[]{:S(2)}, u32[]{:S(2)}) async-start(bf16[64,96,128]{2,1,0:T(8,128)(2,1)} %shard_map.86), calls=%async_computation | async-start | bytes 3145728 | tf_op jit(solution)/shard_map/all_to_all | solution.py:397
  17.6 2.1 %collective-permute-start = (bf16[2096,128]{1,0:T(8,128)(2,1)S(1)}, bf16[2096,128]{1,0:T(8,128)(2,1)S(1)}, u32[]{:S(2)}, u32[]{:S(2)}) collective-permute-start(bf16[2096,128]{1,0:T(8,128)(2,1)S(1)} %shard_map.87.mine_ref), channel_id=1, source_target_pairs={{0,4},{4,0},{8,12},{12,8},{16,20},{20,16},{24,28},{28,24},{32,36},... | collective-permute-start | bytes 1609736 | tf_op jit(solution)/shard_map/ppermute | solution.py:401
  58.0 7.3 %collective-permute-start.2 = (bf16[32,64,128]{2,1,0:T(8,128)(2,1)}, bf16[32,64,128]{2,1,0:T(8,128)(2,1)}, u32[]{:S(2)}, u32[]{:S(2)}) collective-permute-start(bf16[32,64,128]{2,1,0:T(8,128)(2,1)} %slice.10), channel_id=1, source_target_pairs={{0,4},{4,0},{8,12},{12,8},{16,20},{20,16},{24,28},{28,24},{32,36},... | collective-permute-start | bytes 1572872 | tf_op jit(solution)/shard_map/ppermute | solution.py:401
  58.1 7.2 %collective-permute-start.1 = (bf16[32,64,128]{2,1,0:T(8,128)(2,1)}, bf16[32,64,128]{2,1,0:T(8,128)(2,1)}, u32[]{:S(2)}, u32[]{:S(2)}) collective-permute-start(bf16[32,64,128]{2,1,0:T(8,128)(2,1)} %slice.9), channel_id=1, source_target_pairs={{0,4},{4,0},{8,12},{12,8},{16,20},{20,16},{24,28},{28,24},{32,36},... | collective-permute-start | bytes 1572872 | tf_op jit(solution)/shard_map/ppermute | solution.py:401
  58.5 15.4 %collective-permute-start.3 = (bf16[32,64,128]{2,1,0:T(8,128)(2,1)}, bf16[32,64,128]{2,1,0:T(8,128)(2,1)}, u32[]{:S(2)}, u32[]{:S(2)}) collective-permute-start(bf16[32,64,128]{2,1,0:T(8,128)(2,1)} %slice.9), channel_id=1, source_target_pairs={{0,64},{4,68},{8,72},{12,76},{16,80},{20,84},{24,88},{28,92},{32,9... | collective-permute-start | bytes 1572872 | tf_op jit(solution)/shard_map/ppermute | solution.py:401
  59.7 26.5 %all-to-all-start.1 = ((bf16[64,24,128]{2,1,0:T(8,128)(2,1)}), bf16[64,24,128]{2,1,0:T(8,128)(2,1)S(1)}, u32[]{:S(2)}, u32[]{:S(2)}) async-start(bf16[64,24,128]{2,1,0:T(8,128)(2,1)} %shard_map.88), calls=%async_computation.1 | async-start | bytes 786432 | tf_op jit(solution)/shard_map/all_to_all | solution.py:397
  73.9 4.2 %collective-permute-start.4 = (bf16[32,64,128]{2,1,0:T(8,128)(2,1)}, bf16[32,64,128]{2,1,0:T(8,128)(2,1)S(1)}, u32[]{:S(2)}, u32[]{:S(2)}) collective-permute-start(bf16[32,64,128]{2,1,0:T(8,128)(2,1)} %collective-permute-done.3.refs_3_.refs_2_), channel_id=1, source_target_pairs={{0,4},{4,0},{8,12},{12,8},{16,20},{20,16},{24,28},{28,24},{32,36},... | collective-permute-start | bytes 1572872 | tf_op jit(solution)/shard_map/ppermute | solution.py:401
  75.9 14.7 %collective-permute-start.5 = (bf16[32,64,128]{2,1,0:T(8,128)(2,1)}, bf16[32,64,128]{2,1,0:T(8,128)(2,1)}, u32[]{:S(2)}, u32[]{:S(2)}) collective-permute-start(bf16[32,64,128]{2,1,0:T(8,128)(2,1)} %slice.10), channel_id=1, source_target_pairs={{0,64},{4,68},{8,72},{12,76},{16,80},{20,84},{24,88},{28,92},{32,9... | collective-permute-start | bytes 1572872 | tf_op jit(solution)/shard_map/ppermute | solution.py:401
  78.0 0.8 copy-start.5
  85.5 0.7 copy-start.4
  90.7 9.1 %collective-permute-start.7 = (bf16[32,64,128]{2,1,0:T(8,128)(2,1)}, bf16[32,64,128]{2,1,0:T(8,128)(2,1)}, u32[]{:S(2)}, u32[]{:S(2)}) collective-permute-start(bf16[32,64,128]{2,1,0:T(8,128)(2,1)} %collective-permute-done.5.refs_3_), channel_id=1, source_target_pairs={{0,4},{4,0},{8,12},{12,8},{16,20},{20,16},{24,28},{28,24},{32,36},... | collective-permute-start | bytes 1572872 | tf_op jit(solution)/shard_map/ppermute | solution.py:401
  92.1 19.6 %all-to-all-start.2 = ((bf16[64,16,128]{2,1,0:T(8,128)(2,1)}), bf16[64,16,128]{2,1,0:T(8,128)(2,1)S(1)}, u32[]{:S(2)}, u32[]{:S(2)}) async-start(bf16[64,16,128]{2,1,0:T(8,128)(2,1)} %shard_map.91), calls=%async_computation.2 | async-start | bytes 524288 | tf_op jit(solution)/shard_map/all_to_all | solution.py:397
  99.8 21.2 %copy-start.2 = (bf16[128,2048]{1,0:T(8,128)(2,1)S(1)}, bf16[128,2048]{1,0:T(8,128)(2,1)}, u32[]{:S(2)}) copy-start(bf16[128,2048]{1,0:T(8,128)(2,1)} %value_ref.5) | copy-start | bytes 1572868
  111.8 24.8 %all-to-all-start.3 = ((bf16[64,32,128]{2,1,0:T(8,128)(2,1)}), bf16[64,32,128]{2,1,0:T(8,128)(2,1)S(1)}, u32[]{:S(2)}, u32[]{:S(2)}) async-start(bf16[64,32,128]{2,1,0:T(8,128)(2,1)} %shard_map.93), calls=%async_computation.3 | async-start | bytes 1048576 | tf_op jit(solution)/shard_map/all_to_all | solution.py:397
  119.3 1.7 %collective-permute-start.6 = (bf16[1024,128]{1,0:T(8,128)(2,1)S(1)}, bf16[1024,128]{1,0:T(8,128)(2,1)S(1)}, u32[]{:S(2)}, u32[]{:S(2)}) collective-permute-start(bf16[1024,128]{1,0:T(8,128)(2,1)S(1)} %bitcast.3), channel_id=1, source_target_pairs={{0,4},{4,0},{8,12},{12,8},{16,20},{20,16},{24,28},{28,24},{32,36},... | collective-permute-start | bytes 786440 | tf_op jit(solution)/shard_map/ppermute | solution.py:401
  121.0 1.0 copy-start.3

commit v6 on v4

--- a/solution.py
+++ b/solution.py
@@ -22,6 +22,11 @@
 SLICE = HALF * HEAD_DIM // BLOCKS
 QUARTER, CORE = range(2)
 QUERY_TILE = 8
+TILE_ROWS = QUERY_TILE * PIECE
+LANES = TILE_ROWS // HEAD_DIM
+TILES = BLOCKS // QUERY_TILE
+HALF_TILES = TILES // 2
+EARLY, LATE = range(HALF_TILES), range(HALF_TILES, TILES)
 
 
 def place_of(device):
@@ -72,7 +77,7 @@
         scratch_shapes=list(scratch),
         compiler_params=pltpu.CompilerParams(vmem_limit_bytes=limit << 20),
         cost_estimate=pl.CostEstimate(
-            flops=flops, bytes_accessed=bytes_moved, transcendentals=0
+            flops=flops, bytes_accessed=bytes_moved if flops else 0, transcendentals=0
         ),
     )(*operands)
 
@@ -178,165 +183,246 @@
     lax.fori_loop(0, BLOCKS // 2, step, (zero, zero), unroll=4)
 
 
-def attention_kernel(which, keys, queries, finished, has_state, place_ref, query_ref, *refs):
-    count = QUERY_TILE * PIECE
-    number = len(which)
-    segments, refs = refs[:number], refs[number:]
-    if has_state:
-        state_in, refs = refs[:2], refs[2 + 1 :]
-    if finished.stop and finished.start:
-        earlier_ref, refs = refs[0], refs[1:]
-    best_all, total_all, score_ref, bias_ref, final_ref, semaphores, final_semaphores = refs[-7:]
-    results = refs[:-7]
-    held = (best_all, total_all)
-    carried = range(finished.stop, queries.stop)
+def tile_pairs(queries, keys):
+    return [(query, key) for query in queries for key in keys if key <= query]
+
+
+def tile_blocks(index):
+    return slice(index * QUERY_TILE, (index + 1) * QUERY_TILE)
+
+
+class Attention:
+    def __init__(self, queries, keys, slots, query_ref, part, bias_ref, best_ref, total_ref, score_ref):
+        self.queries, self.keys, self.slots = queries, keys, slots
+        self.query_ref, self.part, self.bias_ref = query_ref, part, bias_ref
+        self.best_ref, self.total_ref, self.score_ref = best_ref, total_ref, score_ref
+        self.pairs = tile_pairs(queries, keys)
+        best_ref[...] = jnp.full(best_ref.shape, masked_score, jnp.float32)
+
+    def here(self, query_tile):
+        start = (query_tile - self.queries.start) * TILE_ROWS
+        return slice(start, start + TILE_ROWS)
+
+    def place(self, query_tile, key_tile, slot):
+        return len(self.slots) * self.pairs.index((query_tile, key_tile)) + self.slots.index(slot)
+
+    def find_best(self, query_tile, slots):
+        here = self.here(query_tile)
+        query = self.query_ref[tile_blocks(query_tile), rows(0), :].reshape(TILE_ROWS, HEAD_DIM)
+        for key_tile in self.keys:
+            if key_tile > query_tile or not slots:
+                continue
+            best = self.best_ref[here, :]
+            for slot in slots:
+                score = dot(query, self.part(slot, key_tile, 2), 1, 1)
+                if key_tile == query_tile:
+                    score += self.bias_ref[slot]
+                self.score_ref[self.place(query_tile, key_tile, slot)] = score
+                for lane in range(LANES):
+                    best = jnp.maximum(best, score[:, columns(lane)])
+            self.best_ref[here, :] = best
+
+    def add_up(self, query_tile):
+        here = self.here(query_tile)
+        best = jnp.max(self.best_ref[here, :], axis=1, keepdims=True)
+        self.best_ref[here, :] = jnp.broadcast_to(best, (TILE_ROWS, HEAD_DIM))
+        self.total_ref[here, :] = jnp.zeros((TILE_ROWS, 2 * HEAD_DIM), jnp.float32)
+        ones = jnp.ones((TILE_ROWS, HEAD_DIM), jnp.bfloat16)
+        for key_tile in self.keys:
+            if key_tile > query_tile:
+                continue
+            best_wide = jnp.concatenate([self.best_ref[here, :]] * LANES, axis=1)
+            weights, values = [], []
+            for slot in self.slots:
+                score = self.score_ref[self.place(query_tile, key_tile, slot)]
+                weight = jnp.exp2((score - best_wide) * exponent_scale)
+                weights.append(weight.astype(jnp.bfloat16))
+                values.append(jnp.concatenate([self.part(slot, key_tile, 1), ones], axis=1))
+            self.total_ref[here, :] += dot(
+                jnp.concatenate(weights, axis=1), jnp.concatenate(values, axis=0), 1, 0
+            )
+
+
+def load_part(array, place, from_end):
+    wanted = rows(array.shape[1] // PIECE - from_end)
+    return array[tile_blocks(place), wanted, :].reshape(TILE_ROWS, HEAD_DIM)
+
+
+def fill_bias(place_ref, bias_ref, steps):
     mine = place_ref[QUARTER]
-    ones = jnp.ones((count, HEAD_DIM), jnp.bfloat16)
-    lanes = count // HEAD_DIM
-
-    def tile(index):
-        return slice(index * QUERY_TILE, (index + 1) * QUERY_TILE)
-
-    def tile_rows(index):
-        return pl.ds(index * count, count)
-
-    def state_copies(index, inward):
-        copies = []
-        for array in range(2):
-            inside = held[array].at[tile_rows(index - queries.start), :]
-            if inward:
-                ends = state_in[array].at[tile_rows(index - queries.start), :], inside
-            else:
-                ends = inside, results[array - 2].at[tile_rows(index - carried.start), :]
-            semaphore = semaphores.at[int(inward), array, index]
-            copies.append(pltpu.make_async_copy(*ends, semaphore))
-        return copies
-
-    if has_state:
-        for index in queries:
-            for copy in state_copies(index, True):
-                copy.start()
-    final_copies = []
-    if finished.stop and finished.start:
-        place = results[0].at[0 : finished.start * QUERY_TILE]
-        final_copies.append(pltpu.make_async_copy(earlier_ref, place, final_semaphores.at[0]))
-        final_copies[0].start()
 
     def positions(shape, dim, quarter):
         row = lax.broadcasted_iota(jnp.int32, shape, dim)
         return (row // PIECE) * TOKENS + row % PIECE + quarter * PIECE
 
-    def widen(value):
-        return jnp.concatenate([value] * lanes, axis=1)
-
-    query_places = widen(positions((count, HEAD_DIM), 0, mine))
-    for slot, step in enumerate(which):
-        allowed = positions((1, count), 1, mine ^ step) <= query_places
+    queries = positions((TILE_ROWS, HEAD_DIM), 0, mine)
+    queries = jnp.concatenate([queries] * LANES, axis=1)
+    for slot, step in enumerate(steps):
+        allowed = positions((1, TILE_ROWS), 1, mine ^ step) <= queries
         bias_ref[slot] = jnp.where(allowed, 0.0, masked_score)
 
-    for query_tile in queries:
-        here = query_tile - queries.start
-        best_ref = best_all.at[tile_rows(here), :]
-        total_ref = total_all.at[tile_rows(here), :]
-        query = query_ref[tile(query_tile), rows(0), :].reshape(count, HEAD_DIM)
-        if has_state:
-            for copy in state_copies(query_tile, True):
-                copy.wait()
-            best_before = best_ref[...]
-        else:
-            best_before = jnp.full((count, HEAD_DIM), masked_score, jnp.float32)
-        seen = [key_tile for key_tile in keys if key_tile <= query_tile]
-
-        best = best_before
-        for key_tile in seen:
-            for slot, segment in enumerate(segments):
-                part = tile(key_tile - keys.start)
-                key = segment[part, rows(segment.shape[1] // PIECE - 2), :]
-                score = dot(query, key.reshape(count, HEAD_DIM), 1, 1)
-                if key_tile == query_tile:
-                    score += bias_ref[slot]
-                score_ref[number * (key_tile - keys.start) + slot] = score
-                for lane in range(lanes):
-                    best = jnp.maximum(best, score[:, columns(lane)])
-        best = jnp.broadcast_to(jnp.max(best, axis=1, keepdims=True), best.shape)
-        best_ref[...] = best
-        if has_state:
-            shrink = jnp.exp2((best_before - best) * exponent_scale)
-            total_ref[...] *= jnp.concatenate([shrink, shrink], axis=1)
-        else:
-            total_ref[...] = jnp.zeros((count, 2 * HEAD_DIM), jnp.float32)
-
-        for key_tile in seen:
-            best_wide = widen(best_ref[...])
-            weights, values = [], []
-            for slot, segment in enumerate(segments):
-                score = score_ref[number * (key_tile - keys.start) + slot]
-                weight = jnp.exp2((score - best_wide) * exponent_scale)
-                weights.append(weight.astype(jnp.bfloat16))
-                part = tile(key_tile - keys.start)
-                value = segment[part, rows(segment.shape[1] // PIECE - 1), :]
-                values.append(jnp.concatenate([value.reshape(count, HEAD_DIM), ones], axis=1))
-            total_ref[...] += dot(
-                jnp.concatenate(weights, axis=1), jnp.concatenate(values, axis=0), 1, 0
+
+def start_copies(sources, targets, semaphores):
+    copies = [
+        pltpu.make_async_copy(source, target, semaphores.at[number])
+        for number, (source, target) in enumerate(zip(sources, targets))
+    ]
+    for copy in copies:
+        copy.start()
+    return copies
+
+
+def ratio(total):
+    outcome = (total[:, :HEAD_DIM] / total[:, HEAD_DIM:]).astype(jnp.bfloat16)
+    return outcome.reshape(QUERY_TILE, PIECE, HEAD_DIM)
+
+
+def first_kernel(
+    place_ref, packed_ref, early_ref, late_ref, best_out, total_out, token_ref,
+    kv_ref, bias_ref, best_ref, total_ref, score_ref, kv_sems, out_sems,
+):
+    copies = start_copies((early_ref, late_ref), (kv_ref.at[0], kv_ref.at[1]), kv_sems)
+    fill_bias(place_ref, bias_ref, (0, 1))
+
+    def part(slot, key_tile, from_end):
+        if slot == 0:
+            return load_part(packed_ref, key_tile, from_end)
+        return load_part(kv_ref.at[key_tile // HALF_TILES], key_tile % HALF_TILES, from_end)
+
+    work = Attention(
+        LATE, range(TILES), (0, 1), packed_ref, part, bias_ref, best_ref, total_ref, score_ref
+    )
+    for query_tile in LATE:
+        work.find_best(query_tile, (0,))
+    for copy in copies:
+        copy.wait()
+    outward, sent = [], 0
+    for query_tile in LATE:
+        work.find_best(query_tile, (1,))
+        work.add_up(query_tile)
+        if query_tile >= TILES - 2:
+            done = work.here(query_tile).stop
+            place = pl.ds(sent, done - sent)
+            outward += start_copies(
+                (best_ref.at[place, :], total_ref.at[place, :]),
+                (best_out.at[place, :], total_out.at[place, :]),
+                out_sems.at[query_tile - (TILES - 2)],
             )
-        if query_tile in finished:
-            outcome = total_ref[:, :HEAD_DIM] / total_ref[:, HEAD_DIM:]
-            slot = tile(query_tile - finished.start)
-            final_ref[slot] = outcome.astype(jnp.bfloat16).reshape(QUERY_TILE, PIECE, HEAD_DIM)
-            copy = pltpu.make_async_copy(
-                final_ref.at[slot],
-                results[0].at[tile(query_tile)],
-                final_semaphores.at[1 + query_tile],
-            )
-            copy.start()
-            final_copies.append(copy)
-        else:
-            for copy in state_copies(query_tile, False):
-                copy.start()
-    for query_tile in carried:
-        for copy in state_copies(query_tile, False):
-            copy.wait()
-    for copy in final_copies:
-        copy.wait()
-
-
-def attend(which, keys, queries, finished, place, packed, segments, state=None, token=(), earlier=()):
-    shape = jax.ShapeDtypeStruct
-    count = QUERY_TILE * PIECE
-    kernel = functools.partial(
-        attention_kernel, which, keys, queries, finished, state is not None
-    )
-    out_shape, out_spaces = [], []
-    if finished.stop:
-        out_shape.append(shape((finished.stop * QUERY_TILE, PIECE, HEAD_DIM), jnp.bfloat16))
-        out_spaces.append(pltpu.HBM)
-    left = queries.stop - finished.stop
-    if left:
-        for width in (HEAD_DIM, 2 * HEAD_DIM):
-            out_shape.append(shape((left * count, width), jnp.float32))
-            out_spaces.append(pltpu.HBM)
-    spaces = [pltpu.SMEM, *[pltpu.VMEM] * (1 + len(segments))]
-    if state is not None:
-        spaces += [pltpu.HBM, pltpu.HBM, pltpu.VMEM]
-    spaces += [pltpu.HBM] * len(earlier)
-    return call(
-        kernel,
-        out_shape,
-        (place, packed, *segments, *(state or ()), *token, *earlier),
-        2 * 10**8 * len(which) * len(keys),
-        spaces,
-        out_spaces,
-        (
-            pltpu.VMEM((len(queries) * count, HEAD_DIM), jnp.float32),
-            pltpu.VMEM((len(queries) * count, 2 * HEAD_DIM), jnp.float32),
-            pltpu.VMEM((len(which) * len(keys), count, count), jnp.float32),
-            pltpu.VMEM((len(which), count, count), jnp.float32),
-            pltpu.VMEM((max(len(finished), 1) * QUERY_TILE, PIECE, HEAD_DIM), jnp.bfloat16),
-            pltpu.SemaphoreType.DMA((2, 2, BLOCKS // QUERY_TILE)),
-            pltpu.SemaphoreType.DMA((1 + BLOCKS // QUERY_TILE,)),
-        ),
-        limit=24,
-    )
+            sent = done
+    token_ref[...] = best_ref[0:8, :]
+    for copy in outward:
+        copy.wait()
+
+
+def second_kernel(
+    place_ref, packed_ref, sibling_ref, across_ref, diagonal_ref, order_ref,
+    best_out, total_out, final_out, token_ref,
+    kv_ref, bias_ref, best_ref, total_ref, score_ref, best2_ref, total2_ref, score2_ref, final_ref,
+    kv_sems, out_sems, final_sem,
+):
+    copies = start_copies((across_ref, sibling_ref), (kv_ref.at[1], kv_ref.at[0]), kv_sems)
+    fill_bias(place_ref, bias_ref, (0, 1, 2, 3))
+
+    def part(slot, key_tile, from_end):
+        if slot == 0:
+            return load_part(packed_ref, key_tile, from_end)
+        return load_part(diagonal_ref if slot == 3 else kv_ref.at[slot - 1], key_tile, from_end)
+
+    early = Attention(
+        EARLY, EARLY, (0, 1, 2, 3), packed_ref, part, bias_ref, best2_ref, total2_ref, score2_ref
+    )
+    for query_tile in EARLY:
+        early.find_best(query_tile, (0,))
+    late = Attention(
+        LATE, EARLY, (2, 3), packed_ref, part, bias_ref, best_ref, total_ref, score_ref
+    )
+    for copy in copies:
+        copy.wait()
+    for query_tile in LATE:
+        late.find_best(query_tile, (2, 3))
+        late.add_up(query_tile)
+    outward = start_copies((best_ref, total_ref), (best_out, total_out), out_sems)
+    for query_tile in EARLY:
+        early.find_best(query_tile, (1, 2, 3))
+        early.add_up(query_tile)
+        final_ref[tile_blocks(query_tile)] = ratio(total2_ref[early.here(query_tile), :])
+    copy = pltpu.make_async_copy(final_ref, final_out, final_sem)
+    copy.start()
+    token_ref[...] = best2_ref[0:8, :]
+    for other in outward:
+        other.wait()
+    copy.wait()
+
+
+def third_kernel(
+    place_ref, packed_ref, across_ref, diagonal_ref, best_a, total_a, best_b, total_b, final_in, order_ref,
+    out_ref,
+    kv_ref, bias_ref, best_ref, total_ref, score_ref, bests_ref, totals_ref, final_ref,
+    kv_sems, state_sems, final_sems,
+):
+    copies = start_copies((across_ref, diagonal_ref), (kv_ref.at[0], kv_ref.at[1]), kv_sems)
+    half_blocks = BLOCKS // 2
+    state = start_copies(
+        (best_a, best_b, total_a, total_b, final_in),
+        (bests_ref.at[0], bests_ref.at[1], totals_ref.at[0], totals_ref.at[1], final_ref.at[0:half_blocks]),
+        state_sems,
+    )
+    fill_bias(place_ref, bias_ref, (2, 3))
+
+    def part(slot, key_tile, from_end):
+        return load_part(kv_ref.at[slot], key_tile % HALF_TILES, from_end)
+
+    for copy in copies:
+        copy.wait()
+    work = Attention(
+        LATE, LATE, (0, 1), packed_ref, part, bias_ref, best_ref, total_ref, score_ref
+    )
+    for query_tile in LATE:
+        work.find_best(query_tile, (0, 1))
+        work.add_up(query_tile)
+    for copy in state:
+        copy.wait()
+    outward = start_copies(
+        (final_ref.at[0:half_blocks],), (out_ref.at[0:half_blocks],), final_sems
+    )
+    for query_tile in LATE:
+        here = work.here(query_tile)
+        bests = [best_ref[here, :], bests_ref[0, here, :], bests_ref[1, here, :]]
+        totals = [total_ref[here, :], totals_ref[0, here, :], totals_ref[1, here, :]]
+        best = functools.reduce(jnp.maximum, bests)
+        joined = 0.0
+        for one, total in zip(bests, totals):
+            shrink = jnp.exp2((one - best) * exponent_scale)
+            joined += jnp.concatenate([shrink, shrink], axis=1) * total
+        blocks = tile_blocks(query_tile)
+        final_ref[blocks] = ratio(joined)
+        outward += start_copies(
+            (final_ref.at[blocks],),
+            (out_ref.at[blocks],),
+            final_sems.at[1 + query_tile - LATE.start : 2 + query_tile - LATE.start],
+        )
+    for copy in outward:
+        copy.wait()
+
+
+def work_space(queries, keys, slots):
+    rows_here = len(queries) * TILE_ROWS
+    return [
+        pltpu.VMEM((rows_here, HEAD_DIM), jnp.float32),
+        pltpu.VMEM((rows_here, 2 * HEAD_DIM), jnp.float32),
+        pltpu.VMEM((slots * len(tile_pairs(queries, keys)), TILE_ROWS, TILE_ROWS), jnp.float32),
+    ]
+
+
+def final_space(blocks):
+    return pltpu.VMEM((blocks, PIECE, HEAD_DIM), jnp.bfloat16)
+
+
+def attention_space(segments, slots):
+    return [
+        pltpu.VMEM((segments, BLOCKS // 2, 2 * PIECE, HEAD_DIM), jnp.bfloat16),
+        pltpu.VMEM((slots, TILE_ROWS, TILE_ROWS), jnp.float32),
+    ]
 
 
 def lightning_kernel(
@@ -420,27 +506,73 @@
         scratch=(pltpu.VMEM((HALF, HEAD_DIM), jnp.float32),),
     )
     kv0, chip = lax.optimization_barrier((kv0, chip))
-    early = BLOCKS // 2
-    kv2a = swap(kv0[:early, PIECE:], X_STEP)
-    kv1 = swap(kv0[:, PIECE:], 1)
+    half_blocks = BLOCKS // 2
+    kv0a, kv0 = lax.optimization_barrier((kv0[:half_blocks, PIECE:], kv0))
+    kv0b = kv0[half_blocks:, PIECE:]
+    kv2a = swap(kv0a, X_STEP)
+    kv1a, kv1b = swap(kv0a, 1), swap(kv0b, 1)
     chips = exchange(chip)
 
-    tiles = BLOCKS // QUERY_TILE
-    every, low, high = range(tiles), range(tiles // 2), range(tiles // 2, tiles)
-    state = attend((0, 1), every, every, range(0), place, kv0, (kv0, kv1))
-    token, kv2a, kv0b = lax.optimization_barrier((state[0][0:8, :], kv2a, kv0[early:, PIECE:]))
+    dma = pltpu.SemaphoreType.DMA
+    token_shape = shape((8, HEAD_DIM), jnp.float32)
+    state_shapes = [
+        shape((len(LATE) * TILE_ROWS, HEAD_DIM), jnp.float32),
+        shape((len(LATE) * TILE_ROWS, 2 * HEAD_DIM), jnp.float32),
+    ]
+    in_hbm, in_vmem, in_smem = pltpu.HBM, pltpu.VMEM, pltpu.SMEM
+    best_a, total_a, token = call(
+        first_kernel,
+        [*state_shapes, token_shape],
+        (place, kv0, kv1a, kv1b),
+        0,
+        [in_smem, in_vmem, in_hbm, in_hbm],
+        [in_hbm, in_hbm, in_vmem],
+        [*attention_space(2, 2), *work_space(LATE, range(TILES), 2), dma((2,)), dma((2, 2))],
+        limit=32,
+    )
+    token, kv2a, kv0b = lax.optimization_barrier((token, kv2a, kv0b))
     kv3a = swap(kv2a, 1)
     kv2b = swap(kv0b, X_STEP)
-    first, *state = attend(
-        (2, 3), low, every, low, place, kv0, (kv2a, kv3a), state, (token,)
-    )
-    token, chips = lax.optimization_barrier((state[0][0:8, :], chips))
+    best_b, total_b, first, token = call(
+        second_kernel,
+        [*state_shapes, shape((half_blocks, PIECE, HEAD_DIM), half), token_shape],
+        (place, kv0, kv1a, kv2a, kv3a, token),
+        0,
+        [in_smem, in_vmem, in_hbm, in_hbm, in_vmem, in_vmem],
+        [in_hbm, in_hbm, in_hbm, in_vmem],
+        [
+            *attention_space(2, 4),
+            *work_space(LATE, EARLY, 2),
+            *work_space(EARLY, EARLY, 4),
+            final_space(half_blocks),
+            dma((2,)),
+            dma((2,)),
+            dma,
+        ],
+        limit=40,
+    )
+    token, chips, kv2b = lax.optimization_barrier((token, chips, kv2b))
+    kv3b = swap(kv2b, 1)
     (scanned,) = call(scan_kernel, [shape((BLOCKS, SLICE, HEAD_DIM), half)], (chips,), 10**6)
-    token, kv2b = lax.optimization_barrier((token, kv2b))
-    kv3b = swap(kv2b, 1)
     prior = exchange(scanned).reshape(HALF * HEAD_DIM, HEAD_DIM)
-    (attended,) = attend(
-        (2, 3), high, high, high, place, kv0, (kv2b, kv3b), state, (token,), (first,)
+    (attended,) = call(
+        third_kernel,
+        [shape((BLOCKS, PIECE, HEAD_DIM), half)],
+        (place, kv0, kv2b, kv3b, best_a, total_a, best_b, total_b, first, token),
+        0,
+        [in_smem, in_vmem, *[in_hbm] * 7, in_vmem],
+        [in_hbm],
+        [
+            *attention_space(2, 2),
+            *work_space(LATE, LATE, 2),
+            pltpu.VMEM((2, len(LATE) * TILE_ROWS, HEAD_DIM), jnp.float32),
+            pltpu.VMEM((2, len(LATE) * TILE_ROWS, 2 * HEAD_DIM), jnp.float32),
+            final_space(BLOCKS),
+            dma((2,)),
+            dma((5,)),
+            dma((1 + len(LATE),)),
+        ],
+        limit=32,
     )
     returned = exchange(attended)
     other_prior = swap(prior, 1)

time: 143 us -> 135 us (0.944)
  Pallas kernels: 44.1 us -> 33.1 us
  waiting for transfers between devices: 49 us -> 58.5 us
  starting transfers between devices: 42.6 us -> 38.2 us
  local copies, waits for them, and re-layouts: 5.49 us -> 3.57 us
    pallas_call x9, Pallas kernels: 44.1 us -> 33.1 us  [call(): pl.pallas_call(kernel, out_shape=out_shape, in_specs=[whole(space) for sp...]
    all_to_all x4, starting transfers between devices: 37.7 us -> 30.7 us  [exchange(): return lax.all_to_all(value, 'ctx', split_axis=0, concat_axis=0, tiled=True)]
    ppermute x7 -> x8, waiting for transfers between devices: 2.87 us -> 8.16 us  [swap(): return lax.ppermute(value, 'ctx', [(d, d ^ step) for d in range(BLOCKS)])]
    all_to_all x4, waiting for transfers between devices: 46.1 us -> 50.3 us  [exchange(): return lax.all_to_all(value, 'ctx', split_axis=0, concat_axis=0, tiled=True)]
    ppermute x7 -> x8, starting transfers between devices: 4.84 us -> 7.56 us  [swap(): return lax.ppermute(value, 'ctx', [(d, d ^ step) for d in range(BLOCKS)])]
    slice x4 -> x2, local copies, waits for them, and re-layouts: 3.65 us -> 1.73 us  [the longest x1 0.86 us: shards(): kv0a, kv0 = lax.optimization_barrier((kv0[:half_blocks, PIECE:], kv0))]
  transfers between devices with their start and end apart: 11 -> 12, of which waited for: 6 -> 7; matrix products, arithmetic and copies ran while one was open for 2% -> 1% of each run, Pallas kernels for 29% -> 22%
where the time goes in v6:
time: 135 us; the launch traced here: 134 us
  waiting for transfers between devices  58.5 us (43%)
  starting transfers between devices  38.2 us (28%)
  Pallas kernels  33.1 us (25%)
  local copies, waits for them, and re-layouts  3.57 us (3%)
    all_to_all x4, waiting for transfers between devices, exchange(): return lax.all_to_all(value, 'ctx', split_axis=0, concat_axis=0, tiled=True)  50.3 us
    pallas_call x9, Pallas kernels, call(): pl.pallas_call(kernel, out_shape=out_shape, in_specs=[whole(space) for sp...  33.1 us
    all_to_all x4, starting transfers between devices, exchange(): return lax.all_to_all(value, 'ctx', split_axis=0, concat_axis=0, tiled=True)  30.7 us
    ppermute x8, waiting for transfers between devices, swap(): return lax.ppermute(value, 'ctx', [(d, d ^ step) for d in range(BLOCKS)])  8.16 us
    ppermute x8, starting transfers between devices, swap(): return lax.ppermute(value, 'ctx', [(d, d ^ step) for d in range(BLOCKS)])  7.56 us
  transfers between devices with their start and end apart: 12, of which 7 were waited for; matrix products, arithmetic and copies ran while one was open for 1% of the time, Pallas kernels for 22%

profile of v6, /device:TPU:1, one launch (start us, length us, event | category | flops | bytes accessed | tf_op | source)
XLA Modules:
  0.0 134.3 jit_solution(14415097687549396428)
XLA Ops:
  0.6 2.6 %shard_map.86 = bf16[64,96,128]{2,1,0:T(8,128)(2,1)} custom-call(bf16[128,2048]{1,0:T(8,128)(2,1)} %query_ref.2, bf16[128,2048]{1,0:T(8,128)(2,1)} %key_ref.3, bf16[128,2048]{1,0:T(8,128)(2,1)} %value_ref.3), custom_call_target="tpu_custom_call" | custom-call | flops 1000 | bytes 3145728 | tf_op jit(solution)/shard_map/pallas_call | solution.py:72
  3.3 0.0 copy-start.4
  3.3 0.0 copy-start
  3.3 0.0 copy-start.1
  3.3 13.1 %all-to-all-start = ((bf16[64,96,128]{2,1,0:T(8,128)(2,1)}), bf16[64,96,128]{2,1,0:T(8,128)(2,1)S(1)}, u32[]{:S(2)}, u32[]{:S(2)}) async-start(bf16[64,96,128]{2,1,0:T(8,128)(2,1)} %shard_map.86), calls=%async_computation | async-start | bytes 3145728 | tf_op jit(solution)/shard_map/all_to_all | solution.py:469
  16.4 0.0 copy-done.4
  16.5 0.1 copy.10.decay_ref
  16.6 0.0 copy-done
  16.6 0.0 copy-done.1
  16.6 1.0 shard_map.87.mine_ref
  17.6 0.5 collective-permute-start
  18.2 0.1 pad_add_fusion.place_ref
  18.2 1.5 %collective-permute-done.other_ref.sibling_ref = bf16[2096,128]{1,0:T(8,128)(2,1)S(1)} collective-permute-done((bf16[2096,128]{1,0:T(8,128)(2,1)S(1)}, bf16[2096,128]{1,0:T(8,128)(2,1)S(1)}, u32[]{:S(2)}, u32[]{:S(2)}) %collective-permute-start) | collective-permute-done | bytes 536608 | tf_op jit(solution)/shard_map/ppermute | solution.py:473
  19.7 1.5 %shard_map.88 = bf16[64,24,128]{2,1,0:T(8,128)(2,1)} custom-call(s32[2]{0:T(128)S(1)} %pad_add_fusion.place_ref, bf16[2096,128]{1,0:T(8,128)(2,1)S(1)} %shard_map.87.mine_ref, bf16[2096,128]{1,0:T(8,128)(2,1)S(1)} %collective-permute-done.other_ref.sibling_ref), custom_call_target="tpu_custom_call" | custom-call | flops 10000000 | bytes 1466376 | tf_op jit(solution)/shard_map/pallas_call | solution.py:72
  21.2 35.0 %all-to-all-done.packed_ref = bf16[64,96,128]{2,1,0:T(8,128)(2,1)S(1)} async-done(((bf16[64,96,128]{2,1,0:T(8,128)(2,1)}), bf16[64,96,128]{2,1,0:T(8,128)(2,1)S(1)}, u32[]{:S(2)}, u32[]{:S(2)}) %all-to-all-start) | async-done | bytes 1572896 | tf_op jit(solution)/shard_map/all_to_all | solution.py:469
  56.2 0.9 slice.9
  57.1 0.9 slice.10
  58.0 0.2 collective-permute-start.2
  58.1 0.4 collective-permute-start.1
  58.5 1.2 collective-permute-start.3
  59.7 5.6 %all-to-all-start.1 = ((bf16[64,24,128]{2,1,0:T(8,128)(2,1)}), bf16[64,24,128]{2,1,0:T(8,128)(2,1)S(1)}, u32[]{:S(2)}, u32[]{:S(2)}) async-start(bf16[64,24,128]{2,1,0:T(8,128)(2,1)} %shard_map.88), calls=%async_computation.1 | async-start | bytes 786432 | tf_op jit(solution)/shard_map/all_to_all | solution.py:469
  65.3 0.0 collective-permute-done.2.late_ref
  65.3 0.0 collective-permute-done.1.early_ref.sibling_ref
  65.3 6.5 %shard_map.89 = (f32[1024,128]{1,0:T(8,128)}, f32[1024,256]{1,0:T(8,128)}, f32[8,128]{1,0:T(8,128)S(1)}) custom-call(s32[2]{0:T(128)S(1)} %pad_add_fusion.place_ref, bf16[64,96,128]{2,1,0:T(8,128)(2,1)S(1)} %all-to-all-done.packed_ref, bf16[32,64,128]{2,1,0:T(8,128)(2,1)} %collective-permute-done.1.early_ref.sibling_ref, ...), custom_call_target="tpu_custom_call" | custom-call | tf_op jit(solution)/shard_map/pallas_call | solution.py:72
  71.8 2.1 %collective-permute-done.3.across_ref = bf16[32,64,128]{2,1,0:T(8,128)(2,1)} collective-permute-done((bf16[32,64,128]{2,1,0:T(8,128)(2,1)}, bf16[32,64,128]{2,1,0:T(8,128)(2,1)}, u32[]{:S(2)}, u32[]{:S(2)}) %collective-permute-start.3) | collective-permute-done | bytes 524320 | tf_op jit(solution)/shard_map/ppermute | solution.py:473
  73.9 2.0 %collective-permute-start.4 = (bf16[32,64,128]{2,1,0:T(8,128)(2,1)}, bf16[32,64,128]{2,1,0:T(8,128)(2,1)S(1)}, u32[]{:S(2)}, u32[]{:S(2)}) collective-permute-start(bf16[32,64,128]{2,1,0:T(8,128)(2,1)} %collective-permute-done.3.across_ref), channel_id=1, source_target_pairs={{0,4},{4,0},{8,12},{12,8},{16,20},{20,16},{24,28},{28,24},{32,36},... | collective-permute-start | bytes 1572872 | tf_op jit(solution)/shard_map/ppermute | solution.py:473
  75.9 2.1 %collective-permute-start.5 = (bf16[32,64,128]{2,1,0:T(8,128)(2,1)}, bf16[32,64,128]{2,1,0:T(8,128)(2,1)}, u32[]{:S(2)}, u32[]{:S(2)}) collective-permute-start(bf16[32,64,128]{2,1,0:T(8,128)(2,1)} %slice.10), channel_id=1, source_target_pairs={{0,64},{4,68},{8,72},{12,76},{16,80},{20,84},{24,88},{28,92},{32,9... | collective-permute-start | bytes 1572872 | tf_op jit(solution)/shard_map/ppermute | solution.py:473
  78.0 0.0 collective-permute-done.4.diagonal_ref
  78.1 9.1 %shard_map.90 = (f32[1024,128]{1,0:T(8,128)}, f32[1024,256]{1,0:T(8,128)}, bf16[32,32,128]{2,1,0:T(8,128)(2,1)}, f32[8,128]{1,0:T(8,128)S(1)}) custom-call(s32[2]{0:T(128)S(1)} %pad_add_fusion.place_ref, bf16[64,96,128]{2,1,0:T(8,128)(2,1)S(1)} %all-to-all-done.packed_ref, bf16[32,64,128]{2,1,0:T(8,128)(2,1)} %collective-permute-done.1.early_ref.sibling_ref, ...), custom_call_target="tpu_custom_call" | custom-call | tf_op jit(solution)/shard_map/pallas_call | solution.py:72
  87.2 0.0 all-to-all-done.1.moved_ref
  87.2 3.4 %collective-permute-done.5.across_ref = bf16[32,64,128]{2,1,0:T(8,128)(2,1)} collective-permute-done((bf16[32,64,128]{2,1,0:T(8,128)(2,1)}, bf16[32,64,128]{2,1,0:T(8,128)(2,1)}, u32[]{:S(2)}, u32[]{:S(2)}) %collective-permute-start.5) | collective-permute-done | bytes 524320 | tf_op jit(solution)/shard_map/ppermute | solution.py:473
  90.7 0.6 collective-permute-start.7
  91.2 0.9 shard_map.91
  92.1 5.9 %all-to-all-start.2 = ((bf16[64,16,128]{2,1,0:T(8,128)(2,1)}), bf16[64,16,128]{2,1,0:T(8,128)(2,1)S(1)}, u32[]{:S(2)}, u32[]{:S(2)}) async-start(bf16[64,16,128]{2,1,0:T(8,128)(2,1)} %shard_map.91), calls=%async_computation.2 | async-start | bytes 524288 | tf_op jit(solution)/shard_map/all_to_all | solution.py:469
  98.1 0.0 collective-permute-done.7.diagonal_ref
  98.1 0.0 copy-start.2
  98.1 6.5 %shard_map.93 = bf16[64,32,128]{2,1,0:T(8,128)(2,1)} custom-call(s32[2]{0:T(128)S(1)} %pad_add_fusion.place_ref, bf16[64,96,128]{2,1,0:T(8,128)(2,1)S(1)} %all-to-all-done.packed_ref, bf16[32,64,128]{2,1,0:T(8,128)(2,1)} %collective-permute-done.5.across_ref, bf16[32,64,128]{2,1,0:T(8,128)(2,1)} %collective-permute-done.7.diagonal_ref, ...), custom_call_target="tpu_custom_call" | custom-call | tf_op jit(solution)/shard_map/pallas_call | solution.py:72
  104.6 5.5 %all-to-all-done.2 = bf16[64,16,128]{2,1,0:T(8,128)(2,1)S(1)} async-done(((bf16[64,16,128]{2,1,0:T(8,128)(2,1)}), bf16[64,16,128]{2,1,0:T(8,128)(2,1)S(1)}, u32[]{:S(2)}, u32[]{:S(2)}) %all-to-all-start.2) | async-done | bytes 262176 | tf_op jit(solution)/shard_map/all_to_all | solution.py:469
  110.1 6.0 %all-to-all-start.3 = ((bf16[64,32,128]{2,1,0:T(8,128)(2,1)}), bf16[64,32,128]{2,1,0:T(8,128)(2,1)S(1)}, u32[]{:S(2)}, u32[]{:S(2)}) async-start(bf16[64,32,128]{2,1,0:T(8,128)(2,1)} %shard_map.93), calls=%async_computation.3 | async-start | bytes 1048576 | tf_op jit(solution)/shard_map/all_to_all | solution.py:469
  116.1 0.5 collective-permute-start.6
  116.6 1.2 collective-permute-done.6.other_ref
  117.8 0.0 copy-done.2
  117.8 0.0 copy-start.3
  117.8 1.0 copy-done.3
  118.8 4.1 %shard_map.92 = bf16[128,2048]{1,0:T(8,128)(2,1)} custom-call(s32[2]{0:T(128)S(1)} %pad_add_fusion.place_ref, bf16[128,2048]{1,0:T(8,128)(2,1)S(1)} %copy-done.3, bf16[128,2048]{1,0:T(8,128)(2,1)S(1)} %copy-done, bf16[128,2048]{1,0:T(8,128)(2,1)S(1)} %copy-done.2, f32[128,16]{1,0:T(8,128)S(1)} %copy.10.decay_ref, bf16[1024,128]{1,0:T(8,128)(2,1)S(1)} %bitcast.4, ...), custom_call_target="tpu_custom_call" | custom-call | flops 200000000 | bytes 3166216 | tf_op jit(solution)/shard_map/pallas_call | solution.py:72
  122.9 0.7 slice.12.order_ref
  123.6 9.8 %all-to-all-done.3.moved_ref = bf16[64,32,128]{2,1,0:T(8,128)(2,1)S(1)} async-done(((bf16[64,32,128]{2,1,0:T(8,128)(2,1)}), bf16[64,32,128]{2,1,0:T(8,128)(2,1)S(1)}, u32[]{:S(2)}, u32[]{:S(2)}) %all-to-all-start.3) | async-done | bytes 524320 | tf_op jit(solution)/shard_map/all_to_all | solution.py:469
  133.4 0.9 shard_map.94
Async XLA Ops:
  3.3 13.2 %copy-start.4 = (f32[128,16]{0,1:T(8,128)S(1)}, f32[128,16]{0,1:T(8,128)}, u32[]{:S(2)}) copy-start(f32[128,16]{0,1:T(8,128)} %param.10) | copy-start | bytes 24580
  3.3 13.3 %copy-start = (bf16[128,2048]{1,0:T(8,128)(2,1)S(1)}, bf16[128,2048]{1,0:T(8,128)(2,1)}, u32[]{:S(2)}) copy-start(bf16[128,2048]{1,0:T(8,128)(2,1)} %key_ref.5) | copy-start | bytes 1572868
  3.3 13.3 %copy-start.1 = (bf16[128,2048]{1,0:T(8,128)(2,1)S(1)}, bf16[128,2048]{1,0:T(8,128)(2,1)}, u32[]{:S(2)}) copy-start(bf16[128,2048]{1,0:T(8,128)(2,1)} %value_ref.5) | copy-start | bytes 1572868
  3.3 52.9 %all-to-all-start = ((bf16[64,96,128]{2,1,0:T(8,128)(2,1)}), bf16[64,96,128]{2,1,0:T(8,128)(2,1)S(1)}, u32[]{:S(2)}, u32[]{:S(2)}) async-start(bf16[64,96,128]{2,1,0:T(8,128)(2,1)} %shard_map.86), calls=%async_computation | async-start | bytes 3145728 | tf_op jit(solution)/shard_map/all_to_all | solution.py:469
  17.6 2.1 %collective-permute-start = (bf16[2096,128]{1,0:T(8,128)(2,1)S(1)}, bf16[2096,128]{1,0:T(8,128)(2,1)S(1)}, u32[]{:S(2)}, u32[]{:S(2)}) collective-permute-start(bf16[2096,128]{1,0:T(8,128)(2,1)S(1)} %shard_map.87.mine_ref), channel_id=1, source_target_pairs={{0,4},{4,0},{8,12},{12,8},{16,20},{20,16},{24,28},{28,24},{32,36},... | collective-permute-start | bytes 1609736 | tf_op jit(solution)/shard_map/ppermute | solution.py:473
  58.0 7.3 %collective-permute-start.2 = (bf16[32,64,128]{2,1,0:T(8,128)(2,1)}, bf16[32,64,128]{2,1,0:T(8,128)(2,1)}, u32[]{:S(2)}, u32[]{:S(2)}) collective-permute-start(bf16[32,64,128]{2,1,0:T(8,128)(2,1)} %slice.10), channel_id=1, source_target_pairs={{0,4},{4,0},{8,12},{12,8},{16,20},{20,16},{24,28},{28,24},{32,36},... | collective-permute-start | bytes 1572872 | tf_op jit(solution)/shard_map/ppermute | solution.py:473
  58.1 7.2 %collective-permute-start.1 = (bf16[32,64,128]{2,1,0:T(8,128)(2,1)}, bf16[32,64,128]{2,1,0:T(8,128)(2,1)}, u32[]{:S(2)}, u32[]{:S(2)}) collective-permute-start(bf16[32,64,128]{2,1,0:T(8,128)(2,1)} %slice.9), channel_id=1, source_target_pairs={{0,4},{4,0},{8,12},{12,8},{16,20},{20,16},{24,28},{28,24},{32,36},... | collective-permute-start | bytes 1572872 | tf_op jit(solution)/shard_map/ppermute | solution.py:473
  58.5 15.4 %collective-permute-start.3 = (bf16[32,64,128]{2,1,0:T(8,128)(2,1)}, bf16[32,64,128]{2,1,0:T(8,128)(2,1)}, u32[]{:S(2)}, u32[]{:S(2)}) collective-permute-start(bf16[32,64,128]{2,1,0:T(8,128)(2,1)} %slice.9), channel_id=1, source_target_pairs={{0,64},{4,68},{8,72},{12,76},{16,80},{20,84},{24,88},{28,92},{32,9... | collective-permute-start | bytes 1572872 | tf_op jit(solution)/shard_map/ppermute | solution.py:473
  59.7 27.5 %all-to-all-start.1 = ((bf16[64,24,128]{2,1,0:T(8,128)(2,1)}), bf16[64,24,128]{2,1,0:T(8,128)(2,1)S(1)}, u32[]{:S(2)}, u32[]{:S(2)}) async-start(bf16[64,24,128]{2,1,0:T(8,128)(2,1)} %shard_map.88), calls=%async_computation.1 | async-start | bytes 786432 | tf_op jit(solution)/shard_map/all_to_all | solution.py:469
  73.9 4.2 %collective-permute-start.4 = (bf16[32,64,128]{2,1,0:T(8,128)(2,1)}, bf16[32,64,128]{2,1,0:T(8,128)(2,1)S(1)}, u32[]{:S(2)}, u32[]{:S(2)}) collective-permute-start(bf16[32,64,128]{2,1,0:T(8,128)(2,1)} %collective-permute-done.3.across_ref), channel_id=1, source_target_pairs={{0,4},{4,0},{8,12},{12,8},{16,20},{20,16},{24,28},{28,24},{32,36},... | collective-permute-start | bytes 1572872 | tf_op jit(solution)/shard_map/ppermute | solution.py:473
  75.9 14.7 %collective-permute-start.5 = (bf16[32,64,128]{2,1,0:T(8,128)(2,1)}, bf16[32,64,128]{2,1,0:T(8,128)(2,1)}, u32[]{:S(2)}, u32[]{:S(2)}) collective-permute-start(bf16[32,64,128]{2,1,0:T(8,128)(2,1)} %slice.10), channel_id=1, source_target_pairs={{0,64},{4,68},{8,72},{12,76},{16,80},{20,84},{24,88},{28,92},{32,9... | collective-permute-start | bytes 1572872 | tf_op jit(solution)/shard_map/ppermute | solution.py:473
  90.7 7.4 %collective-permute-start.7 = (bf16[32,64,128]{2,1,0:T(8,128)(2,1)}, bf16[32,64,128]{2,1,0:T(8,128)(2,1)}, u32[]{:S(2)}, u32[]{:S(2)}) collective-permute-start(bf16[32,64,128]{2,1,0:T(8,128)(2,1)} %collective-permute-done.5.across_ref), channel_id=1, source_target_pairs={{0,4},{4,0},{8,12},{12,8},{16,20},{20,16},{24,28},{28,24},{32,36},... | collective-permute-start | bytes 1572872 | tf_op jit(solution)/shard_map/ppermute | solution.py:473
  92.1 17.9 %all-to-all-start.2 = ((bf16[64,16,128]{2,1,0:T(8,128)(2,1)}), bf16[64,16,128]{2,1,0:T(8,128)(2,1)S(1)}, u32[]{:S(2)}, u32[]{:S(2)}) async-start(bf16[64,16,128]{2,1,0:T(8,128)(2,1)} %shard_map.91), calls=%async_computation.2 | async-start | bytes 524288 | tf_op jit(solution)/shard_map/all_to_all | solution.py:469
  98.1 19.7 %copy-start.2 = (bf16[128,2048]{1,0:T(8,128)(2,1)S(1)}, bf16[128,2048]{1,0:T(8,128)(2,1)}, u32[]{:S(2)}) copy-start(bf16[128,2048]{1,0:T(8,128)(2,1)} %value_ref.5) | copy-start | bytes 1572868
  110.1 23.4 %all-to-all-start.3 = ((bf16[64,32,128]{2,1,0:T(8,128)(2,1)}), bf16[64,32,128]{2,1,0:T(8,128)(2,1)S(1)}, u32[]{:S(2)}, u32[]{:S(2)}) async-start(bf16[64,32,128]{2,1,0:T(8,128)(2,1)} %shard_map.93), calls=%async_computation.3 | async-start | bytes 1048576 | tf_op jit(solution)/shard_map/all_to_all | solution.py:469
  116.1 1.7 %collective-permute-start.6 = (bf16[1024,128]{1,0:T(8,128)(2,1)S(1)}, bf16[1024,128]{1,0:T(8,128)(2,1)S(1)}, u32[]{:S(2)}, u32[]{:S(2)}) collective-permute-start(bf16[1024,128]{1,0:T(8,128)(2,1)S(1)} %bitcast.3), channel_id=1, source_target_pairs={{0,4},{4,0},{8,12},{12,8},{16,20},{20,16},{24,28},{28,24},{32,36},... | collective-permute-start | bytes 786440 | tf_op jit(solution)/shard_map/ppermute | solution.py:473
  117.8 1.0 copy-start.3

commit v7 on v6

--- a/solution.py
+++ b/solution.py
@@ -279,26 +279,21 @@
 
 def first_kernel(
     place_ref, packed_ref, early_ref, late_ref, best_out, total_out, token_ref,
-    kv_ref, bias_ref, best_ref, total_ref, score_ref, kv_sems, out_sems,
+    bias_ref, best_ref, total_ref, score_ref, out_sems,
 ):
-    copies = start_copies((early_ref, late_ref), (kv_ref.at[0], kv_ref.at[1]), kv_sems)
     fill_bias(place_ref, bias_ref, (0, 1))
 
     def part(slot, key_tile, from_end):
         if slot == 0:
             return load_part(packed_ref, key_tile, from_end)
-        return load_part(kv_ref.at[key_tile // HALF_TILES], key_tile % HALF_TILES, from_end)
+        return load_part((early_ref, late_ref)[key_tile // HALF_TILES], key_tile % HALF_TILES, from_end)
 
     work = Attention(
         LATE, range(TILES), (0, 1), packed_ref, part, bias_ref, best_ref, total_ref, score_ref
     )
-    for query_tile in LATE:
-        work.find_best(query_tile, (0,))
-    for copy in copies:
-        copy.wait()
     outward, sent = [], 0
     for query_tile in LATE:
-        work.find_best(query_tile, (1,))
+        work.find_best(query_tile, (0, 1))
         work.add_up(query_tile)
         if query_tile >= TILES - 2:
             done = work.here(query_tile).stop
@@ -320,19 +315,19 @@
     kv_ref, bias_ref, best_ref, total_ref, score_ref, best2_ref, total2_ref, score2_ref, final_ref,
     kv_sems, out_sems, final_sem,
 ):
-    copies = start_copies((across_ref, sibling_ref), (kv_ref.at[1], kv_ref.at[0]), kv_sems)
+    copies = start_copies((across_ref,), (kv_ref,), kv_sems)
     fill_bias(place_ref, bias_ref, (0, 1, 2, 3))
 
     def part(slot, key_tile, from_end):
         if slot == 0:
             return load_part(packed_ref, key_tile, from_end)
-        return load_part(diagonal_ref if slot == 3 else kv_ref.at[slot - 1], key_tile, from_end)
+        return load_part((sibling_ref, kv_ref, diagonal_ref)[slot - 1], key_tile, from_end)
 
     early = Attention(
         EARLY, EARLY, (0, 1, 2, 3), packed_ref, part, bias_ref, best2_ref, total2_ref, score2_ref
     )
     for query_tile in EARLY:
-        early.find_best(query_tile, (0,))
+        early.find_best(query_tile, (0, 1))
     late = Attention(
         LATE, EARLY, (2, 3), packed_ref, part, bias_ref, best_ref, total_ref, score_ref
     )
@@ -343,7 +338,7 @@
         late.add_up(query_tile)
     outward = start_copies((best_ref, total_ref), (best_out, total_out), out_sems)
     for query_tile in EARLY:
-        early.find_best(query_tile, (1, 2, 3))
+        early.find_best(query_tile, (2, 3))
         early.add_up(query_tile)
         final_ref[tile_blocks(query_tile)] = ratio(total2_ref[early.here(query_tile), :])
     copy = pltpu.make_async_copy(final_ref, final_out, final_sem)
@@ -360,7 +355,7 @@
     kv_ref, bias_ref, best_ref, total_ref, score_ref, bests_ref, totals_ref, final_ref,
     kv_sems, state_sems, final_sems,
 ):
-    copies = start_copies((across_ref, diagonal_ref), (kv_ref.at[0], kv_ref.at[1]), kv_sems)
+    copies = start_copies((across_ref,), (kv_ref,), kv_sems)
     half_blocks = BLOCKS // 2
     state = start_copies(
         (best_a, best_b, total_a, total_b, final_in),
@@ -370,7 +365,7 @@
     fill_bias(place_ref, bias_ref, (2, 3))
 
     def part(slot, key_tile, from_end):
-        return load_part(kv_ref.at[slot], key_tile % HALF_TILES, from_end)
+        return load_part((kv_ref, diagonal_ref)[slot], key_tile % HALF_TILES, from_end)
 
     for copy in copies:
         copy.wait()
@@ -418,11 +413,12 @@
     return pltpu.VMEM((blocks, PIECE, HEAD_DIM), jnp.bfloat16)
 
 
-def attention_space(segments, slots):
-    return [
-        pltpu.VMEM((segments, BLOCKS // 2, 2 * PIECE, HEAD_DIM), jnp.bfloat16),
-        pltpu.VMEM((slots, TILE_ROWS, TILE_ROWS), jnp.float32),
-    ]
+def half_space():
+    return pltpu.VMEM((BLOCKS // 2, 2 * PIECE, HEAD_DIM), jnp.bfloat16)
+
+
+def bias_space(slots):
+    return pltpu.VMEM((slots, TILE_ROWS, TILE_ROWS), jnp.float32)
 
 
 def lightning_kernel(
@@ -525,9 +521,9 @@
         [*state_shapes, token_shape],
         (place, kv0, kv1a, kv1b),
         0,
-        [in_smem, in_vmem, in_hbm, in_hbm],
+        [in_smem, in_vmem, in_vmem, in_vmem],
         [in_hbm, in_hbm, in_vmem],
-        [*attention_space(2, 2), *work_space(LATE, range(TILES), 2), dma((2,)), dma((2, 2))],
+        [bias_space(2), *work_space(LATE, range(TILES), 2), dma((2, 2))],
         limit=32,
     )
     token, kv2a, kv0b = lax.optimization_barrier((token, kv2a, kv0b))
@@ -538,37 +534,40 @@
         [*state_shapes, shape((half_blocks, PIECE, HEAD_DIM), half), token_shape],
         (place, kv0, kv1a, kv2a, kv3a, token),
         0,
-        [in_smem, in_vmem, in_hbm, in_hbm, in_vmem, in_vmem],
+        [in_smem, in_vmem, in_vmem, in_hbm, in_vmem, in_vmem],
         [in_hbm, in_hbm, in_hbm, in_vmem],
         [
-            *attention_space(2, 4),
+            half_space(),
+            bias_space(4),
             *work_space(LATE, EARLY, 2),
             *work_space(EARLY, EARLY, 4),
             final_space(half_blocks),
-            dma((2,)),
+            dma((1,)),
             dma((2,)),
             dma,
         ],
         limit=40,
     )
-    token, chips, kv2b = lax.optimization_barrier((token, chips, kv2b))
+    (scanned,) = call(scan_kernel, [shape((BLOCKS, SLICE, HEAD_DIM), half)], (chips,), 10**6)
+    prior = exchange(scanned)
+    prior, kv2b, token = lax.optimization_barrier((prior, kv2b, token))
+    prior = prior.reshape(HALF * HEAD_DIM, HEAD_DIM)
     kv3b = swap(kv2b, 1)
-    (scanned,) = call(scan_kernel, [shape((BLOCKS, SLICE, HEAD_DIM), half)], (chips,), 10**6)
-    prior = exchange(scanned).reshape(HALF * HEAD_DIM, HEAD_DIM)
     (attended,) = call(
         third_kernel,
         [shape((BLOCKS, PIECE, HEAD_DIM), half)],
         (place, kv0, kv2b, kv3b, best_a, total_a, best_b, total_b, first, token),
         0,
-        [in_smem, in_vmem, *[in_hbm] * 7, in_vmem],
+        [in_smem, in_vmem, in_hbm, in_vmem, *[in_hbm] * 5, in_vmem],
         [in_hbm],
         [
-            *attention_space(2, 2),
+            half_space(),
+            bias_space(2),
             *work_space(LATE, LATE, 2),
             pltpu.VMEM((2, len(LATE) * TILE_ROWS, HEAD_DIM), jnp.float32),
             pltpu.VMEM((2, len(LATE) * TILE_ROWS, 2 * HEAD_DIM), jnp.float32),
             final_space(BLOCKS),
-            dma((2,)),
+            dma((1,)),
             dma((5,)),
             dma((1 + len(LATE),)),
         ],

time: 135 us -> 141 us (1.044)
  starting transfers between devices: 38.2 us -> 41.4 us
  waiting for transfers between devices: 58.5 us -> 60.6 us
    all_to_all x4, starting transfers between devices: 30.7 us -> 35.4 us  [exchange(): return lax.all_to_all(value, 'ctx', split_axis=0, concat_axis=0, tiled=True)]
    ppermute x8, waiting for transfers between devices: 8.16 us -> 12.8 us  [swap(): return lax.ppermute(value, 'ctx', [(d, d ^ step) for d in range(BLOCKS)])]
    all_to_all x4, waiting for transfers between devices: 50.3 us -> 47.9 us  [exchange(): return lax.all_to_all(value, 'ctx', split_axis=0, concat_axis=0, tiled=True)]
    ppermute x8, starting transfers between devices: 7.56 us -> 6 us  [swap(): return lax.ppermute(value, 'ctx', [(d, d ^ step) for d in range(BLOCKS)])]
  transfers between devices with their start and end apart: 12 -> 12, of which waited for: 7 -> 8; matrix products, arithmetic and copies ran while one was open for 1% -> 1% of each run, Pallas kernels for 22% -> 17%
where the time goes in v7:
time: 141 us; the launch traced here: 140 us
  waiting for transfers between devices  60.6 us (43%)
  starting transfers between devices  41.4 us (29%)
  Pallas kernels  33.6 us (24%)
  local copies, waits for them, and re-layouts  3.54 us (3%)
    all_to_all x4, waiting for transfers between devices, exchange(): return lax.all_to_all(value, 'ctx', split_axis=0, concat_axis=0, tiled=True)  47.9 us
    all_to_all x4, starting transfers between devices, exchange(): return lax.all_to_all(value, 'ctx', split_axis=0, concat_axis=0, tiled=True)  35.4 us
    pallas_call x9, Pallas kernels, call(): pl.pallas_call(kernel, out_shape=out_shape, in_specs=[whole(space) for sp...  33.6 us
    ppermute x8, waiting for transfers between devices, swap(): return lax.ppermute(value, 'ctx', [(d, d ^ step) for d in range(BLOCKS)])  12.8 us
    ppermute x8, starting transfers between devices, swap(): return lax.ppermute(value, 'ctx', [(d, d ^ step) for d in range(BLOCKS)])  6 us
  transfers between devices with their start and end apart: 12, of which 8 were waited for; matrix products, arithmetic and copies ran while one was open for 1% of the time, Pallas kernels for 17%

profile of v7, /device:TPU:1, one launch (start us, length us, event | category | flops | bytes accessed | tf_op | source)
XLA Modules:
  0.0 140.0 jit_solution(3516784241659911226)
XLA Ops:
  0.6 2.6 %shard_map.86 = bf16[64,96,128]{2,1,0:T(8,128)(2,1)} custom-call(bf16[128,2048]{1,0:T(8,128)(2,1)} %query_ref.2, bf16[128,2048]{1,0:T(8,128)(2,1)} %key_ref.3, bf16[128,2048]{1,0:T(8,128)(2,1)} %value_ref.3), custom_call_target="tpu_custom_call" | custom-call | flops 1000 | bytes 3145728 | tf_op jit(solution)/shard_map/pallas_call | solution.py:72
  3.3 0.0 copy-start.5
  3.3 0.0 copy-start
  3.3 0.0 copy-start.1
  3.3 13.1 %all-to-all-start = ((bf16[64,96,128]{2,1,0:T(8,128)(2,1)}), bf16[64,96,128]{2,1,0:T(8,128)(2,1)S(1)}, u32[]{:S(2)}, u32[]{:S(2)}) async-start(bf16[64,96,128]{2,1,0:T(8,128)(2,1)} %shard_map.86), calls=%async_computation | async-start | bytes 3145728 | tf_op jit(solution)/shard_map/all_to_all | solution.py:465
  16.4 0.0 copy-done.5
  16.5 0.1 copy.10.decay_ref
  16.6 0.0 copy-done
  16.6 0.0 copy-done.1
  16.6 1.0 shard_map.87.mine_ref
  17.6 0.5 collective-permute-start
  18.2 0.1 pad_add_fusion.place_ref
  18.2 1.5 %collective-permute-done.other_ref.sibling_ref = bf16[2096,128]{1,0:T(8,128)(2,1)S(1)} collective-permute-done((bf16[2096,128]{1,0:T(8,128)(2,1)S(1)}, bf16[2096,128]{1,0:T(8,128)(2,1)S(1)}, u32[]{:S(2)}, u32[]{:S(2)}) %collective-permute-start) | collective-permute-done | bytes 536608 | tf_op jit(solution)/shard_map/ppermute | solution.py:469
  19.7 0.7 shard_map.88
  20.5 0.0 copy-start.3
  20.5 0.8 copy-done.3
  21.2 35.0 %all-to-all-done.packed_ref = bf16[64,96,128]{2,1,0:T(8,128)(2,1)S(1)} async-done(((bf16[64,96,128]{2,1,0:T(8,128)(2,1)}), bf16[64,96,128]{2,1,0:T(8,128)(2,1)S(1)}, u32[]{:S(2)}, u32[]{:S(2)}) %all-to-all-start) | async-done | bytes 1572896 | tf_op jit(solution)/shard_map/all_to_all | solution.py:465
  56.2 6.3 %all-to-all-start.1 = ((bf16[64,24,128]{2,1,0:T(8,128)(2,1)}), bf16[64,24,128]{2,1,0:T(8,128)(2,1)}, u32[]{:S(2)}, u32[]{:S(2)}) async-start(bf16[64,24,128]{2,1,0:T(8,128)(2,1)} %copy-done.3), calls=%async_computation.1 | async-start | bytes 786432 | tf_op jit(solution)/shard_map/all_to_all | solution.py:465
  62.5 0.1 slice.9
  62.6 0.9 slice.10
  63.5 0.5 collective-permute-start.2
  64.0 0.0 collective-permute-start.1
  64.0 1.4 collective-permute-start.3
  65.4 1.1 collective-permute-done.2.late_ref
  66.5 0.0 collective-permute-done.1.early_ref.sibling_ref
  66.5 7.1 %shard_map.90 = (f32[1024,128]{1,0:T(8,128)}, f32[1024,256]{1,0:T(8,128)}, f32[8,128]{1,0:T(8,128)S(1)}) custom-call(s32[2]{0:T(128)S(1)} %pad_add_fusion.place_ref, bf16[64,96,128]{2,1,0:T(8,128)(2,1)S(1)} %all-to-all-done.packed_ref, bf16[32,64,128]{2,1,0:T(8,128)(2,1)S(1)} %collective-permute-done.1.early_ref.sibling_ref, ...), custom_call_target="tpu_custom_call" | custom-call | tf_op jit(solution)/shard_map/pallas_call | solution.py:72
  73.5 7.3 %collective-permute-done.3.across_ref = bf16[32,64,128]{2,1,0:T(8,128)(2,1)} collective-permute-done((bf16[32,64,128]{2,1,0:T(8,128)(2,1)S(1)}, bf16[32,64,128]{2,1,0:T(8,128)(2,1)}, u32[]{:S(2)}, u32[]{:S(2)}) %collective-permute-start.3) | collective-permute-done | bytes 524320 | tf_op jit(solution)/shard_map/ppermute | solution.py:469
  80.8 1.1 collective-permute-start.5
  81.9 1.4 %collective-permute-start.4 = (bf16[32,64,128]{2,1,0:T(8,128)(2,1)}, bf16[32,64,128]{2,1,0:T(8,128)(2,1)}, u32[]{:S(2)}, u32[]{:S(2)}) collective-permute-start(bf16[32,64,128]{2,1,0:T(8,128)(2,1)} %slice.10), channel_id=1, source_target_pairs={{0,64},{4,68},{8,72},{12,76},{16,80},{20,84},{24,88},{28,92},{32,9... | collective-permute-start | bytes 1572872 | tf_op jit(solution)/shard_map/ppermute | solution.py:469
  83.4 0.0 all-to-all-done.1.moved_ref
  83.4 1.9 %shard_map.89 = bf16[64,16,128]{2,1,0:T(8,128)(2,1)} custom-call(bf16[64,24,128]{2,1,0:T(8,128)(2,1)} %all-to-all-done.1.moved_ref), custom_call_target="tpu_custom_call" | custom-call | flops 1000000 | bytes 655360 | tf_op jit(solution)/shard_map/pallas_call | solution.py:72
  85.3 8.7 %all-to-all-start.2 = ((bf16[64,16,128]{2,1,0:T(8,128)(2,1)}), bf16[64,16,128]{2,1,0:T(8,128)(2,1)S(1)}, u32[]{:S(2)}, u32[]{:S(2)}) async-start(bf16[64,16,128]{2,1,0:T(8,128)(2,1)} %shard_map.89), calls=%async_computation.2 | async-start | bytes 524288 | tf_op jit(solution)/shard_map/all_to_all | solution.py:465
  93.9 0.0 collective-permute-done.5.diagonal_ref
  93.9 8.9 %shard_map.91 = (f32[1024,128]{1,0:T(8,128)}, f32[1024,256]{1,0:T(8,128)}, bf16[32,32,128]{2,1,0:T(8,128)(2,1)}, f32[8,128]{1,0:T(8,128)S(1)}) custom-call(s32[2]{0:T(128)S(1)} %pad_add_fusion.place_ref, bf16[64,96,128]{2,1,0:T(8,128)(2,1)S(1)} %all-to-all-done.packed_ref, bf16[32,64,128]{2,1,0:T(8,128)(2,1)S(1)} %collective-permute-done.1.early_ref.sibling_ref, ...), custom_call_target="tpu_custom_call" | custom-call | tf_op jit(solution)/shard_map/pallas_call | solution.py:72
  102.9 0.0 collective-permute-done.4.across_ref
  102.9 3.0 %all-to-all-done.2 = bf16[64,16,128]{2,1,0:T(8,128)(2,1)S(1)} async-done(((bf16[64,16,128]{2,1,0:T(8,128)(2,1)}), bf16[64,16,128]{2,1,0:T(8,128)(2,1)S(1)}, u32[]{:S(2)}, u32[]{:S(2)}) %all-to-all-start.2) | async-done | bytes 262176 | tf_op jit(solution)/shard_map/all_to_all | solution.py:465
  105.9 0.4 collective-permute-start.7
  106.4 1.7 %collective-permute-done.7.diagonal_ref = bf16[32,64,128]{2,1,0:T(8,128)(2,1)S(1)} collective-permute-done((bf16[32,64,128]{2,1,0:T(8,128)(2,1)}, bf16[32,64,128]{2,1,0:T(8,128)(2,1)S(1)}, u32[]{:S(2)}, u32[]{:S(2)}) %collective-permute-start.7) | collective-permute-done | bytes 524320 | tf_op jit(solution)/shard_map/ppermute | solution.py:469
  108.1 0.0 copy-start.2
  108.1 6.3 %shard_map.93 = bf16[64,32,128]{2,1,0:T(8,128)(2,1)} custom-call(s32[2]{0:T(128)S(1)} %pad_add_fusion.place_ref, bf16[64,96,128]{2,1,0:T(8,128)(2,1)S(1)} %all-to-all-done.packed_ref, bf16[32,64,128]{2,1,0:T(8,128)(2,1)} %collective-permute-done.4.across_ref, bf16[32,64,128]{2,1,0:T(8,128)(2,1)S(1)} %collective-permute-done.7.diagonal_ref, ...), custom_call_target="tpu_custom_call" | custom-call | tf_op jit(solution)/shard_map/pallas_call | solution.py:72
  114.5 7.3 %all-to-all-start.3 = ((bf16[64,32,128]{2,1,0:T(8,128)(2,1)}), bf16[64,32,128]{2,1,0:T(8,128)(2,1)S(1)}, u32[]{:S(2)}, u32[]{:S(2)}) async-start(bf16[64,32,128]{2,1,0:T(8,128)(2,1)} %shard_map.93), calls=%async_computation.3 | async-start | bytes 1048576 | tf_op jit(solution)/shard_map/all_to_all | solution.py:465
  121.8 0.5 collective-permute-start.6
  122.4 1.2 collective-permute-done.6.other_ref
  123.5 0.0 copy-done.2
  123.5 0.0 copy-start.4
  123.5 1.0 copy-done.4
  124.6 4.1 %shard_map.92 = bf16[128,2048]{1,0:T(8,128)(2,1)} custom-call(s32[2]{0:T(128)S(1)} %pad_add_fusion.place_ref, bf16[128,2048]{1,0:T(8,128)(2,1)S(1)} %copy-done.4, bf16[128,2048]{1,0:T(8,128)(2,1)S(1)} %copy-done, bf16[128,2048]{1,0:T(8,128)(2,1)S(1)} %copy-done.2, f32[128,16]{1,0:T(8,128)S(1)} %copy.10.decay_ref, bf16[1024,128]{1,0:T(8,128)(2,1)S(1)} %bitcast.4, ...), custom_call_target="tpu_custom_call" | custom-call | flops 200000000 | bytes 3166216 | tf_op jit(solution)/shard_map/pallas_call | solution.py:72
  128.6 0.7 slice.12.order_ref
  129.3 9.8 %all-to-all-done.3.moved_ref = bf16[64,32,128]{2,1,0:T(8,128)(2,1)S(1)} async-done(((bf16[64,32,128]{2,1,0:T(8,128)(2,1)}), bf16[64,32,128]{2,1,0:T(8,128)(2,1)S(1)}, u32[]{:S(2)}, u32[]{:S(2)}) %all-to-all-start.3) | async-done | bytes 524320 | tf_op jit(solution)/shard_map/all_to_all | solution.py:465
  139.1 0.9 shard_map.94
Async XLA Ops:
  3.3 13.2 %copy-start.5 = (f32[128,16]{0,1:T(8,128)S(1)}, f32[128,16]{0,1:T(8,128)}, u32[]{:S(2)}) copy-start(f32[128,16]{0,1:T(8,128)} %param.10) | copy-start | bytes 24580
  3.3 13.3 %copy-start = (bf16[128,2048]{1,0:T(8,128)(2,1)S(1)}, bf16[128,2048]{1,0:T(8,128)(2,1)}, u32[]{:S(2)}) copy-start(bf16[128,2048]{1,0:T(8,128)(2,1)} %key_ref.5) | copy-start | bytes 1572868
  3.3 13.3 %copy-start.1 = (bf16[128,2048]{1,0:T(8,128)(2,1)S(1)}, bf16[128,2048]{1,0:T(8,128)(2,1)}, u32[]{:S(2)}) copy-start(bf16[128,2048]{1,0:T(8,128)(2,1)} %value_ref.5) | copy-start | bytes 1572868
  3.3 52.9 %all-to-all-start = ((bf16[64,96,128]{2,1,0:T(8,128)(2,1)}), bf16[64,96,128]{2,1,0:T(8,128)(2,1)S(1)}, u32[]{:S(2)}, u32[]{:S(2)}) async-start(bf16[64,96,128]{2,1,0:T(8,128)(2,1)} %shard_map.86), calls=%async_computation | async-start | bytes 3145728 | tf_op jit(solution)/shard_map/all_to_all | solution.py:465
  17.6 2.1 %collective-permute-start = (bf16[2096,128]{1,0:T(8,128)(2,1)S(1)}, bf16[2096,128]{1,0:T(8,128)(2,1)S(1)}, u32[]{:S(2)}, u32[]{:S(2)}) collective-permute-start(bf16[2096,128]{1,0:T(8,128)(2,1)S(1)} %shard_map.87.mine_ref), channel_id=1, source_target_pairs={{0,4},{4,0},{8,12},{12,8},{16,20},{20,16},{24,28},{28,24},{32,36},... | collective-permute-start | bytes 1609736 | tf_op jit(solution)/shard_map/ppermute | solution.py:469
  20.5 0.8 copy-start.3
  56.2 27.1 %all-to-all-start.1 = ((bf16[64,24,128]{2,1,0:T(8,128)(2,1)}), bf16[64,24,128]{2,1,0:T(8,128)(2,1)}, u32[]{:S(2)}, u32[]{:S(2)}) async-start(bf16[64,24,128]{2,1,0:T(8,128)(2,1)} %copy-done.3), calls=%async_computation.1 | async-start | bytes 786432 | tf_op jit(solution)/shard_map/all_to_all | solution.py:465
  63.5 3.0 %collective-permute-start.2 = (bf16[32,64,128]{2,1,0:T(8,128)(2,1)}, bf16[32,64,128]{2,1,0:T(8,128)(2,1)S(1)}, u32[]{:S(2)}, u32[]{:S(2)}) collective-permute-start(bf16[32,64,128]{2,1,0:T(8,128)(2,1)} %slice.10), channel_id=1, source_target_pairs={{0,4},{4,0},{8,12},{12,8},{16,20},{20,16},{24,28},{28,24},{32,36},... | collective-permute-start | bytes 1572872 | tf_op jit(solution)/shard_map/ppermute | solution.py:469
  64.0 2.5 %collective-permute-start.1 = (bf16[32,64,128]{2,1,0:T(8,128)(2,1)S(1)}, bf16[32,64,128]{2,1,0:T(8,128)(2,1)S(1)}, u32[]{:S(2)}, u32[]{:S(2)}) collective-permute-start(bf16[32,64,128]{2,1,0:T(8,128)(2,1)S(1)} %slice.9), channel_id=1, source_target_pairs={{0,4},{4,0},{8,12},{12,8},{16,20},{20,16},{24,28},{28,24},{32,36},... | collective-permute-start | bytes 1572872 | tf_op jit(solution)/shard_map/ppermute | solution.py:469
  64.0 16.8 %collective-permute-start.3 = (bf16[32,64,128]{2,1,0:T(8,128)(2,1)S(1)}, bf16[32,64,128]{2,1,0:T(8,128)(2,1)}, u32[]{:S(2)}, u32[]{:S(2)}) collective-permute-start(bf16[32,64,128]{2,1,0:T(8,128)(2,1)S(1)} %slice.9), channel_id=1, source_target_pairs={{0,64},{4,68},{8,72},{12,76},{16,80},{20,84},{24,88},{28,92},{32,9... | collective-permute-start | bytes 1572872 | tf_op jit(solution)/shard_map/ppermute | solution.py:469
  80.8 13.1 %collective-permute-start.5 = (bf16[32,64,128]{2,1,0:T(8,128)(2,1)}, bf16[32,64,128]{2,1,0:T(8,128)(2,1)}, u32[]{:S(2)}, u32[]{:S(2)}) collective-permute-start(bf16[32,64,128]{2,1,0:T(8,128)(2,1)} %collective-permute-done.3.across_ref), channel_id=1, source_target_pairs={{0,4},{4,0},{8,12},{12,8},{16,20},{20,16},{24,28},{28,24},{32,36},... | collective-permute-start | bytes 1572872 | tf_op jit(solution)/shard_map/ppermute | solution.py:469
  81.9 21.0 %collective-permute-start.4 = (bf16[32,64,128]{2,1,0:T(8,128)(2,1)}, bf16[32,64,128]{2,1,0:T(8,128)(2,1)}, u32[]{:S(2)}, u32[]{:S(2)}) collective-permute-start(bf16[32,64,128]{2,1,0:T(8,128)(2,1)} %slice.10), channel_id=1, source_target_pairs={{0,64},{4,68},{8,72},{12,76},{16,80},{20,84},{24,88},{28,92},{32,9... | collective-permute-start | bytes 1572872 | tf_op jit(solution)/shard_map/ppermute | solution.py:469
  85.3 20.7 %all-to-all-start.2 = ((bf16[64,16,128]{2,1,0:T(8,128)(2,1)}), bf16[64,16,128]{2,1,0:T(8,128)(2,1)S(1)}, u32[]{:S(2)}, u32[]{:S(2)}) async-start(bf16[64,16,128]{2,1,0:T(8,128)(2,1)} %shard_map.89), calls=%async_computation.2 | async-start | bytes 524288 | tf_op jit(solution)/shard_map/all_to_all | solution.py:465
  105.9 2.2 %collective-permute-start.7 = (bf16[32,64,128]{2,1,0:T(8,128)(2,1)}, bf16[32,64,128]{2,1,0:T(8,128)(2,1)S(1)}, u32[]{:S(2)}, u32[]{:S(2)}) collective-permute-start(bf16[32,64,128]{2,1,0:T(8,128)(2,1)} %collective-permute-done.4.across_ref), channel_id=1, source_target_pairs={{0,4},{4,0},{8,12},{12,8},{16,20},{20,16},{24,28},{28,24},{32,36},... | collective-permute-start | bytes 1572872 | tf_op jit(solution)/shard_map/ppermute | solution.py:469
  108.1 15.4 %copy-start.2 = (bf16[128,2048]{1,0:T(8,128)(2,1)S(1)}, bf16[128,2048]{1,0:T(8,128)(2,1)}, u32[]{:S(2)}) copy-start(bf16[128,2048]{1,0:T(8,128)(2,1)} %value_ref.5) | copy-start | bytes 1572868
  114.5 24.7 %all-to-all-start.3 = ((bf16[64,32,128]{2,1,0:T(8,128)(2,1)}), bf16[64,32,128]{2,1,0:T(8,128)(2,1)S(1)}, u32[]{:S(2)}, u32[]{:S(2)}) async-start(bf16[64,32,128]{2,1,0:T(8,128)(2,1)} %shard_map.93), calls=%async_computation.3 | async-start | bytes 1048576 | tf_op jit(solution)/shard_map/all_to_all | solution.py:465
  121.8 1.7 %collective-permute-start.6 = (bf16[1024,128]{1,0:T(8,128)(2,1)S(1)}, bf16[1024,128]{1,0:T(8,128)(2,1)S(1)}, u32[]{:S(2)}, u32[]{:S(2)}) collective-permute-start(bf16[1024,128]{1,0:T(8,128)(2,1)S(1)} %bitcast.3), channel_id=1, source_target_pairs={{0,4},{4,0},{8,12},{12,8},{16,20},{20,16},{24,28},{28,24},{32,36},... | collective-permute-start | bytes 786440 | tf_op jit(solution)/shard_map/ppermute | solution.py:469
  123.5 1.0 copy-start.4

commit v8 on v6

--- a/solution.py
+++ b/solution.py
@@ -355,13 +355,16 @@
 
 
 def third_kernel(
-    place_ref, packed_ref, across_ref, diagonal_ref, best_a, total_a, best_b, total_b, final_in, order_ref,
-    out_ref,
+    place_ref, packed_ref, across1_ref, across2_ref, diagonal1_ref, diagonal2_ref, best_a, total_a, best_b, total_b,
+    final_in, order_ref, out_ref,
     kv_ref, bias_ref, best_ref, total_ref, score_ref, bests_ref, totals_ref, final_ref,
     kv_sems, state_sems, final_sems,
 ):
-    copies = start_copies((across_ref, diagonal_ref), (kv_ref.at[0], kv_ref.at[1]), kv_sems)
     half_blocks = BLOCKS // 2
+    middle = half_blocks // 2
+    copies = start_copies(
+        (across1_ref, across2_ref), (kv_ref.at[0:middle], kv_ref.at[middle:half_blocks]), kv_sems
+    )
     state = start_copies(
         (best_a, best_b, total_a, total_b, final_in),
         (bests_ref.at[0], bests_ref.at[1], totals_ref.at[0], totals_ref.at[1], final_ref.at[0:half_blocks]),
@@ -370,7 +373,11 @@
     fill_bias(place_ref, bias_ref, (2, 3))
 
     def part(slot, key_tile, from_end):
-        return load_part(kv_ref.at[slot], key_tile % HALF_TILES, from_end)
+        place = key_tile % HALF_TILES
+        if slot == 0:
+            return load_part(kv_ref, place, from_end)
+        diagonal = (diagonal1_ref, diagonal2_ref)[place // (HALF_TILES // 2)]
+        return load_part(diagonal, place % (HALF_TILES // 2), from_end)
 
     for copy in copies:
         copy.wait()
@@ -508,7 +515,9 @@
     kv0, chip = lax.optimization_barrier((kv0, chip))
     half_blocks = BLOCKS // 2
     kv0a, kv0 = lax.optimization_barrier((kv0[:half_blocks, PIECE:], kv0))
+    middle = half_blocks + half_blocks // 2
     kv0b = kv0[half_blocks:, PIECE:]
+    kv0c, kv0d = kv0[half_blocks:middle, PIECE:], kv0[middle:, PIECE:]
     kv2a = swap(kv0a, X_STEP)
     kv1a, kv1b = swap(kv0a, 1), swap(kv0b, 1)
     chips = exchange(chip)
@@ -530,9 +539,9 @@
         [*attention_space(2, 2), *work_space(LATE, range(TILES), 2), dma((2,)), dma((2, 2))],
         limit=32,
     )
-    token, kv2a, kv0b = lax.optimization_barrier((token, kv2a, kv0b))
+    token, kv2a, kv0c, kv0d = lax.optimization_barrier((token, kv2a, kv0c, kv0d))
     kv3a = swap(kv2a, 1)
-    kv2b = swap(kv0b, X_STEP)
+    kv2b = swap(kv0c, X_STEP), swap(kv0d, X_STEP)
     best_b, total_b, first, token = call(
         second_kernel,
         [*state_shapes, shape((half_blocks, PIECE, HEAD_DIM), half), token_shape],
@@ -551,19 +560,21 @@
         ],
         limit=40,
     )
-    token, chips, kv2b = lax.optimization_barrier((token, chips, kv2b))
-    kv3b = swap(kv2b, 1)
+    token, chips = lax.optimization_barrier((token, chips))
+    token, *kv2b = lax.optimization_barrier((token, *kv2b))
+    kv3b = [swap(part, 1) for part in kv2b]
     (scanned,) = call(scan_kernel, [shape((BLOCKS, SLICE, HEAD_DIM), half)], (chips,), 10**6)
     prior = exchange(scanned).reshape(HALF * HEAD_DIM, HEAD_DIM)
     (attended,) = call(
         third_kernel,
         [shape((BLOCKS, PIECE, HEAD_DIM), half)],
-        (place, kv0, kv2b, kv3b, best_a, total_a, best_b, total_b, first, token),
+        (place, kv0, *kv2b, *kv3b, best_a, total_a, best_b, total_b, first, token),
         0,
-        [in_smem, in_vmem, *[in_hbm] * 7, in_vmem],
+        [in_smem, in_vmem, in_hbm, in_hbm, in_vmem, in_vmem, *[in_hbm] * 5, in_vmem],
         [in_hbm],
         [
-            *attention_space(2, 2),
+            pltpu.VMEM((half_blocks, 2 * PIECE, HEAD_DIM), half),
+            pltpu.VMEM((2, TILE_ROWS, TILE_ROWS), jnp.float32),
             *work_space(LATE, LATE, 2),
             pltpu.VMEM((2, len(LATE) * TILE_ROWS, HEAD_DIM), jnp.float32),
             pltpu.VMEM((2, len(LATE) * TILE_ROWS, 2 * HEAD_DIM), jnp.float32),

time: 135 us -> 133 us (0.985)
  waiting for transfers between devices: 58.5 us -> 53.8 us
  starting transfers between devices: 38.2 us -> 40.7 us
    ppermute x8 -> x10, waiting for transfers between devices: 8.16 us -> 5.53 us  [swap(): return lax.ppermute(value, 'ctx', [(d, d ^ step) for d in range(BLOCKS)])]
    all_to_all x4, starting transfers between devices: 30.7 us -> 33 us  [exchange(): return lax.all_to_all(value, 'ctx', split_axis=0, concat_axis=0, tiled=True)]
    all_to_all x4, waiting for transfers between devices: 50.3 us -> 48.3 us  [exchange(): return lax.all_to_all(value, 'ctx', split_axis=0, concat_axis=0, tiled=True)]
    ppermute x8 -> x10, starting transfers between devices: 7.56 us -> 7.65 us  [swap(): return lax.ppermute(value, 'ctx', [(d, d ^ step) for d in range(BLOCKS)])]
  transfers between devices with their start and end apart: 12 -> 14, of which waited for: 7 -> 8; matrix products, arithmetic and copies ran while one was open for 1% -> 1% of each run, Pallas kernels for 22% -> 22%
where the time goes in v8:
time: 133 us
  waiting for transfers between devices  53.8 us (40%)
  starting transfers between devices  40.7 us (31%)
  Pallas kernels  32.9 us (25%)
  local copies, waits for them, and re-layouts  4.45 us (3%)
    all_to_all x4, waiting for transfers between devices, exchange(): return lax.all_to_all(value, 'ctx', split_axis=0, concat_axis=0, tiled=True)  48.3 us
    all_to_all x4, starting transfers between devices, exchange(): return lax.all_to_all(value, 'ctx', split_axis=0, concat_axis=0, tiled=True)  33 us
    pallas_call x9, Pallas kernels, call(): pl.pallas_call(kernel, out_shape=out_shape, in_specs=[whole(space) for sp...  32.9 us
    ppermute x10, starting transfers between devices, swap(): return lax.ppermute(value, 'ctx', [(d, d ^ step) for d in range(BLOCKS)])  7.65 us
    ppermute x10, waiting for transfers between devices, swap(): return lax.ppermute(value, 'ctx', [(d, d ^ step) for d in range(BLOCKS)])  5.53 us
  transfers between devices with their start and end apart: 14, of which 8 were waited for; matrix products, arithmetic and copies ran while one was open for 1% of the time, Pallas kernels for 22%

profile of v8, /device:TPU:1, one launch (start us, length us, event | category | flops | bytes accessed | tf_op | source)
XLA Modules:
  0.0 132.7 jit_solution(14291686067817359666)
XLA Ops:
  0.6 2.6 %shard_map.86 = bf16[64,96,128]{2,1,0:T(8,128)(2,1)} custom-call(bf16[128,2048]{1,0:T(8,128)(2,1)} %query_ref.2, bf16[128,2048]{1,0:T(8,128)(2,1)} %key_ref.3, bf16[128,2048]{1,0:T(8,128)(2,1)} %value_ref.3), custom_call_target="tpu_custom_call" | custom-call | flops 1000 | bytes 3145728 | tf_op jit(solution)/shard_map/pallas_call | solution.py:72
  3.3 0.0 copy-start.4
  3.3 0.0 copy-start
  3.3 0.0 copy-start.1
  3.3 13.1 %all-to-all-start = ((bf16[64,96,128]{2,1,0:T(8,128)(2,1)}), bf16[64,96,128]{2,1,0:T(8,128)(2,1)S(1)}, u32[]{:S(2)}, u32[]{:S(2)}) async-start(bf16[64,96,128]{2,1,0:T(8,128)(2,1)} %shard_map.86), calls=%async_computation | async-start | bytes 3145728 | tf_op jit(solution)/shard_map/all_to_all | solution.py:476
  16.5 0.0 copy-done.4
  16.5 0.1 copy.10.decay_ref
  16.6 0.0 copy-done
  16.6 0.0 copy-done.1
  16.6 1.0 shard_map.87.mine_ref
  17.6 0.5 collective-permute-start
  18.2 0.1 pad_add_fusion.place_ref
  18.2 1.5 %collective-permute-done.other_ref.sibling_ref = bf16[2096,128]{1,0:T(8,128)(2,1)S(1)} collective-permute-done((bf16[2096,128]{1,0:T(8,128)(2,1)S(1)}, bf16[2096,128]{1,0:T(8,128)(2,1)S(1)}, u32[]{:S(2)}, u32[]{:S(2)}) %collective-permute-start) | collective-permute-done | bytes 536608 | tf_op jit(solution)/shard_map/ppermute | solution.py:480
  19.7 1.5 %shard_map.88 = bf16[64,24,128]{2,1,0:T(8,128)(2,1)} custom-call(s32[2]{0:T(128)S(1)} %pad_add_fusion.place_ref, bf16[2096,128]{1,0:T(8,128)(2,1)S(1)} %shard_map.87.mine_ref, bf16[2096,128]{1,0:T(8,128)(2,1)S(1)} %collective-permute-done.other_ref.sibling_ref), custom_call_target="tpu_custom_call" | custom-call | flops 10000000 | bytes 1466376 | tf_op jit(solution)/shard_map/pallas_call | solution.py:72
  21.2 35.1 %all-to-all-done.packed_ref = bf16[64,96,128]{2,1,0:T(8,128)(2,1)S(1)} async-done(((bf16[64,96,128]{2,1,0:T(8,128)(2,1)}), bf16[64,96,128]{2,1,0:T(8,128)(2,1)S(1)}, u32[]{:S(2)}, u32[]{:S(2)}) %all-to-all-start) | async-done | bytes 1572896 | tf_op jit(solution)/shard_map/all_to_all | solution.py:476
  56.2 0.9 slice.15
  57.1 0.9 slice.16
  58.0 0.2 collective-permute-start.2
  58.1 0.4 collective-permute-start.1
  58.5 1.2 collective-permute-start.3
  59.7 5.6 %all-to-all-start.1 = ((bf16[64,24,128]{2,1,0:T(8,128)(2,1)}), bf16[64,24,128]{2,1,0:T(8,128)(2,1)S(1)}, u32[]{:S(2)}, u32[]{:S(2)}) async-start(bf16[64,24,128]{2,1,0:T(8,128)(2,1)} %shard_map.88), calls=%async_computation.1 | async-start | bytes 786432 | tf_op jit(solution)/shard_map/all_to_all | solution.py:476
  65.3 0.9 fusion
  66.2 0.0 collective-permute-done.2.late_ref
  66.2 0.0 collective-permute-done.1.early_ref.sibling_ref
  66.2 6.5 %shard_map.89 = (f32[1024,128]{1,0:T(8,128)}, f32[1024,256]{1,0:T(8,128)}, f32[8,128]{1,0:T(8,128)S(1)}) custom-call(s32[2]{0:T(128)S(1)} %pad_add_fusion.place_ref, bf16[64,96,128]{2,1,0:T(8,128)(2,1)S(1)} %all-to-all-done.packed_ref, bf16[32,64,128]{2,1,0:T(8,128)(2,1)} %collective-permute-done.1.early_ref.sibling_ref, ...), custom_call_target="tpu_custom_call" | custom-call | tf_op jit(solution)/shard_map/pallas_call | solution.py:72
  72.7 1.2 collective-permute-done.3.across_ref
  73.9 2.0 %collective-permute-start.4 = (bf16[32,64,128]{2,1,0:T(8,128)(2,1)}, bf16[32,64,128]{2,1,0:T(8,128)(2,1)S(1)}, u32[]{:S(2)}, u32[]{:S(2)}) collective-permute-start(bf16[32,64,128]{2,1,0:T(8,128)(2,1)} %collective-permute-done.3.across_ref), channel_id=1, source_target_pairs={{0,4},{4,0},{8,12},{12,8},{16,20},{20,16},{24,28},{28,24},{32,36},... | collective-permute-start | bytes 1572872 | tf_op jit(solution)/shard_map/ppermute | solution.py:480
  75.9 2.1 %collective-permute-start.6 = (bf16[16,64,128]{2,1,0:T(8,128)(2,1)}, bf16[16,64,128]{2,1,0:T(8,128)(2,1)}, u32[]{:S(2)}, u32[]{:S(2)}) collective-permute-start(bf16[16,64,128]{2,1,0:T(8,128)(2,1)} %get-tuple-element.34), channel_id=1, source_target_pairs={{0,64},{4,68},{8,72},{12,76},{16,80},{20,84},{24,88},{28,92},{32,9... | collective-permute-start | bytes 786440 | tf_op jit(solution)/shard_map/ppermute | solution.py:480
  78.1 0.0 collective-permute-start.7
  78.1 0.0 collective-permute-done.4.diagonal_ref
  78.1 9.1 %shard_map.90 = (f32[1024,128]{1,0:T(8,128)}, f32[1024,256]{1,0:T(8,128)}, bf16[32,32,128]{2,1,0:T(8,128)(2,1)}, f32[8,128]{1,0:T(8,128)S(1)}) custom-call(s32[2]{0:T(128)S(1)} %pad_add_fusion.place_ref, bf16[64,96,128]{2,1,0:T(8,128)(2,1)S(1)} %all-to-all-done.packed_ref, bf16[32,64,128]{2,1,0:T(8,128)(2,1)} %collective-permute-done.1.early_ref.sibling_ref, ...), custom_call_target="tpu_custom_call" | custom-call | tf_op jit(solution)/shard_map/pallas_call | solution.py:72
  87.2 0.0 all-to-all-done.1.moved_ref
  87.2 0.9 shard_map.91
  88.1 7.2 %all-to-all-start.2 = ((bf16[64,16,128]{2,1,0:T(8,128)(2,1)}), bf16[64,16,128]{2,1,0:T(8,128)(2,1)S(1)}, u32[]{:S(2)}, u32[]{:S(2)}) async-start(bf16[64,16,128]{2,1,0:T(8,128)(2,1)} %shard_map.91), calls=%async_computation.2 | async-start | bytes 524288 | tf_op jit(solution)/shard_map/all_to_all | solution.py:476
  95.3 0.0 collective-permute-done.6.across1_ref
  95.3 0.0 collective-permute-done.7.across2_ref
  95.4 0.5 collective-permute-start.8
  95.9 0.1 collective-permute-start.9
  96.0 1.3 collective-permute-done.8.diagonal1_ref
  97.3 0.4 collective-permute-done.9.diagonal2_ref
  97.6 0.0 copy-start.2
  97.6 6.3 %shard_map.93 = bf16[64,32,128]{2,1,0:T(8,128)(2,1)} custom-call(s32[2]{0:T(128)S(1)} %pad_add_fusion.place_ref, bf16[64,96,128]{2,1,0:T(8,128)(2,1)S(1)} %all-to-all-done.packed_ref, bf16[16,64,128]{2,1,0:T(8,128)(2,1)} %collective-permute-done.6.across1_ref, bf16[16,64,128]{2,1,0:T(8,128)(2,1)} %collective-permute-done.7.across2_ref, ...), custom_call_target="tpu_custom_call" | custom-call | tf_op jit(solution)/shard_map/pallas_call | solution.py:72
  104.0 3.4 %all-to-all-done.2 = bf16[64,16,128]{2,1,0:T(8,128)(2,1)S(1)} async-done(((bf16[64,16,128]{2,1,0:T(8,128)(2,1)}), bf16[64,16,128]{2,1,0:T(8,128)(2,1)S(1)}, u32[]{:S(2)}, u32[]{:S(2)}) %all-to-all-start.2) | async-done | bytes 262176 | tf_op jit(solution)/shard_map/all_to_all | solution.py:476
  107.3 7.1 %all-to-all-start.3 = ((bf16[64,32,128]{2,1,0:T(8,128)(2,1)}), bf16[64,32,128]{2,1,0:T(8,128)(2,1)S(1)}, u32[]{:S(2)}, u32[]{:S(2)}) async-start(bf16[64,32,128]{2,1,0:T(8,128)(2,1)} %shard_map.93), calls=%async_computation.3 | async-start | bytes 1048576 | tf_op jit(solution)/shard_map/all_to_all | solution.py:476
  114.5 0.5 collective-permute-start.5
  115.0 1.2 collective-permute-done.5.other_ref
  116.2 0.0 copy-done.2
  116.2 0.0 copy-start.3
  116.2 1.0 copy-done.3
  117.2 4.1 %shard_map.92 = bf16[128,2048]{1,0:T(8,128)(2,1)} custom-call(s32[2]{0:T(128)S(1)} %pad_add_fusion.place_ref, bf16[128,2048]{1,0:T(8,128)(2,1)S(1)} %copy-done.3, bf16[128,2048]{1,0:T(8,128)(2,1)S(1)} %copy-done, bf16[128,2048]{1,0:T(8,128)(2,1)S(1)} %copy-done.2, f32[128,16]{1,0:T(8,128)S(1)} %copy.10.decay_ref, bf16[1024,128]{1,0:T(8,128)(2,1)S(1)} %bitcast.4, ...), custom_call_target="tpu_custom_call" | custom-call | flops 200000000 | bytes 3166216 | tf_op jit(solution)/shard_map/pallas_call | solution.py:72
  121.3 0.7 slice.20.order_ref
  122.0 9.8 %all-to-all-done.3.moved_ref = bf16[64,32,128]{2,1,0:T(8,128)(2,1)S(1)} async-done(((bf16[64,32,128]{2,1,0:T(8,128)(2,1)}), bf16[64,32,128]{2,1,0:T(8,128)(2,1)S(1)}, u32[]{:S(2)}, u32[]{:S(2)}) %all-to-all-start.3) | async-done | bytes 524320 | tf_op jit(solution)/shard_map/all_to_all | solution.py:476
  131.8 0.9 shard_map.94
Async XLA Ops:
  3.3 13.2 %copy-start.4 = (f32[128,16]{0,1:T(8,128)S(1)}, f32[128,16]{0,1:T(8,128)}, u32[]{:S(2)}) copy-start(f32[128,16]{0,1:T(8,128)} %param.10) | copy-start | bytes 24580
  3.3 13.3 %copy-start = (bf16[128,2048]{1,0:T(8,128)(2,1)S(1)}, bf16[128,2048]{1,0:T(8,128)(2,1)}, u32[]{:S(2)}) copy-start(bf16[128,2048]{1,0:T(8,128)(2,1)} %key_ref.5) | copy-start | bytes 1572868
  3.3 13.3 %copy-start.1 = (bf16[128,2048]{1,0:T(8,128)(2,1)S(1)}, bf16[128,2048]{1,0:T(8,128)(2,1)}, u32[]{:S(2)}) copy-start(bf16[128,2048]{1,0:T(8,128)(2,1)} %value_ref.5) | copy-start | bytes 1572868
  3.3 52.9 %all-to-all-start = ((bf16[64,96,128]{2,1,0:T(8,128)(2,1)}), bf16[64,96,128]{2,1,0:T(8,128)(2,1)S(1)}, u32[]{:S(2)}, u32[]{:S(2)}) async-start(bf16[64,96,128]{2,1,0:T(8,128)(2,1)} %shard_map.86), calls=%async_computation | async-start | bytes 3145728 | tf_op jit(solution)/shard_map/all_to_all | solution.py:476
  17.6 2.1 %collective-permute-start = (bf16[2096,128]{1,0:T(8,128)(2,1)S(1)}, bf16[2096,128]{1,0:T(8,128)(2,1)S(1)}, u32[]{:S(2)}, u32[]{:S(2)}) collective-permute-start(bf16[2096,128]{1,0:T(8,128)(2,1)S(1)} %shard_map.87.mine_ref), channel_id=1, source_target_pairs={{0,4},{4,0},{8,12},{12,8},{16,20},{20,16},{24,28},{28,24},{32,36},... | collective-permute-start | bytes 1609736 | tf_op jit(solution)/shard_map/ppermute | solution.py:480
  58.0 8.2 %collective-permute-start.2 = (bf16[32,64,128]{2,1,0:T(8,128)(2,1)}, bf16[32,64,128]{2,1,0:T(8,128)(2,1)}, u32[]{:S(2)}, u32[]{:S(2)}) collective-permute-start(bf16[32,64,128]{2,1,0:T(8,128)(2,1)} %slice.16), channel_id=1, source_target_pairs={{0,4},{4,0},{8,12},{12,8},{16,20},{20,16},{24,28},{28,24},{32,36},... | collective-permute-start | bytes 1572872 | tf_op jit(solution)/shard_map/ppermute | solution.py:480
  58.1 8.0 %collective-permute-start.1 = (bf16[32,64,128]{2,1,0:T(8,128)(2,1)}, bf16[32,64,128]{2,1,0:T(8,128)(2,1)}, u32[]{:S(2)}, u32[]{:S(2)}) collective-permute-start(bf16[32,64,128]{2,1,0:T(8,128)(2,1)} %slice.15), channel_id=1, source_target_pairs={{0,4},{4,0},{8,12},{12,8},{16,20},{20,16},{24,28},{28,24},{32,36},... | collective-permute-start | bytes 1572872 | tf_op jit(solution)/shard_map/ppermute | solution.py:480
  58.5 15.4 %collective-permute-start.3 = (bf16[32,64,128]{2,1,0:T(8,128)(2,1)}, bf16[32,64,128]{2,1,0:T(8,128)(2,1)}, u32[]{:S(2)}, u32[]{:S(2)}) collective-permute-start(bf16[32,64,128]{2,1,0:T(8,128)(2,1)} %slice.15), channel_id=1, source_target_pairs={{0,64},{4,68},{8,72},{12,76},{16,80},{20,84},{24,88},{28,92},{32,9... | collective-permute-start | bytes 1572872 | tf_op jit(solution)/shard_map/ppermute | solution.py:480
  59.7 27.5 %all-to-all-start.1 = ((bf16[64,24,128]{2,1,0:T(8,128)(2,1)}), bf16[64,24,128]{2,1,0:T(8,128)(2,1)S(1)}, u32[]{:S(2)}, u32[]{:S(2)}) async-start(bf16[64,24,128]{2,1,0:T(8,128)(2,1)} %shard_map.88), calls=%async_computation.1 | async-start | bytes 786432 | tf_op jit(solution)/shard_map/all_to_all | solution.py:476
  73.9 4.2 %collective-permute-start.4 = (bf16[32,64,128]{2,1,0:T(8,128)(2,1)}, bf16[32,64,128]{2,1,0:T(8,128)(2,1)S(1)}, u32[]{:S(2)}, u32[]{:S(2)}) collective-permute-start(bf16[32,64,128]{2,1,0:T(8,128)(2,1)} %collective-permute-done.3.across_ref), channel_id=1, source_target_pairs={{0,4},{4,0},{8,12},{12,8},{16,20},{20,16},{24,28},{28,24},{32,36},... | collective-permute-start | bytes 1572872 | tf_op jit(solution)/shard_map/ppermute | solution.py:480
  75.9 19.4 %collective-permute-start.6 = (bf16[16,64,128]{2,1,0:T(8,128)(2,1)}, bf16[16,64,128]{2,1,0:T(8,128)(2,1)}, u32[]{:S(2)}, u32[]{:S(2)}) collective-permute-start(bf16[16,64,128]{2,1,0:T(8,128)(2,1)} %get-tuple-element.34), channel_id=1, source_target_pairs={{0,64},{4,68},{8,72},{12,76},{16,80},{20,84},{24,88},{28,92},{32,9... | collective-permute-start | bytes 786440 | tf_op jit(solution)/shard_map/ppermute | solution.py:480
  78.1 17.3 %collective-permute-start.7 = (bf16[16,64,128]{2,1,0:T(8,128)(2,1)}, bf16[16,64,128]{2,1,0:T(8,128)(2,1)}, u32[]{:S(2)}, u32[]{:S(2)}) collective-permute-start(bf16[16,64,128]{2,1,0:T(8,128)(2,1)} %get-tuple-element.35), channel_id=1, source_target_pairs={{0,64},{4,68},{8,72},{12,76},{16,80},{20,84},{24,88},{28,92},{32,9... | collective-permute-start | bytes 786440 | tf_op jit(solution)/shard_map/ppermute | solution.py:480
  88.1 19.2 %all-to-all-start.2 = ((bf16[64,16,128]{2,1,0:T(8,128)(2,1)}), bf16[64,16,128]{2,1,0:T(8,128)(2,1)S(1)}, u32[]{:S(2)}, u32[]{:S(2)}) async-start(bf16[64,16,128]{2,1,0:T(8,128)(2,1)} %shard_map.91), calls=%async_computation.2 | async-start | bytes 524288 | tf_op jit(solution)/shard_map/all_to_all | solution.py:476
  95.4 1.9 %collective-permute-start.8 = (bf16[16,64,128]{2,1,0:T(8,128)(2,1)}, bf16[16,64,128]{2,1,0:T(8,128)(2,1)S(1)}, u32[]{:S(2)}, u32[]{:S(2)}) collective-permute-start(bf16[16,64,128]{2,1,0:T(8,128)(2,1)} %collective-permute-done.6.across1_ref), channel_id=1, source_target_pairs={{0,4},{4,0},{8,12},{12,8},{16,20},{20,16},{24,28},{28,24},{32,36},... | collective-permute-start | bytes 786440 | tf_op jit(solution)/shard_map/ppermute | solution.py:480
  95.9 1.7 %collective-permute-start.9 = (bf16[16,64,128]{2,1,0:T(8,128)(2,1)}, bf16[16,64,128]{2,1,0:T(8,128)(2,1)S(1)}, u32[]{:S(2)}, u32[]{:S(2)}) collective-permute-start(bf16[16,64,128]{2,1,0:T(8,128)(2,1)} %collective-permute-done.7.across2_ref), channel_id=1, source_target_pairs={{0,4},{4,0},{8,12},{12,8},{16,20},{20,16},{24,28},{28,24},{32,36},... | collective-permute-start | bytes 786440 | tf_op jit(solution)/shard_map/ppermute | solution.py:480
  97.6 18.5 %copy-start.2 = (bf16[128,2048]{1,0:T(8,128)(2,1)S(1)}, bf16[128,2048]{1,0:T(8,128)(2,1)}, u32[]{:S(2)}) copy-start(bf16[128,2048]{1,0:T(8,128)(2,1)} %value_ref.5) | copy-start | bytes 1572868
  107.3 24.4 %all-to-all-start.3 = ((bf16[64,32,128]{2,1,0:T(8,128)(2,1)}), bf16[64,32,128]{2,1,0:T(8,128)(2,1)S(1)}, u32[]{:S(2)}, u32[]{:S(2)}) async-start(bf16[64,32,128]{2,1,0:T(8,128)(2,1)} %shard_map.93), calls=%async_computation.3 | async-start | bytes 1048576 | tf_op jit(solution)/shard_map/all_to_all | solution.py:476
  114.5 1.7 %collective-permute-start.5 = (bf16[1024,128]{1,0:T(8,128)(2,1)S(1)}, bf16[1024,128]{1,0:T(8,128)(2,1)S(1)}, u32[]{:S(2)}, u32[]{:S(2)}) collective-permute-start(bf16[1024,128]{1,0:T(8,128)(2,1)S(1)} %bitcast.3), channel_id=1, source_target_pairs={{0,4},{4,0},{8,12},{12,8},{16,20},{20,16},{24,28},{28,24},{32,36},... | collective-permute-start | bytes 786440 | tf_op jit(solution)/shard_map/ppermute | solution.py:480
  116.2 1.0 copy-start.3

commit v9 on v8

--- a/solution.py
+++ b/solution.py
@@ -315,10 +315,42 @@
 
 
 def second_kernel(
-    place_ref, packed_ref, sibling_ref, across_ref, diagonal_ref, order_ref,
-    best_out, total_out, final_out, token_ref,
-    kv_ref, bias_ref, best_ref, total_ref, score_ref, best2_ref, total2_ref, score2_ref, final_ref,
-    kv_sems, out_sems, final_sem,
+    place_ref, packed_ref, across_ref, diagonal_ref, order_ref, best_out, total_out, token_ref,
+    kv_ref, best_ref, total_ref, score_ref, kv_sems, out_sems,
+):
+    copies = start_copies((across_ref,), (kv_ref,), kv_sems)
+
+    def part(slot, key_tile, from_end):
+        return load_part((kv_ref, diagonal_ref)[slot], key_tile, from_end)
+
+    work = Attention(
+        LATE, EARLY, (0, 1), packed_ref, part, None, best_ref, total_ref, score_ref
+    )
+    for query_tile in LATE:
+        work.find_best(query_tile, (1,))
+    for copy in copies:
+        copy.wait()
+    outward, sent = [], 0
+    for query_tile in LATE:
+        work.find_best(query_tile, (0,))
+        work.add_up(query_tile)
+        if query_tile >= TILES - 2:
+            done = work.here(query_tile).stop
+            place = pl.ds(sent, done - sent)
+            outward += start_copies(
+                (best_ref.at[place, :], total_ref.at[place, :]),
+                (best_out.at[place, :], total_out.at[place, :]),
+                out_sems.at[query_tile - (TILES - 2)],
+            )
+            sent = done
+    token_ref[...] = best_ref[0:8, :]
+    for copy in outward:
+        copy.wait()
+
+
+def early_kernel(
+    place_ref, packed_ref, sibling_ref, across_ref, diagonal_ref, order_ref, final_out,
+    kv_ref, bias_ref, best_ref, total_ref, score_ref, final_ref, kv_sems, final_sem,
 ):
     copies = start_copies((across_ref, sibling_ref), (kv_ref.at[1], kv_ref.at[0]), kv_sems)
     fill_bias(place_ref, bias_ref, (0, 1, 2, 3))
@@ -328,29 +360,19 @@
             return load_part(packed_ref, key_tile, from_end)
         return load_part(diagonal_ref if slot == 3 else kv_ref.at[slot - 1], key_tile, from_end)
 
-    early = Attention(
-        EARLY, EARLY, (0, 1, 2, 3), packed_ref, part, bias_ref, best2_ref, total2_ref, score2_ref
+    work = Attention(
+        EARLY, EARLY, (0, 1, 2, 3), packed_ref, part, bias_ref, best_ref, total_ref, score_ref
     )
     for query_tile in EARLY:
-        early.find_best(query_tile, (0,))
-    late = Attention(
-        LATE, EARLY, (2, 3), packed_ref, part, bias_ref, best_ref, total_ref, score_ref
-    )
+        work.find_best(query_tile, (0,))
     for copy in copies:
         copy.wait()
-    for query_tile in LATE:
-        late.find_best(query_tile, (2, 3))
-        late.add_up(query_tile)
-    outward = start_copies((best_ref, total_ref), (best_out, total_out), out_sems)
     for query_tile in EARLY:
-        early.find_best(query_tile, (1, 2, 3))
-        early.add_up(query_tile)
-        final_ref[tile_blocks(query_tile)] = ratio(total2_ref[early.here(query_tile), :])
+        work.find_best(query_tile, (1, 2, 3))
+        work.add_up(query_tile)
+        final_ref[tile_blocks(query_tile)] = ratio(total_ref[work.here(query_tile), :])
     copy = pltpu.make_async_copy(final_ref, final_out, final_sem)
     copy.start()
-    token_ref[...] = best2_ref[0:8, :]
-    for other in outward:
-        other.wait()
     copy.wait()
 
 
@@ -542,23 +564,36 @@
     token, kv2a, kv0c, kv0d = lax.optimization_barrier((token, kv2a, kv0c, kv0d))
     kv3a = swap(kv2a, 1)
     kv2b = swap(kv0c, X_STEP), swap(kv0d, X_STEP)
-    best_b, total_b, first, token = call(
+    best_b, total_b, token = call(
         second_kernel,
-        [*state_shapes, shape((half_blocks, PIECE, HEAD_DIM), half), token_shape],
+        [*state_shapes, token_shape],
+        (place, kv0, kv2a, kv3a, token),
+        0,
+        [in_smem, in_vmem, in_hbm, in_vmem, in_vmem],
+        [in_hbm, in_hbm, in_vmem],
+        [
+            pltpu.VMEM((half_blocks, 2 * PIECE, HEAD_DIM), half),
+            *work_space(LATE, EARLY, 2),
+            dma((1,)),
+            dma((2, 2)),
+        ],
+        limit=32,
+    )
+    (first,) = call(
+        early_kernel,
+        [shape((half_blocks, PIECE, HEAD_DIM), half)],
         (place, kv0, kv1a, kv2a, kv3a, token),
         0,
         [in_smem, in_vmem, in_hbm, in_hbm, in_vmem, in_vmem],
-        [in_hbm, in_hbm, in_hbm, in_vmem],
+        [in_hbm],
         [
             *attention_space(2, 4),
-            *work_space(LATE, EARLY, 2),
             *work_space(EARLY, EARLY, 4),
             final_space(half_blocks),
             dma((2,)),
-            dma((2,)),
             dma,
         ],
-        limit=40,
+        limit=32,
     )
     token, chips = lax.optimization_barrier((token, chips))
     token, *kv2b = lax.optimization_barrier((token, *kv2b))

time: 133 us -> 135 us (1.015)
  waiting for transfers between devices: 53.8 us -> 47.7 us
  starting transfers between devices: 40.7 us -> 45 us
  Pallas kernels: 32.9 us -> 35.9 us
    all_to_all x4, starting transfers between devices: 33 us -> 37.1 us  [exchange(): return lax.all_to_all(value, 'ctx', split_axis=0, concat_axis=0, tiled=True)]
    all_to_all x4, waiting for transfers between devices: 48.3 us -> 44.9 us  [exchange(): return lax.all_to_all(value, 'ctx', split_axis=0, concat_axis=0, tiled=True)]
    pallas_call x9 -> x10, Pallas kernels: 32.9 us -> 35.9 us  [call(): pl.pallas_call(kernel, out_shape=out_shape, in_specs=[whole(space) for sp...]
    ppermute x10, waiting for transfers between devices: 5.53 us -> 2.87 us  [swap(): return lax.ppermute(value, 'ctx', [(d, d ^ step) for d in range(BLOCKS)])]
  transfers between devices with their start and end apart: 14 -> 14, of which waited for: 8 -> 5; matrix products, arithmetic and copies ran while one was open for 1% -> 1% of each run, Pallas kernels for 22% -> 24%
where the time goes in v9:
time: 135 us
  waiting for transfers between devices  47.7 us (35%)
  starting transfers between devices  45 us (33%)
  Pallas kernels  35.9 us (27%)
  local copies, waits for them, and re-layouts  5.23 us (4%)
    all_to_all x4, waiting for transfers between devices, exchange(): return lax.all_to_all(value, 'ctx', split_axis=0, concat_axis=0, tiled=True)  44.9 us
    all_to_all x4, starting transfers between devices, exchange(): return lax.all_to_all(value, 'ctx', split_axis=0, concat_axis=0, tiled=True)  37.1 us
    pallas_call x10, Pallas kernels, call(): pl.pallas_call(kernel, out_shape=out_shape, in_specs=[whole(space) for sp...  35.9 us
    ppermute x10, starting transfers between devices, swap(): return lax.ppermute(value, 'ctx', [(d, d ^ step) for d in range(BLOCKS)])  7.87 us
    ppermute x10, waiting for transfers between devices, swap(): return lax.ppermute(value, 'ctx', [(d, d ^ step) for d in range(BLOCKS)])  2.87 us
  transfers between devices with their start and end apart: 14, of which 5 were waited for; matrix products, arithmetic and copies ran while one was open for 1% of the time, Pallas kernels for 24%

profile of v9, /device:TPU:1, one launch (start us, length us, event | category | flops | bytes accessed | tf_op | source)
XLA Modules:
  0.0 134.8 jit_solution(1520934353165623480)
XLA Ops:
  0.6 2.7 %shard_map.86 = bf16[64,96,128]{2,1,0:T(8,128)(2,1)} custom-call(bf16[128,2048]{1,0:T(8,128)(2,1)} %query_ref.2, bf16[128,2048]{1,0:T(8,128)(2,1)} %key_ref.3, bf16[128,2048]{1,0:T(8,128)(2,1)} %value_ref.3), custom_call_target="tpu_custom_call" | custom-call | flops 1000 | bytes 3145728 | tf_op jit(solution)/shard_map/pallas_call | solution.py:72
  3.3 0.0 copy-start.5
  3.3 0.0 copy-start
  3.3 0.0 copy-start.1
  3.3 13.1 %all-to-all-start = ((bf16[64,96,128]{2,1,0:T(8,128)(2,1)}), bf16[64,96,128]{2,1,0:T(8,128)(2,1)S(1)}, u32[]{:S(2)}, u32[]{:S(2)}) async-start(bf16[64,96,128]{2,1,0:T(8,128)(2,1)} %shard_map.86), calls=%async_computation | async-start | bytes 3145728 | tf_op jit(solution)/shard_map/all_to_all | solution.py:498
  16.5 0.0 copy-done.5
  16.5 0.1 copy.10.decay_ref
  16.6 0.0 copy-done
  16.6 0.0 copy-done.1
  16.6 1.0 shard_map.87.mine_ref
  17.6 0.5 collective-permute-start
  18.2 0.1 pad_add_fusion.place_ref
  18.2 1.5 %collective-permute-done.other_ref.sibling_ref = bf16[2096,128]{1,0:T(8,128)(2,1)S(1)} collective-permute-done((bf16[2096,128]{1,0:T(8,128)(2,1)S(1)}, bf16[2096,128]{1,0:T(8,128)(2,1)S(1)}, u32[]{:S(2)}, u32[]{:S(2)}) %collective-permute-start) | collective-permute-done | bytes 536608 | tf_op jit(solution)/shard_map/ppermute | solution.py:502
  19.7 1.5 %shard_map.88 = bf16[64,24,128]{2,1,0:T(8,128)(2,1)} custom-call(s32[2]{0:T(128)S(1)} %pad_add_fusion.place_ref, bf16[2096,128]{1,0:T(8,128)(2,1)S(1)} %shard_map.87.mine_ref, bf16[2096,128]{1,0:T(8,128)(2,1)S(1)} %collective-permute-done.other_ref.sibling_ref), custom_call_target="tpu_custom_call" | custom-call | flops 10000000 | bytes 1466376 | tf_op jit(solution)/shard_map/pallas_call | solution.py:72
  21.2 35.0 %all-to-all-done.packed_ref = bf16[64,96,128]{2,1,0:T(8,128)(2,1)S(1)} async-done(((bf16[64,96,128]{2,1,0:T(8,128)(2,1)}), bf16[64,96,128]{2,1,0:T(8,128)(2,1)S(1)}, u32[]{:S(2)}, u32[]{:S(2)}) %all-to-all-start) | async-done | bytes 1572896 | tf_op jit(solution)/shard_map/all_to_all | solution.py:498
  56.3 0.9 slice.15
  57.1 0.9 slice.16
  58.0 0.2 collective-permute-start.2
  58.1 0.4 collective-permute-start.1
  58.5 1.2 collective-permute-start.3
  59.7 5.7 %all-to-all-start.1 = ((bf16[64,24,128]{2,1,0:T(8,128)(2,1)}), bf16[64,24,128]{2,1,0:T(8,128)(2,1)}, u32[]{:S(2)}, u32[]{:S(2)}) async-start(bf16[64,24,128]{2,1,0:T(8,128)(2,1)} %shard_map.88), calls=%async_computation.1 | async-start | bytes 786432 | tf_op jit(solution)/shard_map/all_to_all | solution.py:498
  65.5 0.9 fusion
  66.3 0.0 collective-permute-done.2.late_ref
  66.3 0.0 collective-permute-done.1.early_ref.sibling_ref
  66.3 0.0 copy-start.4
  66.3 0.8 copy-done.4
  67.1 6.5 %shard_map.89 = (f32[1024,128]{1,0:T(8,128)}, f32[1024,256]{1,0:T(8,128)}, f32[8,128]{1,0:T(8,128)S(1)}) custom-call(s32[2]{0:T(128)S(1)} %pad_add_fusion.place_ref, bf16[64,96,128]{2,1,0:T(8,128)(2,1)S(1)} %all-to-all-done.packed_ref, bf16[32,64,128]{2,1,0:T(8,128)(2,1)} %copy-done.4, bf16[32,64,128]{2,1,0:T(8,128)(2,1)} %collective-permute-done.2.late_ref), custom_call_target="tpu_custom_call" | custom-call | tf_op jit(solution)/shard_map/pallas_call | solution.py:72
  73.7 0.2 collective-permute-done.3.across_ref
  73.9 2.0 %collective-permute-start.4 = (bf16[32,64,128]{2,1,0:T(8,128)(2,1)}, bf16[32,64,128]{2,1,0:T(8,128)(2,1)S(1)}, u32[]{:S(2)}, u32[]{:S(2)}) collective-permute-start(bf16[32,64,128]{2,1,0:T(8,128)(2,1)} %collective-permute-done.3.across_ref), channel_id=1, source_target_pairs={{0,4},{4,0},{8,12},{12,8},{16,20},{20,16},{24,28},{28,24},{32,36},... | collective-permute-start | bytes 1572872 | tf_op jit(solution)/shard_map/ppermute | solution.py:502
  75.9 2.1 %collective-permute-start.6 = (bf16[16,64,128]{2,1,0:T(8,128)(2,1)}, bf16[16,64,128]{2,1,0:T(8,128)(2,1)}, u32[]{:S(2)}, u32[]{:S(2)}) collective-permute-start(bf16[16,64,128]{2,1,0:T(8,128)(2,1)} %get-tuple-element.33), channel_id=1, source_target_pairs={{0,64},{4,68},{8,72},{12,76},{16,80},{20,84},{24,88},{28,92},{32,9... | collective-permute-start | bytes 786440 | tf_op jit(solution)/shard_map/ppermute | solution.py:502
  78.1 0.0 collective-permute-start.7
  78.1 0.0 collective-permute-done.4.diagonal_ref
  78.1 4.7 %shard_map.90 = (f32[1024,128]{1,0:T(8,128)}, f32[1024,256]{1,0:T(8,128)}, f32[8,128]{1,0:T(8,128)S(1)}) custom-call(s32[2]{0:T(128)S(1)} %pad_add_fusion.place_ref, bf16[64,96,128]{2,1,0:T(8,128)(2,1)S(1)} %all-to-all-done.packed_ref, bf16[32,64,128]{2,1,0:T(8,128)(2,1)} %collective-permute-done.3.across_ref, ...), custom_call_target="tpu_custom_call" | custom-call | tf_op jit(solution)/shard_map/pallas_call | solution.py:72
  82.8 0.0 all-to-all-done.1.moved_ref
  82.8 1.9 %shard_map.91 = bf16[64,16,128]{2,1,0:T(8,128)(2,1)} custom-call(bf16[64,24,128]{2,1,0:T(8,128)(2,1)} %all-to-all-done.1.moved_ref), custom_call_target="tpu_custom_call" | custom-call | flops 1000000 | bytes 655360 | tf_op jit(solution)/shard_map/pallas_call | solution.py:72
  84.7 8.2 %all-to-all-start.2 = ((bf16[64,16,128]{2,1,0:T(8,128)(2,1)}), bf16[64,16,128]{2,1,0:T(8,128)(2,1)S(1)}, u32[]{:S(2)}, u32[]{:S(2)}) async-start(bf16[64,16,128]{2,1,0:T(8,128)(2,1)} %shard_map.91), calls=%async_computation.2 | async-start | bytes 524288 | tf_op jit(solution)/shard_map/all_to_all | solution.py:498
  92.9 0.0 collective-permute-done.6.across1_ref
  92.9 0.0 collective-permute-done.7.across2_ref
  92.9 0.5 collective-permute-start.8
  93.4 0.3 collective-permute-start.9
  93.8 6.3 %shard_map.93.final_in = bf16[32,32,128]{2,1,0:T(8,128)(2,1)} custom-call(s32[2]{0:T(128)S(1)} %pad_add_fusion.place_ref, bf16[64,96,128]{2,1,0:T(8,128)(2,1)S(1)} %all-to-all-done.packed_ref, bf16[32,64,128]{2,1,0:T(8,128)(2,1)} %copy-done.4, bf16[32,64,128]{2,1,0:T(8,128)(2,1)} %collective-permute-done.3.across_ref, ...), custom_call_target="tpu_custom_call" | custom-call | tf_op jit(solution)/shard_map/pallas_call | solution.py:72
  100.1 0.0 collective-permute-done.8.diagonal1_ref
  100.1 0.0 collective-permute-done.9.diagonal2_ref
  100.1 0.0 copy-start.2
  100.1 6.3 %shard_map.94 = bf16[64,32,128]{2,1,0:T(8,128)(2,1)} custom-call(s32[2]{0:T(128)S(1)} %pad_add_fusion.place_ref, bf16[64,96,128]{2,1,0:T(8,128)(2,1)S(1)} %all-to-all-done.packed_ref, bf16[16,64,128]{2,1,0:T(8,128)(2,1)} %collective-permute-done.6.across1_ref, bf16[16,64,128]{2,1,0:T(8,128)(2,1)} %collective-permute-done.7.across2_ref, ...), custom_call_target="tpu_custom_call" | custom-call | tf_op jit(solution)/shard_map/pallas_call | solution.py:72
  106.5 0.0 all-to-all-done.2
  106.5 10.1 %all-to-all-start.3 = ((bf16[64,32,128]{2,1,0:T(8,128)(2,1)}), bf16[64,32,128]{2,1,0:T(8,128)(2,1)S(1)}, u32[]{:S(2)}, u32[]{:S(2)}) async-start(bf16[64,32,128]{2,1,0:T(8,128)(2,1)} %shard_map.94), calls=%async_computation.3 | async-start | bytes 1048576 | tf_op jit(solution)/shard_map/all_to_all | solution.py:498
  116.5 0.5 collective-permute-start.5
  117.1 1.2 collective-permute-done.5.other_ref
  118.3 0.0 copy-done.2
  118.3 0.0 copy-start.3
  118.3 1.0 copy-done.3
  119.3 4.1 %shard_map.92 = bf16[128,2048]{1,0:T(8,128)(2,1)} custom-call(s32[2]{0:T(128)S(1)} %pad_add_fusion.place_ref, bf16[128,2048]{1,0:T(8,128)(2,1)S(1)} %copy-done.3, bf16[128,2048]{1,0:T(8,128)(2,1)S(1)} %copy-done, bf16[128,2048]{1,0:T(8,128)(2,1)S(1)} %copy-done.2, f32[128,16]{1,0:T(8,128)S(1)} %copy.10.decay_ref, bf16[1024,128]{1,0:T(8,128)(2,1)S(1)} %bitcast.4, ...), custom_call_target="tpu_custom_call" | custom-call | flops 200000000 | bytes 3166216 | tf_op jit(solution)/shard_map/pallas_call | solution.py:72
  123.4 0.7 slice.20.order_ref
  124.0 9.8 %all-to-all-done.3.moved_ref = bf16[64,32,128]{2,1,0:T(8,128)(2,1)S(1)} async-done(((bf16[64,32,128]{2,1,0:T(8,128)(2,1)}), bf16[64,32,128]{2,1,0:T(8,128)(2,1)S(1)}, u32[]{:S(2)}, u32[]{:S(2)}) %all-to-all-start.3) | async-done | bytes 524320 | tf_op jit(solution)/shard_map/all_to_all | solution.py:498
  133.9 0.9 shard_map.95
Async XLA Ops:
  3.3 13.2 %copy-start.5 = (f32[128,16]{0,1:T(8,128)S(1)}, f32[128,16]{0,1:T(8,128)}, u32[]{:S(2)}) copy-start(f32[128,16]{0,1:T(8,128)} %param.10) | copy-start | bytes 24580
  3.3 13.3 %copy-start = (bf16[128,2048]{1,0:T(8,128)(2,1)S(1)}, bf16[128,2048]{1,0:T(8,128)(2,1)}, u32[]{:S(2)}) copy-start(bf16[128,2048]{1,0:T(8,128)(2,1)} %key_ref.5) | copy-start | bytes 1572868
  3.3 13.3 %copy-start.1 = (bf16[128,2048]{1,0:T(8,128)(2,1)S(1)}, bf16[128,2048]{1,0:T(8,128)(2,1)}, u32[]{:S(2)}) copy-start(bf16[128,2048]{1,0:T(8,128)(2,1)} %value_ref.5) | copy-start | bytes 1572868
  3.3 52.9 %all-to-all-start = ((bf16[64,96,128]{2,1,0:T(8,128)(2,1)}), bf16[64,96,128]{2,1,0:T(8,128)(2,1)S(1)}, u32[]{:S(2)}, u32[]{:S(2)}) async-start(bf16[64,96,128]{2,1,0:T(8,128)(2,1)} %shard_map.86), calls=%async_computation | async-start | bytes 3145728 | tf_op jit(solution)/shard_map/all_to_all | solution.py:498
  17.6 2.1 %collective-permute-start = (bf16[2096,128]{1,0:T(8,128)(2,1)S(1)}, bf16[2096,128]{1,0:T(8,128)(2,1)S(1)}, u32[]{:S(2)}, u32[]{:S(2)}) collective-permute-start(bf16[2096,128]{1,0:T(8,128)(2,1)S(1)} %shard_map.87.mine_ref), channel_id=1, source_target_pairs={{0,4},{4,0},{8,12},{12,8},{16,20},{20,16},{24,28},{28,24},{32,36},... | collective-permute-start | bytes 1609736 | tf_op jit(solution)/shard_map/ppermute | solution.py:502
  58.0 8.3 %collective-permute-start.2 = (bf16[32,64,128]{2,1,0:T(8,128)(2,1)}, bf16[32,64,128]{2,1,0:T(8,128)(2,1)}, u32[]{:S(2)}, u32[]{:S(2)}) collective-permute-start(bf16[32,64,128]{2,1,0:T(8,128)(2,1)} %slice.16), channel_id=1, source_target_pairs={{0,4},{4,0},{8,12},{12,8},{16,20},{20,16},{24,28},{28,24},{32,36},... | collective-permute-start | bytes 1572872 | tf_op jit(solution)/shard_map/ppermute | solution.py:502
  58.1 8.2 %collective-permute-start.1 = (bf16[32,64,128]{2,1,0:T(8,128)(2,1)}, bf16[32,64,128]{2,1,0:T(8,128)(2,1)S(1)}, u32[]{:S(2)}, u32[]{:S(2)}) collective-permute-start(bf16[32,64,128]{2,1,0:T(8,128)(2,1)} %slice.15), channel_id=1, source_target_pairs={{0,4},{4,0},{8,12},{12,8},{16,20},{20,16},{24,28},{28,24},{32,36},... | collective-permute-start | bytes 1572872 | tf_op jit(solution)/shard_map/ppermute | solution.py:502
  58.5 15.4 %collective-permute-start.3 = (bf16[32,64,128]{2,1,0:T(8,128)(2,1)}, bf16[32,64,128]{2,1,0:T(8,128)(2,1)}, u32[]{:S(2)}, u32[]{:S(2)}) collective-permute-start(bf16[32,64,128]{2,1,0:T(8,128)(2,1)} %slice.15), channel_id=1, source_target_pairs={{0,64},{4,68},{8,72},{12,76},{16,80},{20,84},{24,88},{28,92},{32,9... | collective-permute-start | bytes 1572872 | tf_op jit(solution)/shard_map/ppermute | solution.py:502
  59.7 23.0 %all-to-all-start.1 = ((bf16[64,24,128]{2,1,0:T(8,128)(2,1)}), bf16[64,24,128]{2,1,0:T(8,128)(2,1)}, u32[]{:S(2)}, u32[]{:S(2)}) async-start(bf16[64,24,128]{2,1,0:T(8,128)(2,1)} %shard_map.88), calls=%async_computation.1 | async-start | bytes 786432 | tf_op jit(solution)/shard_map/all_to_all | solution.py:498
  66.3 0.8 copy-start.4
  73.9 4.2 %collective-permute-start.4 = (bf16[32,64,128]{2,1,0:T(8,128)(2,1)}, bf16[32,64,128]{2,1,0:T(8,128)(2,1)S(1)}, u32[]{:S(2)}, u32[]{:S(2)}) collective-permute-start(bf16[32,64,128]{2,1,0:T(8,128)(2,1)} %collective-permute-done.3.across_ref), channel_id=1, source_target_pairs={{0,4},{4,0},{8,12},{12,8},{16,20},{20,16},{24,28},{28,24},{32,36},... | collective-permute-start | bytes 1572872 | tf_op jit(solution)/shard_map/ppermute | solution.py:502
  75.9 16.9 %collective-permute-start.6 = (bf16[16,64,128]{2,1,0:T(8,128)(2,1)}, bf16[16,64,128]{2,1,0:T(8,128)(2,1)}, u32[]{:S(2)}, u32[]{:S(2)}) collective-permute-start(bf16[16,64,128]{2,1,0:T(8,128)(2,1)} %get-tuple-element.33), channel_id=1, source_target_pairs={{0,64},{4,68},{8,72},{12,76},{16,80},{20,84},{24,88},{28,92},{32,9... | collective-permute-start | bytes 786440 | tf_op jit(solution)/shard_map/ppermute | solution.py:502
  78.1 14.8 %collective-permute-start.7 = (bf16[16,64,128]{2,1,0:T(8,128)(2,1)}, bf16[16,64,128]{2,1,0:T(8,128)(2,1)}, u32[]{:S(2)}, u32[]{:S(2)}) collective-permute-start(bf16[16,64,128]{2,1,0:T(8,128)(2,1)} %get-tuple-element.34), channel_id=1, source_target_pairs={{0,64},{4,68},{8,72},{12,76},{16,80},{20,84},{24,88},{28,92},{32,9... | collective-permute-start | bytes 786440 | tf_op jit(solution)/shard_map/ppermute | solution.py:502
  84.7 21.8 %all-to-all-start.2 = ((bf16[64,16,128]{2,1,0:T(8,128)(2,1)}), bf16[64,16,128]{2,1,0:T(8,128)(2,1)S(1)}, u32[]{:S(2)}, u32[]{:S(2)}) async-start(bf16[64,16,128]{2,1,0:T(8,128)(2,1)} %shard_map.91), calls=%async_computation.2 | async-start | bytes 524288 | tf_op jit(solution)/shard_map/all_to_all | solution.py:498
  92.9 7.2 %collective-permute-start.8 = (bf16[16,64,128]{2,1,0:T(8,128)(2,1)}, bf16[16,64,128]{2,1,0:T(8,128)(2,1)S(1)}, u32[]{:S(2)}, u32[]{:S(2)}) collective-permute-start(bf16[16,64,128]{2,1,0:T(8,128)(2,1)} %collective-permute-done.6.across1_ref), channel_id=1, source_target_pairs={{0,4},{4,0},{8,12},{12,8},{16,20},{20,16},{24,28},{28,24},{32,36},... | collective-permute-start | bytes 786440 | tf_op jit(solution)/shard_map/ppermute | solution.py:502
  93.4 6.7 %collective-permute-start.9 = (bf16[16,64,128]{2,1,0:T(8,128)(2,1)}, bf16[16,64,128]{2,1,0:T(8,128)(2,1)S(1)}, u32[]{:S(2)}, u32[]{:S(2)}) collective-permute-start(bf16[16,64,128]{2,1,0:T(8,128)(2,1)} %collective-permute-done.7.across2_ref), channel_id=1, source_target_pairs={{0,4},{4,0},{8,12},{12,8},{16,20},{20,16},{24,28},{28,24},{32,36},... | collective-permute-start | bytes 786440 | tf_op jit(solution)/shard_map/ppermute | solution.py:502
  100.1 18.1 %copy-start.2 = (bf16[128,2048]{1,0:T(8,128)(2,1)S(1)}, bf16[128,2048]{1,0:T(8,128)(2,1)}, u32[]{:S(2)}) copy-start(bf16[128,2048]{1,0:T(8,128)(2,1)} %value_ref.5) | copy-start | bytes 1572868
  106.5 27.4 %all-to-all-start.3 = ((bf16[64,32,128]{2,1,0:T(8,128)(2,1)}), bf16[64,32,128]{2,1,0:T(8,128)(2,1)S(1)}, u32[]{:S(2)}, u32[]{:S(2)}) async-start(bf16[64,32,128]{2,1,0:T(8,128)(2,1)} %shard_map.94), calls=%async_computation.3 | async-start | bytes 1048576 | tf_op jit(solution)/shard_map/all_to_all | solution.py:498
  116.5 1.7 %collective-permute-start.5 = (bf16[1024,128]{1,0:T(8,128)(2,1)S(1)}, bf16[1024,128]{1,0:T(8,128)(2,1)S(1)}, u32[]{:S(2)}, u32[]{:S(2)}) collective-permute-start(bf16[1024,128]{1,0:T(8,128)(2,1)S(1)} %bitcast.3), channel_id=1, source_target_pairs={{0,4},{4,0},{8,12},{12,8},{16,20},{20,16},{24,28},{28,24},{32,36},... | collective-permute-start | bytes 786440 | tf_op jit(solution)/shard_map/ppermute | solution.py:502
  118.3 1.0 copy-start.3

commit v10 on v8

--- a/solution.py
+++ b/solution.py
@@ -82,19 +82,41 @@
     )(*operands)
 
 
-def pack_kernel(query_ref, key_ref, value_ref, out_ref, held_ref, semaphores):
+def pack_kernel(query_ref, key_ref, value_ref, out_ref, held_ref, packed_ref, semaphores):
     sources = (query_ref, key_ref, value_ref)
     copies = [
-        pltpu.make_async_copy(source, held_ref.at[which], semaphores.at[which])
+        pltpu.make_async_copy(source, held_ref.at[which], semaphores.at[0, which])
         for which, source in enumerate(sources)
     ]
     for copy in copies:
         copy.start()
+    outward = []
     for which, copy in enumerate(copies):
         copy.wait()
         for device in range(BLOCKS):
             head, quarter = place_of(device)
-            out_ref[device, rows(which), :] = held_ref[which, rows(quarter), columns(head)]
+            packed_ref[which, device] = held_ref[which, rows(quarter), columns(head)]
+        outward.append(
+            pltpu.make_async_copy(
+                packed_ref.at[which], out_ref.at[:, rows(which), :], semaphores.at[1, which]
+            )
+        )
+        outward[-1].start()
+    for copy in outward:
+        copy.wait()
+
+
+def slice_kernel(packed_ref, *refs):
+    outs, semaphores = refs[:-1], refs[-1]
+    half, middle = BLOCKS // 2, BLOCKS // 2 + BLOCKS // 4
+    ranges = ((0, half), (half, BLOCKS), (half, middle), (middle, BLOCKS))
+    copies = start_copies(
+        [packed_ref.at[first:last, PIECE : 3 * PIECE, :] for first, last in ranges],
+        outs,
+        semaphores,
+    )
+    for copy in copies:
+        copy.wait()
 
 
 def lower_triangle():
@@ -493,7 +515,12 @@
         (soft_query, soft_key, soft_value),
         1000,
         [pltpu.HBM] * 3,
-        scratch=(pltpu.VMEM((3, TOKENS, width), half), pltpu.SemaphoreType.DMA((3,))),
+        [pltpu.HBM],
+        (
+            pltpu.VMEM((3, TOKENS, width), half),
+            pltpu.VMEM((3, BLOCKS, PIECE, HEAD_DIM), half),
+            pltpu.SemaphoreType.DMA((2, 3)),
+        ),
     )
     kv0 = exchange(packed)
     (states,) = call(
@@ -514,10 +541,18 @@
     )
     kv0, chip = lax.optimization_barrier((kv0, chip))
     half_blocks = BLOCKS // 2
-    kv0a, kv0 = lax.optimization_barrier((kv0[:half_blocks, PIECE:], kv0))
-    middle = half_blocks + half_blocks // 2
-    kv0b = kv0[half_blocks:, PIECE:]
-    kv0c, kv0d = kv0[half_blocks:middle, PIECE:], kv0[middle:, PIECE:]
+    kv0a, kv0b, kv0c, kv0d = call(
+        slice_kernel,
+        [
+            shape((blocks, 2 * PIECE, HEAD_DIM), half)
+            for blocks in (half_blocks, half_blocks, half_blocks // 2, half_blocks // 2)
+        ],
+        (kv0,),
+        0,
+        [pltpu.VMEM],
+        [pltpu.HBM] * 4,
+        [pltpu.SemaphoreType.DMA((4,))],
+    )
     kv2a = swap(kv0a, X_STEP)
     kv1a, kv1b = swap(kv0a, 1), swap(kv0b, 1)
     chips = exchange(chip)

time: 133 us -> 132 us (level)
  local copies, waits for them, and re-layouts: 4.45 us -> 1.85 us
    slice x3 -> x0, local copies, waits for them, and re-layouts: 2.6 us -> none  [the longest x1 0.88 us: shards(): kv0c, kv0d = (kv0[half_blocks:middle, PIECE:], kv0[middle:, PIECE:])]
    pallas_call x9 -> x10, Pallas kernels: 32.9 us -> 33.8 us  [call(): pl.pallas_call(kernel, out_shape=out_shape, in_specs=[whole(space) for sp...]
where the time goes in v10:
time: 132 us; the launch traced here: 131 us
  waiting for transfers between devices  54.6 us (41%)
  starting transfers between devices  40 us (30%)
  Pallas kernels  33.8 us (26%)
  local copies, waits for them, and re-layouts  1.85 us (1%)
    all_to_all x4, waiting for transfers between devices, exchange(): return lax.all_to_all(value, 'ctx', split_axis=0, concat_axis=0, tiled=True)  48.3 us
    pallas_call x10, Pallas kernels, call(): pl.pallas_call(kernel, out_shape=out_shape, in_specs=[whole(space) for sp...  33.8 us
    all_to_all x4, starting transfers between devices, exchange(): return lax.all_to_all(value, 'ctx', split_axis=0, concat_axis=0, tiled=True)  32.1 us
    ppermute x10, starting transfers between devices, swap(): return lax.ppermute(value, 'ctx', [(d, d ^ step) for d in range(BLOCKS)])  7.87 us
    ppermute x10, waiting for transfers between devices, swap(): return lax.ppermute(value, 'ctx', [(d, d ^ step) for d in range(BLOCKS)])  6.3 us
  transfers between devices with their start and end apart: 14, of which 8 were waited for; matrix products, arithmetic and copies ran while one was open for 1% of the time, Pallas kernels for 22%

profile of v10, /device:TPU:1, one launch (start us, length us, event | category | flops | bytes accessed | tf_op | source)
XLA Modules:
  0.0 131.0 jit_solution(2853886589979012548)
XLA Ops:
  0.6 2.3 %shard_map.86 = bf16[64,96,128]{2,1,0:T(8,128)(2,1)} custom-call(bf16[128,2048]{1,0:T(8,128)(2,1)} %query_ref.2, bf16[128,2048]{1,0:T(8,128)(2,1)} %key_ref.3, bf16[128,2048]{1,0:T(8,128)(2,1)} %value_ref.3), custom_call_target="tpu_custom_call" | custom-call | flops 1000 | bytes 3145728 | tf_op jit(solution)/shard_map/pallas_call | solution.py:72
  3.0 0.0 copy-start.4
  3.0 0.0 copy-start
  3.0 0.0 copy-start.1
  3.0 13.1 %all-to-all-start = ((bf16[64,96,128]{2,1,0:T(8,128)(2,1)}), bf16[64,96,128]{2,1,0:T(8,128)(2,1)S(1)}, u32[]{:S(2)}, u32[]{:S(2)}) async-start(bf16[64,96,128]{2,1,0:T(8,128)(2,1)} %shard_map.86), calls=%async_computation | async-start | bytes 3145728 | tf_op jit(solution)/shard_map/all_to_all | solution.py:498
  16.2 0.0 copy-done.4
  16.2 0.1 copy.10.decay_ref
  16.3 0.0 copy-done
  16.3 0.0 copy-done.1
  16.3 1.0 shard_map.87.mine_ref
  17.3 0.5 collective-permute-start
  17.9 0.1 pad_add_fusion.place_ref
  17.9 1.5 %collective-permute-done.other_ref.sibling_ref = bf16[2096,128]{1,0:T(8,128)(2,1)S(1)} collective-permute-done((bf16[2096,128]{1,0:T(8,128)(2,1)S(1)}, bf16[2096,128]{1,0:T(8,128)(2,1)S(1)}, u32[]{:S(2)}, u32[]{:S(2)}) %collective-permute-start) | collective-permute-done | bytes 536608 | tf_op jit(solution)/shard_map/ppermute | solution.py:502
  19.4 1.5 %shard_map.88 = bf16[64,24,128]{2,1,0:T(8,128)(2,1)} custom-call(s32[2]{0:T(128)S(1)} %pad_add_fusion.place_ref, bf16[2096,128]{1,0:T(8,128)(2,1)S(1)} %shard_map.87.mine_ref, bf16[2096,128]{1,0:T(8,128)(2,1)S(1)} %collective-permute-done.other_ref.sibling_ref), custom_call_target="tpu_custom_call" | custom-call | flops 10000000 | bytes 1466376 | tf_op jit(solution)/shard_map/pallas_call | solution.py:72
  20.9 35.1 %all-to-all-done.packed_ref = bf16[64,96,128]{2,1,0:T(8,128)(2,1)S(1)} async-done(((bf16[64,96,128]{2,1,0:T(8,128)(2,1)}), bf16[64,96,128]{2,1,0:T(8,128)(2,1)S(1)}, u32[]{:S(2)}, u32[]{:S(2)}) %all-to-all-start) | async-done | bytes 1572896 | tf_op jit(solution)/shard_map/all_to_all | solution.py:498
  56.0 1.2 shard_map.89
  57.1 0.2 collective-permute-start.2
  57.4 0.4 collective-permute-start.1
  57.7 1.2 collective-permute-start.3
  59.0 5.5 %all-to-all-start.1 = ((bf16[64,24,128]{2,1,0:T(8,128)(2,1)}), bf16[64,24,128]{2,1,0:T(8,128)(2,1)S(1)}, u32[]{:S(2)}, u32[]{:S(2)}) async-start(bf16[64,24,128]{2,1,0:T(8,128)(2,1)} %shard_map.88), calls=%async_computation.1 | async-start | bytes 786432 | tf_op jit(solution)/shard_map/all_to_all | solution.py:498
  64.5 0.0 collective-permute-done.2.late_ref
  64.5 0.0 collective-permute-done.1.early_ref.sibling_ref
  64.5 6.5 %shard_map.90 = (f32[1024,128]{1,0:T(8,128)}, f32[1024,256]{1,0:T(8,128)}, f32[8,128]{1,0:T(8,128)S(1)}) custom-call(s32[2]{0:T(128)S(1)} %pad_add_fusion.place_ref, bf16[64,96,128]{2,1,0:T(8,128)(2,1)S(1)} %all-to-all-done.packed_ref, bf16[32,64,128]{2,1,0:T(8,128)(2,1)} %collective-permute-done.1.early_ref.sibling_ref, ...), custom_call_target="tpu_custom_call" | custom-call | tf_op jit(solution)/shard_map/pallas_call | solution.py:72
  71.0 2.0 %collective-permute-done.3.across_ref = bf16[32,64,128]{2,1,0:T(8,128)(2,1)} collective-permute-done((bf16[32,64,128]{2,1,0:T(8,128)(2,1)}, bf16[32,64,128]{2,1,0:T(8,128)(2,1)}, u32[]{:S(2)}, u32[]{:S(2)}) %collective-permute-start.3) | collective-permute-done | bytes 524320 | tf_op jit(solution)/shard_map/ppermute | solution.py:502
  73.0 2.1 %collective-permute-start.4 = (bf16[32,64,128]{2,1,0:T(8,128)(2,1)}, bf16[32,64,128]{2,1,0:T(8,128)(2,1)S(1)}, u32[]{:S(2)}, u32[]{:S(2)}) collective-permute-start(bf16[32,64,128]{2,1,0:T(8,128)(2,1)} %collective-permute-done.3.across_ref), channel_id=1, source_target_pairs={{0,4},{4,0},{8,12},{12,8},{16,20},{20,16},{24,28},{28,24},{32,36},... | collective-permute-start | bytes 1572872 | tf_op jit(solution)/shard_map/ppermute | solution.py:502
  75.2 2.1 %collective-permute-start.6 = (bf16[16,64,128]{2,1,0:T(8,128)(2,1)}, bf16[16,64,128]{2,1,0:T(8,128)(2,1)}, u32[]{:S(2)}, u32[]{:S(2)}) collective-permute-start(bf16[16,64,128]{2,1,0:T(8,128)(2,1)} %get-tuple-element.38), channel_id=1, source_target_pairs={{0,64},{4,68},{8,72},{12,76},{16,80},{20,84},{24,88},{28,92},{32,9... | collective-permute-start | bytes 786440 | tf_op jit(solution)/shard_map/ppermute | solution.py:502
  77.3 0.0 collective-permute-start.7
  77.3 0.0 collective-permute-done.4.diagonal_ref
  77.3 9.1 %shard_map.91 = (f32[1024,128]{1,0:T(8,128)}, f32[1024,256]{1,0:T(8,128)}, bf16[32,32,128]{2,1,0:T(8,128)(2,1)}, f32[8,128]{1,0:T(8,128)S(1)}) custom-call(s32[2]{0:T(128)S(1)} %pad_add_fusion.place_ref, bf16[64,96,128]{2,1,0:T(8,128)(2,1)S(1)} %all-to-all-done.packed_ref, bf16[32,64,128]{2,1,0:T(8,128)(2,1)} %collective-permute-done.1.early_ref.sibling_ref, ...), custom_call_target="tpu_custom_call" | custom-call | tf_op jit(solution)/shard_map/pallas_call | solution.py:72
  86.5 0.0 all-to-all-done.1.moved_ref
  86.5 0.9 shard_map.92
  87.4 6.3 %all-to-all-start.2 = ((bf16[64,16,128]{2,1,0:T(8,128)(2,1)}), bf16[64,16,128]{2,1,0:T(8,128)(2,1)S(1)}, u32[]{:S(2)}, u32[]{:S(2)}) async-start(bf16[64,16,128]{2,1,0:T(8,128)(2,1)} %shard_map.92), calls=%async_computation.2 | async-start | bytes 524288 | tf_op jit(solution)/shard_map/all_to_all | solution.py:498
  93.7 0.0 collective-permute-done.6.across1_ref
  93.7 0.0 collective-permute-done.7.across2_ref
  93.7 0.5 collective-permute-start.8
  94.3 0.1 collective-permute-start.9
  94.4 1.3 collective-permute-done.8.diagonal1_ref
  95.6 0.4 collective-permute-done.9.diagonal2_ref
  96.0 0.0 copy-start.2
  96.0 6.3 %shard_map.94 = bf16[64,32,128]{2,1,0:T(8,128)(2,1)} custom-call(s32[2]{0:T(128)S(1)} %pad_add_fusion.place_ref, bf16[64,96,128]{2,1,0:T(8,128)(2,1)S(1)} %all-to-all-done.packed_ref, bf16[16,64,128]{2,1,0:T(8,128)(2,1)} %collective-permute-done.6.across1_ref, bf16[16,64,128]{2,1,0:T(8,128)(2,1)} %collective-permute-done.7.across2_ref, ...), custom_call_target="tpu_custom_call" | custom-call | tf_op jit(solution)/shard_map/pallas_call | solution.py:72
  102.3 3.4 %all-to-all-done.2 = bf16[64,16,128]{2,1,0:T(8,128)(2,1)S(1)} async-done(((bf16[64,16,128]{2,1,0:T(8,128)(2,1)}), bf16[64,16,128]{2,1,0:T(8,128)(2,1)S(1)}, u32[]{:S(2)}, u32[]{:S(2)}) %all-to-all-start.2) | async-done | bytes 262176 | tf_op jit(solution)/shard_map/all_to_all | solution.py:498
  105.7 7.1 %all-to-all-start.3 = ((bf16[64,32,128]{2,1,0:T(8,128)(2,1)}), bf16[64,32,128]{2,1,0:T(8,128)(2,1)S(1)}, u32[]{:S(2)}, u32[]{:S(2)}) async-start(bf16[64,32,128]{2,1,0:T(8,128)(2,1)} %shard_map.94), calls=%async_computation.3 | async-start | bytes 1048576 | tf_op jit(solution)/shard_map/all_to_all | solution.py:498
  112.8 0.5 collective-permute-start.5
  113.4 1.2 collective-permute-done.5.other_ref
  114.5 0.0 copy-done.2
  114.5 0.0 copy-start.3
  114.5 1.0 copy-done.3
  115.6 4.1 %shard_map.93 = bf16[128,2048]{1,0:T(8,128)(2,1)} custom-call(s32[2]{0:T(128)S(1)} %pad_add_fusion.place_ref, bf16[128,2048]{1,0:T(8,128)(2,1)S(1)} %copy-done.3, bf16[128,2048]{1,0:T(8,128)(2,1)S(1)} %copy-done, bf16[128,2048]{1,0:T(8,128)(2,1)S(1)} %copy-done.2, f32[128,16]{1,0:T(8,128)S(1)} %copy.10.decay_ref, bf16[1024,128]{1,0:T(8,128)(2,1)S(1)} %bitcast.4, ...), custom_call_target="tpu_custom_call" | custom-call | flops 200000000 | bytes 3166216 | tf_op jit(solution)/shard_map/pallas_call | solution.py:72
  119.6 0.7 slice.4.order_ref
  120.3 9.8 %all-to-all-done.3.moved_ref = bf16[64,32,128]{2,1,0:T(8,128)(2,1)S(1)} async-done(((bf16[64,32,128]{2,1,0:T(8,128)(2,1)}), bf16[64,32,128]{2,1,0:T(8,128)(2,1)S(1)}, u32[]{:S(2)}, u32[]{:S(2)}) %all-to-all-start.3) | async-done | bytes 524320 | tf_op jit(solution)/shard_map/all_to_all | solution.py:498
  130.1 0.9 shard_map.95
Async XLA Ops:
  3.0 13.2 %copy-start.4 = (f32[128,16]{0,1:T(8,128)S(1)}, f32[128,16]{0,1:T(8,128)}, u32[]{:S(2)}) copy-start(f32[128,16]{0,1:T(8,128)} %param.10) | copy-start | bytes 24580
  3.0 13.3 %copy-start = (bf16[128,2048]{1,0:T(8,128)(2,1)S(1)}, bf16[128,2048]{1,0:T(8,128)(2,1)}, u32[]{:S(2)}) copy-start(bf16[128,2048]{1,0:T(8,128)(2,1)} %key_ref.5) | copy-start | bytes 1572868
  3.0 13.3 %copy-start.1 = (bf16[128,2048]{1,0:T(8,128)(2,1)S(1)}, bf16[128,2048]{1,0:T(8,128)(2,1)}, u32[]{:S(2)}) copy-start(bf16[128,2048]{1,0:T(8,128)(2,1)} %value_ref.5) | copy-start | bytes 1572868
  3.0 52.9 %all-to-all-start = ((bf16[64,96,128]{2,1,0:T(8,128)(2,1)}), bf16[64,96,128]{2,1,0:T(8,128)(2,1)S(1)}, u32[]{:S(2)}, u32[]{:S(2)}) async-start(bf16[64,96,128]{2,1,0:T(8,128)(2,1)} %shard_map.86), calls=%async_computation | async-start | bytes 3145728 | tf_op jit(solution)/shard_map/all_to_all | solution.py:498
  17.3 2.1 %collective-permute-start = (bf16[2096,128]{1,0:T(8,128)(2,1)S(1)}, bf16[2096,128]{1,0:T(8,128)(2,1)S(1)}, u32[]{:S(2)}, u32[]{:S(2)}) collective-permute-start(bf16[2096,128]{1,0:T(8,128)(2,1)S(1)} %shard_map.87.mine_ref), channel_id=1, source_target_pairs={{0,4},{4,0},{8,12},{12,8},{16,20},{20,16},{24,28},{28,24},{32,36},... | collective-permute-start | bytes 1609736 | tf_op jit(solution)/shard_map/ppermute | solution.py:502
  57.1 7.4 %collective-permute-start.2 = (bf16[32,64,128]{2,1,0:T(8,128)(2,1)}, bf16[32,64,128]{2,1,0:T(8,128)(2,1)}, u32[]{:S(2)}, u32[]{:S(2)}) collective-permute-start(bf16[32,64,128]{2,1,0:T(8,128)(2,1)} %get-tuple-element.28), channel_id=1, source_target_pairs={{0,4},{4,0},{8,12},{12,8},{16,20},{20,16},{24,28},{28,24},{32,36},... | collective-permute-start | bytes 1572872 | tf_op jit(solution)/shard_map/ppermute | solution.py:502
  57.4 7.2 %collective-permute-start.1 = (bf16[32,64,128]{2,1,0:T(8,128)(2,1)}, bf16[32,64,128]{2,1,0:T(8,128)(2,1)}, u32[]{:S(2)}, u32[]{:S(2)}) collective-permute-start(bf16[32,64,128]{2,1,0:T(8,128)(2,1)} %get-tuple-element.27), channel_id=1, source_target_pairs={{0,4},{4,0},{8,12},{12,8},{16,20},{20,16},{24,28},{28,24},{32,36},... | collective-permute-start | bytes 1572872 | tf_op jit(solution)/shard_map/ppermute | solution.py:502
  57.7 15.3 %collective-permute-start.3 = (bf16[32,64,128]{2,1,0:T(8,128)(2,1)}, bf16[32,64,128]{2,1,0:T(8,128)(2,1)}, u32[]{:S(2)}, u32[]{:S(2)}) collective-permute-start(bf16[32,64,128]{2,1,0:T(8,128)(2,1)} %get-tuple-element.27), channel_id=1, source_target_pairs={{0,64},{4,68},{8,72},{12,76},{16,80},{20,84},{24,88},{28,92},{32,9... | collective-permute-start | bytes 1572872 | tf_op jit(solution)/shard_map/ppermute | solution.py:502
  59.0 27.5 %all-to-all-start.1 = ((bf16[64,24,128]{2,1,0:T(8,128)(2,1)}), bf16[64,24,128]{2,1,0:T(8,128)(2,1)S(1)}, u32[]{:S(2)}, u32[]{:S(2)}) async-start(bf16[64,24,128]{2,1,0:T(8,128)(2,1)} %shard_map.88), calls=%async_computation.1 | async-start | bytes 786432 | tf_op jit(solution)/shard_map/all_to_all | solution.py:498
  73.0 4.3 %collective-permute-start.4 = (bf16[32,64,128]{2,1,0:T(8,128)(2,1)}, bf16[32,64,128]{2,1,0:T(8,128)(2,1)S(1)}, u32[]{:S(2)}, u32[]{:S(2)}) collective-permute-start(bf16[32,64,128]{2,1,0:T(8,128)(2,1)} %collective-permute-done.3.across_ref), channel_id=1, source_target_pairs={{0,4},{4,0},{8,12},{12,8},{16,20},{20,16},{24,28},{28,24},{32,36},... | collective-permute-start | bytes 1572872 | tf_op jit(solution)/shard_map/ppermute | solution.py:502
  75.2 18.5 %collective-permute-start.6 = (bf16[16,64,128]{2,1,0:T(8,128)(2,1)}, bf16[16,64,128]{2,1,0:T(8,128)(2,1)}, u32[]{:S(2)}, u32[]{:S(2)}) collective-permute-start(bf16[16,64,128]{2,1,0:T(8,128)(2,1)} %get-tuple-element.38), channel_id=1, source_target_pairs={{0,64},{4,68},{8,72},{12,76},{16,80},{20,84},{24,88},{28,92},{32,9... | collective-permute-start | bytes 786440 | tf_op jit(solution)/shard_map/ppermute | solution.py:502
  77.3 16.4 %collective-permute-start.7 = (bf16[16,64,128]{2,1,0:T(8,128)(2,1)}, bf16[16,64,128]{2,1,0:T(8,128)(2,1)}, u32[]{:S(2)}, u32[]{:S(2)}) collective-permute-start(bf16[16,64,128]{2,1,0:T(8,128)(2,1)} %get-tuple-element.39), channel_id=1, source_target_pairs={{0,64},{4,68},{8,72},{12,76},{16,80},{20,84},{24,88},{28,92},{32,9... | collective-permute-start | bytes 786440 | tf_op jit(solution)/shard_map/ppermute | solution.py:502
  87.4 18.3 %all-to-all-start.2 = ((bf16[64,16,128]{2,1,0:T(8,128)(2,1)}), bf16[64,16,128]{2,1,0:T(8,128)(2,1)S(1)}, u32[]{:S(2)}, u32[]{:S(2)}) async-start(bf16[64,16,128]{2,1,0:T(8,128)(2,1)} %shard_map.92), calls=%async_computation.2 | async-start | bytes 524288 | tf_op jit(solution)/shard_map/all_to_all | solution.py:498
  93.7 1.9 %collective-permute-start.8 = (bf16[16,64,128]{2,1,0:T(8,128)(2,1)}, bf16[16,64,128]{2,1,0:T(8,128)(2,1)S(1)}, u32[]{:S(2)}, u32[]{:S(2)}) collective-permute-start(bf16[16,64,128]{2,1,0:T(8,128)(2,1)} %collective-permute-done.6.across1_ref), channel_id=1, source_target_pairs={{0,4},{4,0},{8,12},{12,8},{16,20},{20,16},{24,28},{28,24},{32,36},... | collective-permute-start | bytes 786440 | tf_op jit(solution)/shard_map/ppermute | solution.py:502
  94.3 1.7 %collective-permute-start.9 = (bf16[16,64,128]{2,1,0:T(8,128)(2,1)}, bf16[16,64,128]{2,1,0:T(8,128)(2,1)S(1)}, u32[]{:S(2)}, u32[]{:S(2)}) collective-permute-start(bf16[16,64,128]{2,1,0:T(8,128)(2,1)} %collective-permute-done.7.across2_ref), channel_id=1, source_target_pairs={{0,4},{4,0},{8,12},{12,8},{16,20},{20,16},{24,28},{28,24},{32,36},... | collective-permute-start | bytes 786440 | tf_op jit(solution)/shard_map/ppermute | solution.py:502
  96.0 18.5 %copy-start.2 = (bf16[128,2048]{1,0:T(8,128)(2,1)S(1)}, bf16[128,2048]{1,0:T(8,128)(2,1)}, u32[]{:S(2)}) copy-start(bf16[128,2048]{1,0:T(8,128)(2,1)} %value_ref.5) | copy-start | bytes 1572868
  105.7 24.4 %all-to-all-start.3 = ((bf16[64,32,128]{2,1,0:T(8,128)(2,1)}), bf16[64,32,128]{2,1,0:T(8,128)(2,1)S(1)}, u32[]{:S(2)}, u32[]{:S(2)}) async-start(bf16[64,32,128]{2,1,0:T(8,128)(2,1)} %shard_map.94), calls=%async_computation.3 | async-start | bytes 1048576 | tf_op jit(solution)/shard_map/all_to_all | solution.py:498
  112.8 1.7 %collective-permute-start.5 = (bf16[1024,128]{1,0:T(8,128)(2,1)S(1)}, bf16[1024,128]{1,0:T(8,128)(2,1)S(1)}, u32[]{:S(2)}, u32[]{:S(2)}) collective-permute-start(bf16[1024,128]{1,0:T(8,128)(2,1)S(1)} %bitcast.3), channel_id=1, source_target_pairs={{0,4},{4,0},{8,12},{12,8},{16,20},{20,16},{24,28},{28,24},{32,36},... | collective-permute-start | bytes 786440 | tf_op jit(solution)/shard_map/ppermute | solution.py:502
  114.5 1.0 copy-start.3

commit v11 on v10

--- a/solution.py
+++ b/solution.py
@@ -202,7 +202,7 @@
         return tuple(following)
 
     zero = jnp.zeros((SLICE, HEAD_DIM), jnp.float32)
-    lax.fori_loop(0, BLOCKS // 2, step, (zero, zero), unroll=4)
+    lax.fori_loop(0, BLOCKS // 2, step, (zero, zero), unroll=16)
 
 
 def tile_pairs(queries, keys):
@@ -367,13 +367,14 @@
     for query_tile in EARLY:
         early.find_best(query_tile, (1, 2, 3))
         early.add_up(query_tile)
-        final_ref[tile_blocks(query_tile)] = ratio(total2_ref[early.here(query_tile), :])
-    copy = pltpu.make_async_copy(final_ref, final_out, final_sem)
-    copy.start()
+        blocks = tile_blocks(query_tile)
+        final_ref[blocks] = ratio(total2_ref[early.here(query_tile), :])
+        outward += start_copies(
+            (final_ref.at[blocks],), (final_out.at[blocks],), final_sem.at[query_tile : query_tile + 1]
+        )
     token_ref[...] = best2_ref[0:8, :]
-    for other in outward:
-        other.wait()
-    copy.wait()
+    for copy in outward:
+        copy.wait()
 
 
 def third_kernel(
@@ -591,7 +592,7 @@
             final_space(half_blocks),
             dma((2,)),
             dma((2,)),
-            dma,
+            dma((len(EARLY),)),
         ],
         limit=40,
     )

time: 132 us -> 131 us (level)
  no operation moved by 1% of the time
where the time goes in v11:
time: 131 us
  waiting for transfers between devices  54.6 us (42%)
  starting transfers between devices  40 us (31%)
  Pallas kernels  33.4 us (25%)
  local copies, waits for them, and re-layouts  1.85 us (1%)
    all_to_all x4, waiting for transfers between devices, exchange(): return lax.all_to_all(value, 'ctx', split_axis=0, concat_axis=0, tiled=True)  48.3 us
    pallas_call x10, Pallas kernels, call(): pl.pallas_call(kernel, out_shape=out_shape, in_specs=[whole(space) for sp...  33.4 us
    all_to_all x4, starting transfers between devices, exchange(): return lax.all_to_all(value, 'ctx', split_axis=0, concat_axis=0, tiled=True)  32.1 us
    ppermute x10, starting transfers between devices, swap(): return lax.ppermute(value, 'ctx', [(d, d ^ step) for d in range(BLOCKS)])  7.87 us
    ppermute x10, waiting for transfers between devices, swap(): return lax.ppermute(value, 'ctx', [(d, d ^ step) for d in range(BLOCKS)])  6.3 us
  transfers between devices with their start and end apart: 14, of which 8 were waited for; matrix products, arithmetic and copies ran while one was open for 1% of the time, Pallas kernels for 22%

profile of v11, /device:TPU:1, one launch (start us, length us, event | category | flops | bytes accessed | tf_op | source)
XLA Modules:
  0.0 130.6 jit_solution(4124129082369552706)
XLA Ops:
  0.6 2.3 %shard_map.86 = bf16[64,96,128]{2,1,0:T(8,128)(2,1)} custom-call(bf16[128,2048]{1,0:T(8,128)(2,1)} %query_ref.2, bf16[128,2048]{1,0:T(8,128)(2,1)} %key_ref.3, bf16[128,2048]{1,0:T(8,128)(2,1)} %value_ref.3), custom_call_target="tpu_custom_call" | custom-call | flops 1000 | bytes 3145728 | tf_op jit(solution)/shard_map/pallas_call | solution.py:72
  3.0 0.0 copy-start.4
  3.0 0.0 copy-start
  3.0 0.0 copy-start.1
  3.0 13.1 %all-to-all-start = ((bf16[64,96,128]{2,1,0:T(8,128)(2,1)}), bf16[64,96,128]{2,1,0:T(8,128)(2,1)S(1)}, u32[]{:S(2)}, u32[]{:S(2)}) async-start(bf16[64,96,128]{2,1,0:T(8,128)(2,1)} %shard_map.86), calls=%async_computation | async-start | bytes 3145728 | tf_op jit(solution)/shard_map/all_to_all | solution.py:499
  16.2 0.0 copy-done.4
  16.2 0.1 copy.10.decay_ref
  16.3 0.0 copy-done
  16.3 0.0 copy-done.1
  16.3 1.0 shard_map.87.mine_ref
  17.3 0.5 collective-permute-start
  17.9 0.1 pad_add_fusion.place_ref
  17.9 1.5 %collective-permute-done.other_ref.sibling_ref = bf16[2096,128]{1,0:T(8,128)(2,1)S(1)} collective-permute-done((bf16[2096,128]{1,0:T(8,128)(2,1)S(1)}, bf16[2096,128]{1,0:T(8,128)(2,1)S(1)}, u32[]{:S(2)}, u32[]{:S(2)}) %collective-permute-start) | collective-permute-done | bytes 536608 | tf_op jit(solution)/shard_map/ppermute | solution.py:503
  19.4 1.5 %shard_map.88 = bf16[64,24,128]{2,1,0:T(8,128)(2,1)} custom-call(s32[2]{0:T(128)S(1)} %pad_add_fusion.place_ref, bf16[2096,128]{1,0:T(8,128)(2,1)S(1)} %shard_map.87.mine_ref, bf16[2096,128]{1,0:T(8,128)(2,1)S(1)} %collective-permute-done.other_ref.sibling_ref), custom_call_target="tpu_custom_call" | custom-call | flops 10000000 | bytes 1466376 | tf_op jit(solution)/shard_map/pallas_call | solution.py:72
  20.9 35.1 %all-to-all-done.packed_ref = bf16[64,96,128]{2,1,0:T(8,128)(2,1)S(1)} async-done(((bf16[64,96,128]{2,1,0:T(8,128)(2,1)}), bf16[64,96,128]{2,1,0:T(8,128)(2,1)S(1)}, u32[]{:S(2)}, u32[]{:S(2)}) %all-to-all-start) | async-done | bytes 1572896 | tf_op jit(solution)/shard_map/all_to_all | solution.py:499
  56.0 1.2 shard_map.89
  57.1 0.2 collective-permute-start.2
  57.4 0.4 collective-permute-start.1
  57.7 1.2 collective-permute-start.3
  59.0 5.5 %all-to-all-start.1 = ((bf16[64,24,128]{2,1,0:T(8,128)(2,1)}), bf16[64,24,128]{2,1,0:T(8,128)(2,1)S(1)}, u32[]{:S(2)}, u32[]{:S(2)}) async-start(bf16[64,24,128]{2,1,0:T(8,128)(2,1)} %shard_map.88), calls=%async_computation.1 | async-start | bytes 786432 | tf_op jit(solution)/shard_map/all_to_all | solution.py:499
  64.5 0.0 collective-permute-done.2.late_ref
  64.5 0.0 collective-permute-done.1.early_ref.sibling_ref
  64.5 6.5 %shard_map.90 = (f32[1024,128]{1,0:T(8,128)}, f32[1024,256]{1,0:T(8,128)}, f32[8,128]{1,0:T(8,128)S(1)}) custom-call(s32[2]{0:T(128)S(1)} %pad_add_fusion.place_ref, bf16[64,96,128]{2,1,0:T(8,128)(2,1)S(1)} %all-to-all-done.packed_ref, bf16[32,64,128]{2,1,0:T(8,128)(2,1)} %collective-permute-done.1.early_ref.sibling_ref, ...), custom_call_target="tpu_custom_call" | custom-call | tf_op jit(solution)/shard_map/pallas_call | solution.py:72
  71.0 2.0 %collective-permute-done.3.across_ref = bf16[32,64,128]{2,1,0:T(8,128)(2,1)} collective-permute-done((bf16[32,64,128]{2,1,0:T(8,128)(2,1)}, bf16[32,64,128]{2,1,0:T(8,128)(2,1)}, u32[]{:S(2)}, u32[]{:S(2)}) %collective-permute-start.3) | collective-permute-done | bytes 524320 | tf_op jit(solution)/shard_map/ppermute | solution.py:503
  73.0 2.1 %collective-permute-start.4 = (bf16[32,64,128]{2,1,0:T(8,128)(2,1)}, bf16[32,64,128]{2,1,0:T(8,128)(2,1)S(1)}, u32[]{:S(2)}, u32[]{:S(2)}) collective-permute-start(bf16[32,64,128]{2,1,0:T(8,128)(2,1)} %collective-permute-done.3.across_ref), channel_id=1, source_target_pairs={{0,4},{4,0},{8,12},{12,8},{16,20},{20,16},{24,28},{28,24},{32,36},... | collective-permute-start | bytes 1572872 | tf_op jit(solution)/shard_map/ppermute | solution.py:503
  75.2 2.1 %collective-permute-start.6 = (bf16[16,64,128]{2,1,0:T(8,128)(2,1)}, bf16[16,64,128]{2,1,0:T(8,128)(2,1)}, u32[]{:S(2)}, u32[]{:S(2)}) collective-permute-start(bf16[16,64,128]{2,1,0:T(8,128)(2,1)} %get-tuple-element.38), channel_id=1, source_target_pairs={{0,64},{4,68},{8,72},{12,76},{16,80},{20,84},{24,88},{28,92},{32,9... | collective-permute-start | bytes 786440 | tf_op jit(solution)/shard_map/ppermute | solution.py:503
  77.3 0.0 collective-permute-start.7
  77.3 0.0 collective-permute-done.4.diagonal_ref
  77.3 8.8 %shard_map.91 = (f32[1024,128]{1,0:T(8,128)}, f32[1024,256]{1,0:T(8,128)}, bf16[32,32,128]{2,1,0:T(8,128)(2,1)}, f32[8,128]{1,0:T(8,128)S(1)}) custom-call(s32[2]{0:T(128)S(1)} %pad_add_fusion.place_ref, bf16[64,96,128]{2,1,0:T(8,128)(2,1)S(1)} %all-to-all-done.packed_ref, bf16[32,64,128]{2,1,0:T(8,128)(2,1)} %collective-permute-done.1.early_ref.sibling_ref, ...), custom_call_target="tpu_custom_call" | custom-call | tf_op jit(solution)/shard_map/pallas_call | solution.py:72
  86.1 0.0 all-to-all-done.1.moved_ref
  86.1 0.9 shard_map.92
  87.0 6.3 %all-to-all-start.2 = ((bf16[64,16,128]{2,1,0:T(8,128)(2,1)}), bf16[64,16,128]{2,1,0:T(8,128)(2,1)S(1)}, u32[]{:S(2)}, u32[]{:S(2)}) async-start(bf16[64,16,128]{2,1,0:T(8,128)(2,1)} %shard_map.92), calls=%async_computation.2 | async-start | bytes 524288 | tf_op jit(solution)/shard_map/all_to_all | solution.py:499
  93.3 0.0 collective-permute-done.6.across1_ref
  93.3 0.0 collective-permute-done.7.across2_ref
  93.3 0.5 collective-permute-start.8
  93.9 0.1 collective-permute-start.9
  94.0 1.3 collective-permute-done.8.diagonal1_ref
  95.2 0.4 collective-permute-done.9.diagonal2_ref
  95.6 0.0 copy-start.2
  95.6 6.3 %shard_map.94 = bf16[64,32,128]{2,1,0:T(8,128)(2,1)} custom-call(s32[2]{0:T(128)S(1)} %pad_add_fusion.place_ref, bf16[64,96,128]{2,1,0:T(8,128)(2,1)S(1)} %all-to-all-done.packed_ref, bf16[16,64,128]{2,1,0:T(8,128)(2,1)} %collective-permute-done.6.across1_ref, bf16[16,64,128]{2,1,0:T(8,128)(2,1)} %collective-permute-done.7.across2_ref, ...), custom_call_target="tpu_custom_call" | custom-call | tf_op jit(solution)/shard_map/pallas_call | solution.py:72
  101.9 3.4 %all-to-all-done.2 = bf16[64,16,128]{2,1,0:T(8,128)(2,1)S(1)} async-done(((bf16[64,16,128]{2,1,0:T(8,128)(2,1)}), bf16[64,16,128]{2,1,0:T(8,128)(2,1)S(1)}, u32[]{:S(2)}, u32[]{:S(2)}) %all-to-all-start.2) | async-done | bytes 262176 | tf_op jit(solution)/shard_map/all_to_all | solution.py:499
  105.3 7.1 %all-to-all-start.3 = ((bf16[64,32,128]{2,1,0:T(8,128)(2,1)}), bf16[64,32,128]{2,1,0:T(8,128)(2,1)S(1)}, u32[]{:S(2)}, u32[]{:S(2)}) async-start(bf16[64,32,128]{2,1,0:T(8,128)(2,1)} %shard_map.94), calls=%async_computation.3 | async-start | bytes 1048576 | tf_op jit(solution)/shard_map/all_to_all | solution.py:499
  112.4 0.5 collective-permute-start.5
  113.0 1.2 collective-permute-done.5.other_ref
  114.1 0.0 copy-done.2
  114.1 0.0 copy-start.3
  114.1 1.0 copy-done.3
  115.2 4.1 %shard_map.93 = bf16[128,2048]{1,0:T(8,128)(2,1)} custom-call(s32[2]{0:T(128)S(1)} %pad_add_fusion.place_ref, bf16[128,2048]{1,0:T(8,128)(2,1)S(1)} %copy-done.3, bf16[128,2048]{1,0:T(8,128)(2,1)S(1)} %copy-done, bf16[128,2048]{1,0:T(8,128)(2,1)S(1)} %copy-done.2, f32[128,16]{1,0:T(8,128)S(1)} %copy.10.decay_ref, bf16[1024,128]{1,0:T(8,128)(2,1)S(1)} %bitcast.4, ...), custom_call_target="tpu_custom_call" | custom-call | flops 200000000 | bytes 3166216 | tf_op jit(solution)/shard_map/pallas_call | solution.py:72
  119.2 0.7 slice.4.order_ref
  119.9 9.8 %all-to-all-done.3.moved_ref = bf16[64,32,128]{2,1,0:T(8,128)(2,1)S(1)} async-done(((bf16[64,32,128]{2,1,0:T(8,128)(2,1)}), bf16[64,32,128]{2,1,0:T(8,128)(2,1)S(1)}, u32[]{:S(2)}, u32[]{:S(2)}) %all-to-all-start.3) | async-done | bytes 524320 | tf_op jit(solution)/shard_map/all_to_all | solution.py:499
  129.7 0.9 shard_map.95
Async XLA Ops:
  3.0 13.2 %copy-start.4 = (f32[128,16]{0,1:T(8,128)S(1)}, f32[128,16]{0,1:T(8,128)}, u32[]{:S(2)}) copy-start(f32[128,16]{0,1:T(8,128)} %param.10) | copy-start | bytes 24580
  3.0 13.3 %copy-start = (bf16[128,2048]{1,0:T(8,128)(2,1)S(1)}, bf16[128,2048]{1,0:T(8,128)(2,1)}, u32[]{:S(2)}) copy-start(bf16[128,2048]{1,0:T(8,128)(2,1)} %key_ref.5) | copy-start | bytes 1572868
  3.0 13.3 %copy-start.1 = (bf16[128,2048]{1,0:T(8,128)(2,1)S(1)}, bf16[128,2048]{1,0:T(8,128)(2,1)}, u32[]{:S(2)}) copy-start(bf16[128,2048]{1,0:T(8,128)(2,1)} %value_ref.5) | copy-start | bytes 1572868
  3.0 52.9 %all-to-all-start = ((bf16[64,96,128]{2,1,0:T(8,128)(2,1)}), bf16[64,96,128]{2,1,0:T(8,128)(2,1)S(1)}, u32[]{:S(2)}, u32[]{:S(2)}) async-start(bf16[64,96,128]{2,1,0:T(8,128)(2,1)} %shard_map.86), calls=%async_computation | async-start | bytes 3145728 | tf_op jit(solution)/shard_map/all_to_all | solution.py:499
  17.3 2.1 %collective-permute-start = (bf16[2096,128]{1,0:T(8,128)(2,1)S(1)}, bf16[2096,128]{1,0:T(8,128)(2,1)S(1)}, u32[]{:S(2)}, u32[]{:S(2)}) collective-permute-start(bf16[2096,128]{1,0:T(8,128)(2,1)S(1)} %shard_map.87.mine_ref), channel_id=1, source_target_pairs={{0,4},{4,0},{8,12},{12,8},{16,20},{20,16},{24,28},{28,24},{32,36},... | collective-permute-start | bytes 1609736 | tf_op jit(solution)/shard_map/ppermute | solution.py:503
  57.1 7.4 %collective-permute-start.2 = (bf16[32,64,128]{2,1,0:T(8,128)(2,1)}, bf16[32,64,128]{2,1,0:T(8,128)(2,1)}, u32[]{:S(2)}, u32[]{:S(2)}) collective-permute-start(bf16[32,64,128]{2,1,0:T(8,128)(2,1)} %get-tuple-element.28), channel_id=1, source_target_pairs={{0,4},{4,0},{8,12},{12,8},{16,20},{20,16},{24,28},{28,24},{32,36},... | collective-permute-start | bytes 1572872 | tf_op jit(solution)/shard_map/ppermute | solution.py:503
  57.4 7.2 %collective-permute-start.1 = (bf16[32,64,128]{2,1,0:T(8,128)(2,1)}, bf16[32,64,128]{2,1,0:T(8,128)(2,1)}, u32[]{:S(2)}, u32[]{:S(2)}) collective-permute-start(bf16[32,64,128]{2,1,0:T(8,128)(2,1)} %get-tuple-element.27), channel_id=1, source_target_pairs={{0,4},{4,0},{8,12},{12,8},{16,20},{20,16},{24,28},{28,24},{32,36},... | collective-permute-start | bytes 1572872 | tf_op jit(solution)/shard_map/ppermute | solution.py:503
  57.7 15.3 %collective-permute-start.3 = (bf16[32,64,128]{2,1,0:T(8,128)(2,1)}, bf16[32,64,128]{2,1,0:T(8,128)(2,1)}, u32[]{:S(2)}, u32[]{:S(2)}) collective-permute-start(bf16[32,64,128]{2,1,0:T(8,128)(2,1)} %get-tuple-element.27), channel_id=1, source_target_pairs={{0,64},{4,68},{8,72},{12,76},{16,80},{20,84},{24,88},{28,92},{32,9... | collective-permute-start | bytes 1572872 | tf_op jit(solution)/shard_map/ppermute | solution.py:503
  59.0 27.2 %all-to-all-start.1 = ((bf16[64,24,128]{2,1,0:T(8,128)(2,1)}), bf16[64,24,128]{2,1,0:T(8,128)(2,1)S(1)}, u32[]{:S(2)}, u32[]{:S(2)}) async-start(bf16[64,24,128]{2,1,0:T(8,128)(2,1)} %shard_map.88), calls=%async_computation.1 | async-start | bytes 786432 | tf_op jit(solution)/shard_map/all_to_all | solution.py:499
  73.0 4.3 %collective-permute-start.4 = (bf16[32,64,128]{2,1,0:T(8,128)(2,1)}, bf16[32,64,128]{2,1,0:T(8,128)(2,1)S(1)}, u32[]{:S(2)}, u32[]{:S(2)}) collective-permute-start(bf16[32,64,128]{2,1,0:T(8,128)(2,1)} %collective-permute-done.3.across_ref), channel_id=1, source_target_pairs={{0,4},{4,0},{8,12},{12,8},{16,20},{20,16},{24,28},{28,24},{32,36},... | collective-permute-start | bytes 1572872 | tf_op jit(solution)/shard_map/ppermute | solution.py:503
  75.2 18.1 %collective-permute-start.6 = (bf16[16,64,128]{2,1,0:T(8,128)(2,1)}, bf16[16,64,128]{2,1,0:T(8,128)(2,1)}, u32[]{:S(2)}, u32[]{:S(2)}) collective-permute-start(bf16[16,64,128]{2,1,0:T(8,128)(2,1)} %get-tuple-element.38), channel_id=1, source_target_pairs={{0,64},{4,68},{8,72},{12,76},{16,80},{20,84},{24,88},{28,92},{32,9... | collective-permute-start | bytes 786440 | tf_op jit(solution)/shard_map/ppermute | solution.py:503
  77.3 16.0 %collective-permute-start.7 = (bf16[16,64,128]{2,1,0:T(8,128)(2,1)}, bf16[16,64,128]{2,1,0:T(8,128)(2,1)}, u32[]{:S(2)}, u32[]{:S(2)}) collective-permute-start(bf16[16,64,128]{2,1,0:T(8,128)(2,1)} %get-tuple-element.39), channel_id=1, source_target_pairs={{0,64},{4,68},{8,72},{12,76},{16,80},{20,84},{24,88},{28,92},{32,9... | collective-permute-start | bytes 786440 | tf_op jit(solution)/shard_map/ppermute | solution.py:503
  87.0 18.3 %all-to-all-start.2 = ((bf16[64,16,128]{2,1,0:T(8,128)(2,1)}), bf16[64,16,128]{2,1,0:T(8,128)(2,1)S(1)}, u32[]{:S(2)}, u32[]{:S(2)}) async-start(bf16[64,16,128]{2,1,0:T(8,128)(2,1)} %shard_map.92), calls=%async_computation.2 | async-start | bytes 524288 | tf_op jit(solution)/shard_map/all_to_all | solution.py:499
  93.3 1.9 %collective-permute-start.8 = (bf16[16,64,128]{2,1,0:T(8,128)(2,1)}, bf16[16,64,128]{2,1,0:T(8,128)(2,1)S(1)}, u32[]{:S(2)}, u32[]{:S(2)}) collective-permute-start(bf16[16,64,128]{2,1,0:T(8,128)(2,1)} %collective-permute-done.6.across1_ref), channel_id=1, source_target_pairs={{0,4},{4,0},{8,12},{12,8},{16,20},{20,16},{24,28},{28,24},{32,36},... | collective-permute-start | bytes 786440 | tf_op jit(solution)/shard_map/ppermute | solution.py:503
  93.9 1.7 %collective-permute-start.9 = (bf16[16,64,128]{2,1,0:T(8,128)(2,1)}, bf16[16,64,128]{2,1,0:T(8,128)(2,1)S(1)}, u32[]{:S(2)}, u32[]{:S(2)}) collective-permute-start(bf16[16,64,128]{2,1,0:T(8,128)(2,1)} %collective-permute-done.7.across2_ref), channel_id=1, source_target_pairs={{0,4},{4,0},{8,12},{12,8},{16,20},{20,16},{24,28},{28,24},{32,36},... | collective-permute-start | bytes 786440 | tf_op jit(solution)/shard_map/ppermute | solution.py:503
  95.6 18.5 %copy-start.2 = (bf16[128,2048]{1,0:T(8,128)(2,1)S(1)}, bf16[128,2048]{1,0:T(8,128)(2,1)}, u32[]{:S(2)}) copy-start(bf16[128,2048]{1,0:T(8,128)(2,1)} %value_ref.5) | copy-start | bytes 1572868
  105.3 24.4 %all-to-all-start.3 = ((bf16[64,32,128]{2,1,0:T(8,128)(2,1)}), bf16[64,32,128]{2,1,0:T(8,128)(2,1)S(1)}, u32[]{:S(2)}, u32[]{:S(2)}) async-start(bf16[64,32,128]{2,1,0:T(8,128)(2,1)} %shard_map.94), calls=%async_computation.3 | async-start | bytes 1048576 | tf_op jit(solution)/shard_map/all_to_all | solution.py:499
  112.4 1.7 %collective-permute-start.5 = (bf16[1024,128]{1,0:T(8,128)(2,1)S(1)}, bf16[1024,128]{1,0:T(8,128)(2,1)S(1)}, u32[]{:S(2)}, u32[]{:S(2)}) collective-permute-start(bf16[1024,128]{1,0:T(8,128)(2,1)S(1)} %bitcast.3), channel_id=1, source_target_pairs={{0,4},{4,0},{8,12},{12,8},{16,20},{20,16},{24,28},{28,24},{32,36},... | collective-permute-start | bytes 786440 | tf_op jit(solution)/shard_map/ppermute | solution.py:503
  114.1 1.0 copy-start.3
